TPU v7x, 512 devices: a whole 4x8x8 slice. The times are simulated.
512 devices in a mesh: outer: 16 (over y_hi, x), inner: 32 (over z, y_lo, core).
Axes of the slice: x: 4, y: 8 (y_hi: 4, y_lo: 2; y = y_hi * 2 + y_lo), z: 8, core: 2. Of those that a mesh axis runs over, the one named last changes fastest.
Arguments:
- queries: bfloat16 [16384, 768], P('inner'), may hold values from -8 to 8
- passages: bfloat16 [32768, 768], P(('outer', 'inner')), may hold values from -8 to 8
- positive: int32 [16384], P('inner'), may hold values from 0 to 32767
Outputs:
- query_grad: bfloat16 [16384, 768], P('inner', 'outer')
- loss: float32 [16384], P('inner')
All inputs are finite; a program needn't handle non-finite values.
Results may differ from a plain program's by a relative error of at most 0.0085.
Values may be sent and summed in bfloat16 or wider, within the bound.
No kernel may reach another device: no remote copies, remote signals or barrier semaphores. Data moves between devices by JAX's collectives and lax.ppermute only.
A program may use at most 64 MiB of HBM per device.

v0:
```python
import math

import jax
import jax.numpy as jnp
from jax import lax
from jax.sharding import Mesh
from jax.sharding import PartitionSpec as P

INNER = ("inner_0", "inner_1", "inner_2")
OUTER_INNER = ("outer", "inner_0", "inner_1", "inner_2")


def from_everyone(shard, axis):
    copies = jnp.broadcast_to(shard, (lax.axis_size(axis), *shard.shape))
    return lax.all_to_all(copies, axis, split_axis=0, concat_axis=0, tiled=True)


def joined_along(blocks, dim):
    blocks = jnp.moveaxis(blocks, 0, dim)
    shape = blocks.shape
    return blocks.reshape(*shape[:dim], shape[dim] * shape[dim + 1], *shape[dim + 2 :])


def gathered_by_axis(shard, axes, dim):
    far, near = axes
    first = from_everyone(shard, far)
    blocks = jnp.swapaxes(from_everyone(first, near), 0, 1)
    return joined_along(blocks.reshape(-1, *shard.shape), dim)


def over_copies(shard, axis):
    return from_everyone(shard, axis).max(axis=0)


def over_copies_2(shard, axis):
    return from_everyone(shard, axis).sum(axis=0)


def packed_total(arrays, axis):
    ends = [0]
    for a in arrays:
        ends.append(ends[-1] + a.size)
    running = over_copies_2(jnp.concatenate([a.ravel() for a in arrays]), axis)
    return tuple((running[b:e].reshape(a.shape) for a, b, e in zip(arrays, ends, ends[1:])))


def cut_along(shard, dim, devices):
    shape = shard.shape
    blocks = shard.reshape(*shape[:dim], devices, shape[dim] // devices, *shape[dim + 1 :])
    return jnp.moveaxis(blocks, dim, 0)


def sum_at_owner(shard, axis, dim):
    blocks = cut_along(shard, dim, lax.axis_size(axis))
    arrived = lax.all_to_all(blocks, axis, split_axis=0, concat_axis=0, tiled=True)
    return arrived.astype(jnp.float32).sum(axis=0)


def in_one_piece(arrays, axis, dim, along):
    ends, at = ([], 0)
    for a in arrays[:-1]:
        at += a.shape[along]
        ends.append(at)
    both = jnp.concatenate(arrays, axis=along)
    return tuple(jnp.split(sum_at_owner(both, axis, dim), ends, axis=along))


def shards(queries, passages, positive):
    width = queries.shape[1]
    count = queries.shape[0]
    scale = 3.0 / math.sqrt(width)
    group_rows = passages.shape[0] * lax.axis_size(INNER)
    offset = lax.axis_index("outer") * group_rows
    piece = gathered_by_axis(passages, (("inner_0", "inner_1"), "inner_2"), 0)
    top = jnp.full((count,), -1e30, jnp.float32)
    scores = (
        lax.dot_general(
            piece, queries, (((1,), (1,)), ((), ())), preferred_element_type=jnp.float32
        )
        * scale
    )
    ids = offset + lax.broadcasted_iota(jnp.int32, (piece.shape[0], 1), 0)
    hits = ids == positive[None, :]
    new_top = jnp.maximum(top, jnp.max(scores, axis=0))
    expd = jnp.exp(scores - new_top[None, :])
    total = jnp.sum(expd, axis=0)
    stacked = jnp.concatenate([expd.astype(jnp.bfloat16), hits.astype(jnp.bfloat16)], axis=1)
    both = lax.dot_general(
        stacked, piece, (((0,), (0,)), ((), ())), preferred_element_type=jnp.float32
    )
    mixture = both[:count]
    chosen = both[count:]
    pscore = jnp.sum(jnp.where(hits, scores, 0.0), axis=0)
    top, total, mixture, chosen, pscore = (new_top, total, mixture, chosen, pscore)
    top_all = over_copies(top, "outer")
    fade = jnp.exp(top - top_all)
    total, pscore = packed_total((total * fade, pscore), "outer")
    scaled = mixture * fade[:, None]
    mixture, chosen = in_one_piece(
        (scaled.astype(jnp.bfloat16), chosen.astype(jnp.bfloat16)), "outer", 1, 0
    )
    query_grad = (scale * (mixture / total[:, None] - chosen)).astype(jnp.bfloat16)
    loss = top_all + jnp.log(total) - pscore
    return (query_grad, loss)


def solution(mesh):
    torus = Mesh(
        mesh.devices.reshape(mesh.shape["outer"], 8, 2, 2),
        ("outer", "inner_0", "inner_1", "inner_2"),
    )
    in_specs = (P(INNER, None), P(OUTER_INNER, None), P(INNER))
    out_specs = (P(INNER, "outer"), P(INNER))
    return jax.shard_map(
        shards, mesh=torus, in_specs=in_specs, out_specs=out_specs, check_vma=False
    )
```

profile of v0, /device:TPU:8, one launch (start us, length us, event | category | flops | bytes accessed | tf_op | source)
XLA Modules:
  0.0 149.0 jit_solution(10822292836511678323)
XLA Ops:
  0.6 0.0 copy-start
  0.6 0.0 copy-start.3
  0.7 2.3 %broadcast_in_dim.23 = bf16[16,64,768]{2,1,0:T(8,128)(2,1)} broadcast(bf16[64,768]{1,0:T(8,128)(2,1)} %param.4), dimensions={1,2} | broadcast | bytes 1671168 | tf_op jit(solution)/shard_map/broadcast_in_dim | solution.py:14
  2.9 11.8 %all-to-all-start = ((bf16[16,64,768]{2,1,0:T(8,128)(2,1)}), bf16[16,64,768]{2,1,0:T(8,128)(2,1)S(1)}, u32[]{:S(2)}, u32[]{:S(2)}) async-start(bf16[16,64,768]{2,1,0:T(8,128)(2,1)} %broadcast_in_dim.23), calls=%async_computation | async-start | bytes 3145728 | tf_op jit(solution)/shard_map/all_to_all | solution.py:15
  14.7 0.0 copy-done.3
  14.7 1.6 %compare_convert_fusion = bf16[2048,512]{1,0:T(8,128)(2,1)} fusion(s32[512]{0:T(512)S(1)} %copy-done.3, s32[2048]{0:T(1024)S(1)} %iota_add_fusion), kind=kLoop, calls=%fused_computation.1 | loop fusion | flops 2097152 | bytes 2107392 | tf_op jit(solution)/shard_map/convert_element_type | solution.py:87
  16.4 36.9 %all-to-all-done = bf16[16,64,768]{2,1,0:T(8,128)(2,1)S(1)} async-done(((bf16[16,64,768]{2,1,0:T(8,128)(2,1)}), bf16[16,64,768]{2,1,0:T(8,128)(2,1)S(1)}, u32[]{:S(2)}, u32[]{:S(2)}) %all-to-all-start) | async-done | bytes 1572896 | tf_op jit(solution)/shard_map/all_to_all | solution.py:15
  53.2 0.4 broadcast_in_dim.24
  53.7 6.3 %all_to_all.27 = bf16[2,16,64,768]{3,2,1,0:T(8,128)(2,1)S(1)} all-to-all(bf16[2,16,64,768]{3,2,1,0:T(8,128)(2,1)S(1)} %broadcast_in_dim.24), channel_id=1, replica_groups=mesh['outer'=16,'inner_0'=8,'inner_1'=2,'inner_2'=2] {'inner_2'}, dimensions={0} | all-to-all | bytes 6291456 | tf_op jit(solution)/shard_map/all_to_all | solution.py:15
  59.9 0.3 copy.10
  60.2 0.0 copy-start.1
  60.3 1.9 %multiply_reduce_fusion = (f32[512]{0:T(512)S(1)}, f32[2048,512]{1,0:T(8,128)S(1)}) fusion(bf16[2048,768]{1,0:T(8,128)(2,1)S(1)} %bitcast.9, bf16[512,768]{1,0:T(8,128)(2,1)S(1)} %copy-done), kind=kOutput, calls=%fused_computation.10 | convolution fusion | flops 1612709376 | bytes 8128512 | tf_op jit(solution)/shard_map/dot_general | solution.py:77
  62.2 0.0 copy-done.1
  62.2 1.3 fusion.5
  63.5 0.6 broadcast_in_dim.26
  64.1 8.8 %all-to-all-start.2 = ((f32[16,1,512]{2,1,0:T(1,128)}), f32[16,1,512]{2,1,0:T(1,128)S(1)}, u32[]{:S(2)}, u32[]{:S(2)}) async-start(f32[16,1,512]{2,1,0:T(1,128)} %broadcast_in_dim.26), calls=%async_computation.2 | async-start | bytes 65536 | tf_op jit(solution)/shard_map/all_to_all | solution.py:15
  72.9 6.0 %fusion.1 = f32[1024,768]{1,0:T(8,128)S(1)} fusion(bf16[2048,768]{1,0:T(8,128)(2,1)} %bitcast.10, bf16[2048,512]{1,0:T(8,128)(2,1)} %compare_convert_fusion, bf16[2048,512]{1,0:T(8,128)(2,1)S(1)} %get-tuple-element.6), kind=kOutput, calls=%fused_computation.3 | convolution fusion | flops 3229614080 | bytes 10485760 | tf_op jit(solution)/shard_map/dot_general | solution.py:88
  78.9 1.7 %copy-done.2 = f32[1024,768]{1,0:T(8,128)} copy-done((f32[1024,768]{1,0:T(8,128)}, f32[1024,768]{1,0:T(8,128)S(1)}, u32[]{:S(2)}) %copy-start.2) | copy-done | bytes 3145752
  80.5 0.1 slice.25
  80.6 2.2 %all-to-all-done.2 = f32[16,1,512]{2,1,0:T(1,128)S(1)} async-done(((f32[16,1,512]{2,1,0:T(1,128)}), f32[16,1,512]{2,1,0:T(1,128)S(1)}, u32[]{:S(2)}, u32[]{:S(2)}) %all-to-all-start.2) | async-done | bytes 32800 | tf_op jit(solution)/shard_map/all_to_all | solution.py:15
  82.9 2.4 %fusion.7 = bf16[512,768]{1,0:T(8,128)(2,1)} fusion(f32[1024,768]{1,0:T(8,128)} %copy-done.2, f32[512]{0:T(512)S(1)} %get-tuple-element.5), kind=kLoop, calls=%fused_computation.14 | loop fusion | flops 786432 | bytes 2361344 | tf_op jit(solution)/shard_map/convert_element_type | solution.py:100
  85.4 0.7 broadcast_in_dim.28
  86.0 7.4 %all-to-all-start.4 = ((f32[16,1,1024]{2,1,0:T(1,128)}), f32[16,1,1024]{2,1,0:T(1,128)S(1)}, u32[]{:S(2)}, u32[]{:S(2)}) async-start(f32[16,1,1024]{2,1,0:T(1,128)} %broadcast_in_dim.28), calls=%async_computation.4 | async-start | bytes 131072 | tf_op jit(solution)/shard_map/all_to_all | solution.py:15
  93.4 1.2 pad_maximum_fusion
  94.7 1.7 %copy.12 = bf16[1024,768]{0,1:T(8,128)(2,1)} copy(bf16[1024,768]{1,0:T(8,128)(2,1)S(1)} %pad_maximum_fusion) | data formatting | bytes 3145728 | tf_op jit(solution)/shard_map/concatenate | solution.py:64
  96.3 7.1 %all-to-all-done.4 = f32[16,1,1024]{2,1,0:T(1,128)S(1)} async-done(((f32[16,1,1024]{2,1,0:T(1,128)}), f32[16,1,1024]{2,1,0:T(1,128)S(1)}, u32[]{:S(2)}, u32[]{:S(2)}) %all-to-all-start.4) | async-done | bytes 65568 | tf_op jit(solution)/shard_map/all_to_all | solution.py:15
  103.5 3.7 %all-to-all-start.3 = ((bf16[16,1024,48]{1,2,0:T(8,128)(2,1)}), bf16[16,1024,48]{1,2,0:T(8,128)(2,1)S(1)}, u32[]{:S(2)}, u32[]{:S(2)}) async-start(bf16[16,1024,48]{1,2,0:T(8,128)(2,1)} %bitcast.3), calls=%async_computation.3 | async-start | bytes 3145728 | tf_op jit(solution)/shard_map/all_to_all | solution.py:55
  107.2 0.1 reduce_sum.39
  107.2 0.6 slice_subtract_fusion.1
  107.8 40.3 %all-to-all-done.3 = bf16[16,1024,48]{1,2,0:T(8,128)(2,1)S(1)} async-done(((bf16[16,1024,48]{1,2,0:T(8,128)(2,1)}), bf16[16,1024,48]{1,2,0:T(8,128)(2,1)S(1)}, u32[]{:S(2)}, u32[]{:S(2)}) %all-to-all-start.3) | async-done | bytes 1572896 | tf_op jit(solution)/shard_map/all_to_all | solution.py:55
  148.1 0.3 convert_reduce_fusion
  148.4 0.6 fusion.9
  (7 shorter events, 0.1 us)
Async XLA Ops:
  0.6 59.6 %copy-start = (bf16[512,768]{1,0:T(8,128)(2,1)S(1)}, bf16[512,768]{1,0:T(8,128)(2,1)}, u32[]{:S(2)}) copy-start(bf16[512,768]{1,0:T(8,128)(2,1)} %param.3) | copy-start | bytes 2359300
  0.6 14.1 %copy-start.3 = (s32[512]{0:T(512)S(1)}, s32[512]{0:T(512)}, u32[]{:S(2)}) copy-start(s32[512]{0:T(512)} %param.5) | copy-start | bytes 6148
  2.9 50.3 %all-to-all-start = ((bf16[16,64,768]{2,1,0:T(8,128)(2,1)}), bf16[16,64,768]{2,1,0:T(8,128)(2,1)S(1)}, u32[]{:S(2)}, u32[]{:S(2)}) async-start(bf16[16,64,768]{2,1,0:T(8,128)(2,1)} %broadcast_in_dim.23), calls=%async_computation | async-start | bytes 3145728 | tf_op jit(solution)/shard_map/all_to_all | solution.py:15
  60.2 1.9 %copy-start.1 = (bf16[2,16,64,768]{3,2,0,1:T(8,128)(2,1)}, bf16[2,16,64,768]{3,2,0,1:T(8,128)(2,1)S(1)}, u32[]{:S(2)}) copy-start(bf16[2,16,64,768]{3,2,0,1:T(8,128)(2,1)S(1)} %copy.10) | copy-start | bytes 9437188
  64.1 18.8 %all-to-all-start.2 = ((f32[16,1,512]{2,1,0:T(1,128)}), f32[16,1,512]{2,1,0:T(1,128)S(1)}, u32[]{:S(2)}, u32[]{:S(2)}) async-start(f32[16,1,512]{2,1,0:T(1,128)} %broadcast_in_dim.26), calls=%async_computation.2 | async-start | bytes 65536 | tf_op jit(solution)/shard_map/all_to_all | solution.py:15
  78.9 1.7 %copy-start.2 = (f32[1024,768]{1,0:T(8,128)}, f32[1024,768]{1,0:T(8,128)S(1)}, u32[]{:S(2)}) copy-start(f32[1024,768]{1,0:T(8,128)S(1)} %fusion.1) | copy-start | bytes 9437188
  86.0 17.4 %all-to-all-start.4 = ((f32[16,1,1024]{2,1,0:T(1,128)}), f32[16,1,1024]{2,1,0:T(1,128)S(1)}, u32[]{:S(2)}, u32[]{:S(2)}) async-start(f32[16,1,1024]{2,1,0:T(1,128)} %broadcast_in_dim.28), calls=%async_computation.4 | async-start | bytes 131072 | tf_op jit(solution)/shard_map/all_to_all | solution.py:15
  103.5 44.6 %all-to-all-start.3 = ((bf16[16,1024,48]{1,2,0:T(8,128)(2,1)}), bf16[16,1024,48]{1,2,0:T(8,128)(2,1)S(1)}, u32[]{:S(2)}, u32[]{:S(2)}) async-start(bf16[16,1024,48]{1,2,0:T(8,128)(2,1)} %bitcast.3), calls=%async_computation.3 | async-start | bytes 3145728 | tf_op jit(solution)/shard_map/all_to_all | solution.py:55
where the time goes:
time: 150 us; the launch traced here: 149 us
  waiting for transfers between devices  86.5 us (58%)
  starting transfers between devices  31.7 us (21%)
  other arithmetic  8.21 us (5%)
  matrix products  7.91 us (5%)
  local copies, waits for them, and re-layouts  7.7 us (5%)
  blocking collectives  6.26 us (4%)
    all_to_all x3, waiting for transfers between devices, from_everyone(): return lax.all_to_all(copies, axis, split_axis=0, concat_axis=0, tiled=True)  46.2 us
    all_to_all x1, waiting for transfers between devices, sum_at_owner(): lax.all_to_all(blocks, axis, split_axis=0, concat_axis=0, tiled=True)  40.3 us
    all_to_all x3, starting transfers between devices, from_everyone(): return lax.all_to_all(copies, axis, split_axis=0, concat_axis=0, tiled=True)  28 us
    all_to_all x1, blocking collectives, from_everyone(): return lax.all_to_all(copies, axis, split_axis=0, concat_axis=0, tiled=True)  6.26 us
    dot_general x1, matrix products, shards(): lax.dot_general(stacked, piece, (((0,), (0,)), ((), ())), preferred_eleme...  6.01 us
    broadcast_in_dim x4, local copies, waits for them, and re-layouts, from_everyone(): copies = jnp.broadcast_to(shard, (lax.axis_size(axis), *shard.shape))  3.97 us
    all_to_all x1, starting transfers between devices, sum_at_owner(): lax.all_to_all(blocks, axis, split_axis=0, concat_axis=0, tiled=True)  3.71 us
  transfers between devices with their start and end apart: 4, of which 4 were waited for; matrix products, arithmetic and copies ran while one was open for 8% of the time, Pallas kernels for 0%

commit v1 on v0

v1 whole, which is shorter than its diff:
```python
import math

import jax
import jax.numpy as jnp
from jax import lax
from jax.sharding import Mesh
from jax.sharding import PartitionSpec as P

INNER = ("z", "yl", "c")
OUTER = ("yh", "x")
LANE = ("yh", "yl", "c")


def swapped(x):
    return lax.ppermute(x, "c", [(0, 1), (1, 0)])


def to_sides(x, ny):
    perm = []
    for y in range(ny):
        perm.append((2 * y, 2 * ((y - 1) % ny)))
        perm.append((2 * y + 1, 2 * ((y + 1) % ny) + 1))
    return lax.ppermute(x, LANE, perm)


def dot(a, b, dims):
    return lax.dot_general(a, b, (dims, ((), ())), preferred_element_type=jnp.float32)


def part(p, q, ids, positive, scale):
    scores = dot(p, q, ((1,), (1,))) * scale
    hits = ids[:, None] == positive[None, :]
    top = jnp.max(scores, axis=0)
    expd = jnp.exp(scores - top[None, :])
    total = jnp.sum(expd, axis=0)
    pscore = jnp.sum(jnp.where(hits, scores, 0.0), axis=0)
    mix = dot(p, expd.astype(jnp.bfloat16), ((0,), (0,)))
    chosen = dot(p, hits.astype(jnp.bfloat16), ((0,), (0,)))
    return top, total, pscore, mix, chosen


def shards(queries, passages, positive):
    count, width = queries.shape
    rows = passages.shape[0]
    scale = 3.0 / math.sqrt(width)
    nz, nx = lax.axis_size("z"), lax.axis_size("x")
    ny = lax.axis_size("yh") * 2
    x, c = lax.axis_index("x"), lax.axis_index("c")
    y = lax.axis_index("yh") * 2 + lax.axis_index("yl")

    def ids_of(yy, cc):
        yy = yy % ny
        first = (((yy // 2) * nx + x) * nz * 2 + yy % 2) * 2 + cc
        local = lax.broadcasted_iota(jnp.int32, (nz, rows), 1)
        z = lax.broadcasted_iota(jnp.int32, (nz, rows), 0)
        return ((first + z * 4) * rows + local).reshape(-1)

    copies = jnp.broadcast_to(passages, (nz, rows, width))
    column = lax.all_to_all(copies, "z", split_axis=0, concat_axis=0, tiled=True)
    column = column.reshape(nz * rows, width)
    side = to_sides(column, ny)
    column2 = swapped(column)
    side2 = swapped(side)

    own = jnp.concatenate([column, column2], axis=0)
    own_ids = jnp.concatenate([ids_of(y, c), ids_of(y, 1 - c)])
    near = jnp.concatenate([side, side2], axis=0)
    at = y + 1 - 2 * c
    at2 = y - 1 + 2 * c
    near_ids = jnp.concatenate([ids_of(at, c), ids_of(at2, 1 - c)])

    top1, total1, ps1, mix1, ch1 = part(own, queries, own_ids, positive, scale)
    top2, total2, ps2, mix2, ch2 = part(near, queries, near_ids, positive, scale)
    top = jnp.maximum(top1, top2)
    f1, f2 = jnp.exp(top1 - top), jnp.exp(top2 - top)
    stats = jnp.stack([top, total1 * f1 + total2 * f2, ps1 + ps2])
    n_outer = lax.axis_size(OUTER)
    copies = jnp.broadcast_to(stats, (n_outer, *stats.shape))
    every = lax.all_to_all(copies, OUTER, split_axis=0, concat_axis=0, tiled=True)
    top_all = jnp.max(every[:, 0], axis=0)
    total = jnp.sum(every[:, 1] * jnp.exp(every[:, 0] - top_all[None, :]), axis=0)
    pscore = jnp.sum(every[:, 2], axis=0)
    inv = jnp.exp(top - top_all) / total
    out = mix1 * (f1 * inv)[None, :] + mix2 * (f2 * inv)[None, :] - (ch1 + ch2)
    out = out.astype(jnp.bfloat16).reshape(n_outer, width // n_outer, count)
    got = lax.all_to_all(out, OUTER, split_axis=0, concat_axis=0, tiled=True)
    grad = scale * jnp.sum(got.astype(jnp.float32), axis=0)
    loss = top_all + jnp.log(total) - pscore
    return grad.astype(jnp.bfloat16).T, loss


def solution(mesh):
    devices = mesh.devices
    torus = Mesh(devices.reshape(4, 4, 8, 2, 2), ("yh", "x", "z", "yl", "c"))
    in_specs = (P(INNER, None), P((*OUTER, *INNER), None), P(INNER))
    out_specs = (P(INNER, OUTER), P(INNER))
    return jax.shard_map(
        shards, mesh=torus, in_specs=in_specs, out_specs=out_specs, check_vma=False
    )
```

time: 150 us -> 117 us (0.78)
  waiting for transfers between devices: 86.5 us -> 38.7 us
  blocking collectives: 6.26 us -> 26.8 us
  matrix products: 7.91 us -> 17.5 us
  starting transfers between devices: 31.7 us -> 26.1 us
  other arithmetic: 8.21 us -> 3.22 us
  local copies, waits for them, and re-layouts: 7.7 us -> 2.99 us
    all_to_all x4 -> x2, waiting for transfers between devices: 86.5 us -> 30.5 us  [the longest x1 23 us: shards(): lax.all_to_all(copies, 'z', split_axis=0, concat_axis=0, tiled=True)]
    all_to_all x1, blocking collectives: 6.26 us -> 26.8 us  [shards(): got = lax.all_to_all(out, OUTER, split_axis=0, concat_axis=0, tiled=True)]
    all_to_all x4 -> x2, starting transfers between devices: 31.7 us -> 19.1 us  [the longest x1 10.3 us: shards(): lax.all_to_all(copies, 'z', split_axis=0, concat_axis=0, tiled=True)]
    dot_general x2 -> x6, matrix products: 7.91 us -> 17.5 us  [dot(): lax.dot_general(a, b, (dims, ((), ())), preferred_element_type=jnp.float32)]
    ppermute x0 -> x3, waiting for transfers between devices: none -> 8.21 us  [the longest x1 8.21 us: to_sides(): return lax.ppermute(x, LANE, perm)]
    ppermute x0 -> x3, starting transfers between devices: none -> 7.03 us  [the longest x2 4.68 us: swapped(): return lax.ppermute(x, 'c', [(0, 1), (1, 0)])]
    convert_element_type x3 -> x1, other arithmetic: 4.72 us -> 0.63 us  [shards(): return (grad.astype(jnp.bfloat16).T, loss)]
    unnamed x8 -> x7, local copies, waits for them, and re-layouts: 1.68 us -> 0.07 us
  transfers between devices with their start and end apart: 4 -> 5, of which waited for: 4 -> 3; matrix products, arithmetic and copies ran while one was open for 8% -> 11% of each run, Pallas kernels for 0% -> 0%
where the time goes in v1:
time: 117 us; the launch traced here: 116 us
  waiting for transfers between devices  38.7 us (33%)
  blocking collectives  26.8 us (23%)
  starting transfers between devices  26.1 us (22%)
  matrix products  17.5 us (15%)
  other arithmetic  3.22 us (3%)
  local copies, waits for them, and re-layouts  2.99 us (3%)
    all_to_all x1, blocking collectives, shards(): got = lax.all_to_all(out, OUTER, split_axis=0, concat_axis=0, tiled=True)  26.8 us
    all_to_all x1, waiting for transfers between devices, shards(): lax.all_to_all(copies, 'z', split_axis=0, concat_axis=0, tiled=True)  23 us
    dot_general x6, matrix products, dot(): lax.dot_general(a, b, (dims, ((), ())), preferred_element_type=jnp.float32)  17.5 us
    all_to_all x1, starting transfers between devices, shards(): lax.all_to_all(copies, 'z', split_axis=0, concat_axis=0, tiled=True)  10.3 us
    all_to_all x1, starting transfers between devices, shards(): lax.all_to_all(copies, OUTER, split_axis=0, concat_axis=0, tiled=True)  8.77 us
    ppermute x1, waiting for transfers between devices, to_sides(): return lax.ppermute(x, LANE, perm)  8.21 us
    all_to_all x1, waiting for transfers between devices, shards(): lax.all_to_all(copies, OUTER, split_axis=0, concat_axis=0, tiled=True)  7.57 us
    ppermute x2, starting transfers between devices, swapped(): return lax.ppermute(x, 'c', [(0, 1), (1, 0)])  4.68 us
  transfers between devices with their start and end apart: 5, of which 3 were waited for; matrix products, arithmetic and copies ran while one was open for 11% of the time, Pallas kernels for 0%

profile of v1, /device:TPU:8, one launch (start us, length us, event | category | flops | bytes accessed | tf_op | source)
XLA Modules:
  0.0 116.1 jit_solution(7328533539302943539)
XLA Ops:
  0.7 1.9 %broadcast_in_dim.9 = bf16[8,64,768]{2,1,0:T(8,128)(2,1)} broadcast(bf16[64,768]{1,0:T(8,128)(2,1)} %param.4), dimensions={1,2} | broadcast | bytes 884736 | tf_op jit(solution)/shard_map/broadcast_in_dim | solution.py:58
  2.6 10.3 %all-to-all-start = ((bf16[8,64,768]{2,1,0:T(8,128)(2,1)}), bf16[8,64,768]{2,1,0:T(8,128)(2,1)S(1)}, u32[]{:S(2)}, u32[]{:S(2)}) async-start(bf16[8,64,768]{2,1,0:T(8,128)(2,1)} %broadcast_in_dim.9), calls=%async_computation | async-start | bytes 1572864 | tf_op jit(solution)/shard_map/all_to_all | solution.py:59
  12.9 0.1 iota_add_fusion.1
  13.0 0.1 iota_add_fusion
  13.0 23.0 %all-to-all-done = bf16[8,64,768]{2,1,0:T(8,128)(2,1)S(1)} async-done(((bf16[8,64,768]{2,1,0:T(8,128)(2,1)}), bf16[8,64,768]{2,1,0:T(8,128)(2,1)S(1)}, u32[]{:S(2)}, u32[]{:S(2)}) %all-to-all-start) | async-done | bytes 786464 | tf_op jit(solution)/shard_map/all_to_all | solution.py:59
  36.0 2.3 %collective-permute-start.1 = (bf16[512,768]{1,0:T(8,128)(2,1)S(1)}, bf16[512,768]{1,0:T(8,128)(2,1)S(1)}, u32[]{:S(2)}, u32[]{:S(2)}) collective-permute-start(bf16[512,768]{1,0:T(8,128)(2,1)S(1)} %bitcast.26), channel_id=1, source_target_pairs={{0,386},{1,3},{2,0},{3,129},{128,2},{129,131},{130,128},{131,257},... | collective-permute-start | bytes 2359304 | tf_op jit(solution)/shard_map/ppermute | solution.py:23
  38.3 2.8 %collective-permute-start = (bf16[512,768]{1,0:T(8,128)(2,1)S(1)}, bf16[512,768]{1,0:T(8,128)(2,1)}, u32[]{:S(2)}, u32[]{:S(2)}) collective-permute-start(bf16[512,768]{1,0:T(8,128)(2,1)S(1)} %bitcast.27), channel_id=1, source_target_pairs={{0,1},{1,0},{2,3},{3,2},{4,5},{5,4},{6,7},{7,6},{8,9},{9,8},{10,11... | collective-permute-start | bytes 2359304 | tf_op jit(solution)/shard_map/ppermute | solution.py:15
  41.2 0.1 add.179
  41.2 0.1 add.189
  41.3 0.1 iota_add_fusion.3
  41.4 0.1 add.164
  41.5 0.1 iota_add_fusion.2
  41.6 0.1 add.169
  41.6 8.2 %collective-permute-done.1 = bf16[512,768]{1,0:T(8,128)(2,1)S(1)} collective-permute-done((bf16[512,768]{1,0:T(8,128)(2,1)S(1)}, bf16[512,768]{1,0:T(8,128)(2,1)S(1)}, u32[]{:S(2)}, u32[]{:S(2)}) %collective-permute-start.1) | collective-permute-done | bytes 786464 | tf_op jit(solution)/shard_map/ppermute | solution.py:23
  49.9 1.9 %collective-permute-start.2 = (bf16[512,768]{1,0:T(8,128)(2,1)S(1)}, bf16[512,768]{1,0:T(8,128)(2,1)S(1)}, u32[]{:S(2)}, u32[]{:S(2)}) collective-permute-start(bf16[512,768]{1,0:T(8,128)(2,1)S(1)} %collective-permute-done.1), channel_id=1, source_target_pairs={{0,1},{1,0},{2,3},{3,2},{4,5},{5,4},{6,7},{7,6},{8,9},{9,8},{10,11... | collective-permute-start | bytes 2359304 | tf_op jit(solution)/shard_map/ppermute | solution.py:15
  51.8 3.4 %fusion.2 = f32[768,512]{1,0:T(8,128)} fusion(s32[512]{0:T(512)S(1)} %copy-done.2, s32[1024]{0:T(1024)S(1)} %get-tuple-element.21, bf16[512,768]{1,0:T(8,128)(2,1)} %collective-permute-done, bf16[512,768]{1,0:T(8,128)(2,1)S(1)} %bitcast.28), kind=kOutput, calls=%fused_computation.3 | convolution fusion | flops 808976384 | bytes 3151872 | tf_op jit(solution)/shard_map/dot_general | solution.py:27
  55.2 0.1 constant_dynamic-update-slice_fusion.1
  55.2 2.2 %multiply_reduce_fusion.1 = (f32[512]{0:T(512)S(1)}, f32[1024,512]{1,0:T(8,128)S(1)}) fusion(bf16[512,768]{1,0:T(8,128)(2,1)S(1)} %copy-done, bf16[512,768]{1,0:T(8,128)(2,1)} %collective-permute-done, bf16[512,768]{1,0:T(8,128)(2,1)S(1)} %bitcast.29), kind=kOutput, calls=%fused_computation.15 | convolution fusion | flops 809500160 | bytes 4458496 | tf_op jit(solution)/shard_map/dot_general | solution.py:27
  57.4 3.3 %fusion.14 = f32[768,512]{1,0:T(8,128)} fusion(f32[1024,512]{1,0:T(8,128)S(1)} %get-tuple-element.20, f32[512]{0:T(512)S(1)} %get-tuple-element.19, bf16[512,768]{1,0:T(8,128)(2,1)} %collective-permute-done, bf16[512,768]{1,0:T(8,128)(2,1)S(1)} %bitcast.30), kind=kOutput, calls=%fused_computation.20 | convolution fusion | flops 810024960 | bytes 5244928 | tf_op jit(solution)/shard_map/dot_general | solution.py:27
  60.7 0.1 constant_dynamic-update-slice_fusion
  60.8 1.0 multiply_reduce_fusion
  61.8 1.4 %fusion.9 = (f32[512]{0:T(512)S(1)}, f32[512]{0:T(512)S(1)}, f32[512]{0:T(512)S(1)}, f32[512]{0:T(512)S(1)}) fusion(f32[1024,512]{1,0:T(8,128)S(1)} %get-tuple-element.18, f32[512]{0:T(512)S(1)} %get-tuple-element.17, s32[512]{0:T(512)S(1)} %copy-done.2, s32[1024]{0:T(1024)S(1)} %get-tuple-element.22, s32[1024]{0:T(1024)S(1)} %get-tuple-element.21, ...), kind=kLoop, calls=%fused_computation.13 | loop fusion | flops 6289408 | bytes 4216832 | tf_op jit(solution)/shard_map/reduce_sum | solution.py:35
  63.3 0.7 broadcast_in_dim.11
  64.0 8.8 %all-to-all-start.1 = ((f32[16,3,512]{2,1,0:T(4,128)}), f32[16,3,512]{2,1,0:T(4,128)S(1)}, u32[]{:S(2)}, u32[]{:S(2)}) async-start(f32[16,3,512]{2,1,0:T(4,128)} %broadcast_in_dim.11), calls=%async_computation.1 | async-start | bytes 262144 | tf_op jit(solution)/shard_map/all_to_all | solution.py:79
  72.7 3.6 %fusion.12 = f32[768,512]{1,0:T(8,128)} fusion(bf16[1024,768]{1,0:T(8,128)(2,1)} %copy-done.1, f32[1024,512]{1,0:T(8,128)S(1)} %get-tuple-element.18, f32[512]{0:T(512)S(1)} %get-tuple-element.17), kind=kOutput, calls=%fused_computation.19 | convolution fusion | flops 806879232 | bytes 5244928 | tf_op jit(solution)/shard_map/dot_general | solution.py:27
  76.3 7.6 %all-to-all-done.1 = f32[16,3,512]{2,1,0:T(4,128)S(1)} async-done(((f32[16,3,512]{2,1,0:T(4,128)}), f32[16,3,512]{2,1,0:T(4,128)S(1)}, u32[]{:S(2)}, u32[]{:S(2)}) %all-to-all-start.1) | async-done | bytes 98336 | tf_op jit(solution)/shard_map/all_to_all | solution.py:79
  83.9 0.1 slice_reduce_fusion
  84.0 0.6 exponential_multiply_fusion.1
  84.6 4.0 %subtract_convert_fusion = bf16[768,512]{1,0:T(8,128)(2,1)S(1)} fusion(f32[768,512]{1,0:T(8,128)} %fusion.2, f32[768,512]{1,0:T(8,128)} %fusion.12, f32[768,512]{1,0:T(8,128)} %fusion.14, bf16[1024,768]{1,0:T(8,128)(2,1)} %copy-done.1, s32[512]{0:T(512)S(1)} %copy-done.2, s32[1024]{0:T(1024)S(1)} %get-tuple-element.22, f32[512]{0:T(512)S(1)} %get-tuple-element.13, ...), kind=kOutput, calls=%fused_computation.18 | convolution fusion | flops 808189952 | bytes 7088128 | tf_op jit(solution)/shard_map/dot_general | solution.py:27
  88.6 26.8 %all_to_all.15 = bf16[16,48,512]{2,1,0:T(8,128)(2,1)S(1)} all-to-all(bf16[16,48,512]{2,1,0:T(8,128)(2,1)S(1)} %bitcast.31), channel_id=1, replica_groups=mesh['yh'=4,'x'=4,'z'=8,'yl'=2,'c'=2] {'yh','x'}, dimensions={0} | all-to-all | bytes 1572864 | tf_op jit(solution)/shard_map/all_to_all | solution.py:86
  115.4 0.1 convert_reduce_fusion
  115.5 0.6 fusion.25
  (17 shorter events, 0.1 us)
Async XLA Ops:
  0.6 54.6 %copy-start = (bf16[512,768]{1,0:T(8,128)(2,1)S(1)}, bf16[512,768]{1,0:T(8,128)(2,1)}, u32[]{:S(2)}) copy-start(bf16[512,768]{1,0:T(8,128)(2,1)} %param.3) | copy-start | bytes 2359300
  0.6 51.1 %copy-start.2 = (s32[512]{0:T(512)S(1)}, s32[512]{0:T(512)}, u32[]{:S(2)}) copy-start(s32[512]{0:T(512)} %param.5) | copy-start | bytes 6148
  2.6 33.4 %all-to-all-start = ((bf16[8,64,768]{2,1,0:T(8,128)(2,1)}), bf16[8,64,768]{2,1,0:T(8,128)(2,1)S(1)}, u32[]{:S(2)}, u32[]{:S(2)}) async-start(bf16[8,64,768]{2,1,0:T(8,128)(2,1)} %broadcast_in_dim.9), calls=%async_computation | async-start | bytes 1572864 | tf_op jit(solution)/shard_map/all_to_all | solution.py:59
  36.0 13.9 %collective-permute-start.1 = (bf16[512,768]{1,0:T(8,128)(2,1)S(1)}, bf16[512,768]{1,0:T(8,128)(2,1)S(1)}, u32[]{:S(2)}, u32[]{:S(2)}) collective-permute-start(bf16[512,768]{1,0:T(8,128)(2,1)S(1)} %bitcast.26), channel_id=1, source_target_pairs={{0,386},{1,3},{2,0},{3,129},{128,2},{129,131},{130,128},{131,257},... | collective-permute-start | bytes 2359304 | tf_op jit(solution)/shard_map/ppermute | solution.py:23
  38.3 13.4 %collective-permute-start = (bf16[512,768]{1,0:T(8,128)(2,1)S(1)}, bf16[512,768]{1,0:T(8,128)(2,1)}, u32[]{:S(2)}, u32[]{:S(2)}) collective-permute-start(bf16[512,768]{1,0:T(8,128)(2,1)S(1)} %bitcast.27), channel_id=1, source_target_pairs={{0,1},{1,0},{2,3},{3,2},{4,5},{5,4},{6,7},{7,6},{8,9},{9,8},{10,11... | collective-permute-start | bytes 2359304 | tf_op jit(solution)/shard_map/ppermute | solution.py:15
  49.9 10.9 %collective-permute-start.2 = (bf16[512,768]{1,0:T(8,128)(2,1)S(1)}, bf16[512,768]{1,0:T(8,128)(2,1)S(1)}, u32[]{:S(2)}, u32[]{:S(2)}) collective-permute-start(bf16[512,768]{1,0:T(8,128)(2,1)S(1)} %collective-permute-done.1), channel_id=1, source_target_pairs={{0,1},{1,0},{2,3},{3,2},{4,5},{5,4},{6,7},{7,6},{8,9},{9,8},{10,11... | collective-permute-start | bytes 2359304 | tf_op jit(solution)/shard_map/ppermute | solution.py:15
  60.8 2.4 %copy-start.1 = (bf16[1024,768]{1,0:T(8,128)(2,1)}, bf16[1024,768]{1,0:T(8,128)(2,1)S(1)}, u32[]{:S(2)}) copy-start(bf16[1024,768]{1,0:T(8,128)(2,1)S(1)} %constant_dynamic-update-slice_fusion) | copy-start | bytes 4718596
  64.0 20.0 %all-to-all-start.1 = ((f32[16,3,512]{2,1,0:T(4,128)}), f32[16,3,512]{2,1,0:T(4,128)S(1)}, u32[]{:S(2)}, u32[]{:S(2)}) async-start(f32[16,3,512]{2,1,0:T(4,128)} %broadcast_in_dim.11), calls=%async_computation.1 | async-start | bytes 262144 | tf_op jit(solution)/shard_map/all_to_all | solution.py:79

commit v2 on v1

v2 whole, which is shorter than its diff:
```python
import functools
import math

import jax
import jax.numpy as jnp
from jax import lax
from jax.experimental import pallas as pl
from jax.experimental.pallas import tpu as pltpu
from jax.sharding import Mesh
from jax.sharding import PartitionSpec as P

INNER = ("z", "yl", "c")
OUTER = ("yh", "x")
LANE = ("yh", "yl", "c")
F32, BF16 = jnp.float32, jnp.bfloat16
VMEM = pl.BlockSpec(memory_space=pltpu.VMEM)
SMEM = pl.BlockSpec(memory_space=pltpu.SMEM)


def swapped(x):
    return lax.ppermute(x, "c", [(0, 1), (1, 0)])


def to_sides(x, ny):
    perm = []
    for y in range(ny):
        perm.append((2 * y, 2 * ((y - 1) % ny)))
        perm.append((2 * y + 1, 2 * ((y + 1) % ny) + 1))
    return lax.ppermute(x, LANE, perm)


def dot(a, b, dims):
    return lax.dot_general(a, b, (dims, ((), ())), preferred_element_type=F32)


def hits_of(pos_ref, base, count, rows):
    j = lax.broadcasted_iota(jnp.int32, (count, 1), 0)
    return (j // rows) * (4 * rows) + j % rows == pos_ref[...] - base


def statistics(p_refs, bases, q_ref, pos_ref, s_ref, scale, rows):
    q = q_ref[...]
    top = ps = None
    for i, p_ref in enumerate(p_refs):
        n = p_ref.shape[0]
        s = dot(p_ref[...], q, ((1,), (1,))) * scale
        s_ref[i * n : (i + 1) * n, :] = s
        hit = hits_of(pos_ref, bases[i], n, rows)
        t = jnp.max(s, axis=0, keepdims=True)
        u = jnp.sum(jnp.where(hit, s, 0.0), axis=0, keepdims=True)
        top = t if top is None else jnp.maximum(top, t)
        ps = u if ps is None else ps + u
    return top, ps


def products(p_refs, bases, w_ref, pos_ref, rows):
    mix = chosen = 0.0
    for i, p_ref in enumerate(p_refs):
        n = p_ref.shape[0]
        p = p_ref[...]
        hit = hits_of(pos_ref, bases[i], n, rows).astype(F32).astype(BF16)
        mix += dot(p, w_ref[i * n : (i + 1) * n, :], ((0,), (0,)))
        chosen += dot(p, hit, ((0,), (0,)))
    return mix, chosen


def own_kernel(scale, rows, base_ref, a_ref, b_ref, q_ref, pos_ref, st_ref, mix_ref, ch_ref, s_ref, w_ref):
    bases = (base_ref[0], base_ref[1])
    top, ps = statistics((a_ref, b_ref), bases, q_ref, pos_ref, s_ref, scale, rows)
    e = jnp.exp(s_ref[...] - top)
    w_ref[...] = e.astype(BF16)
    st_ref[0:1, :] = top
    st_ref[1:2, :] = jnp.sum(e, axis=0, keepdims=True)
    st_ref[2:3, :] = ps
    mix, chosen = products((a_ref, b_ref), bases, w_ref, pos_ref, rows)
    mix_ref[...] = mix
    ch_ref[...] = chosen.astype(BF16)


def side_kernel(scale, rows, base_ref, a_ref, q_ref, pos_ref, s_ref, st_ref):
    top, ps = statistics((a_ref,), (base_ref[2],), q_ref, pos_ref, s_ref, scale, rows)
    st_ref[0:1, :] = top
    st_ref[2:3, :] = ps


def last_kernel(scale, rows, base_ref, b_ref, q_ref, pos_ref, st1_ref, st2_ref, sa_ref, st_ref, w_ref, out_ref, s_ref):
    n = b_ref.shape[0]
    top3, ps = statistics((b_ref,), (base_ref[3],), q_ref, pos_ref, s_ref, scale, rows)
    top1 = st1_ref[0:1, :]
    top = jnp.maximum(jnp.maximum(top1, st2_ref[0:1, :]), top3)
    f1 = jnp.exp(top1 - top)
    total = st1_ref[1:2, :] * f1
    for i, piece in enumerate((sa_ref, s_ref)):
        e = jnp.exp(piece[...] - top)
        w_ref[i * n : (i + 1) * n, :] = e.astype(BF16)
        total += jnp.sum(e, axis=0, keepdims=True)
    ps += st1_ref[2:3, :] + st2_ref[2:3, :]
    st_ref[0:1, :] = top
    st_ref[1:2, :] = f1
    stats = jnp.concatenate([top, total, ps, ps], axis=0)
    out_ref[...] = jnp.broadcast_to(stats[None], out_ref.shape)


def near_kernel(rows, base_ref, a_ref, b_ref, w_ref, pos_ref, st_ref, mix_ref, ch_ref, m_ref, c_ref):
    bases = (base_ref[2], base_ref[3])
    mix, chosen = products((a_ref, b_ref), bases, w_ref, pos_ref, rows)
    m_ref[...] = mix + mix_ref[...] * st_ref[1:2, :]
    c_ref[...] = chosen + ch_ref[...].astype(F32)


def scale_kernel(every_ref, st_ref, m_ref, c_ref, out_ref, fin_ref):
    tops = every_ref[:, 0, :]
    top = jnp.max(tops, axis=0, keepdims=True)
    total = jnp.sum(every_ref[:, 1, :] * jnp.exp(tops - top), axis=0, keepdims=True)
    ps = jnp.sum(every_ref[:, 2, :], axis=0, keepdims=True)
    g = jnp.exp(st_ref[0:1, :] - top) / total
    out_ref[...] = (m_ref[...] * g - c_ref[...]).astype(BF16)
    fin_ref[0:1, :] = top
    fin_ref[1:2, :] = total
    fin_ref[2:3, :] = ps


def call(body, out, operands, scratch=(), flops=0, name=None, vmem=20):
    out_shape = [jax.ShapeDtypeStruct(s, d) for s, d in out]
    return pl.pallas_call(
        body,
        in_specs=[SMEM if o.dtype == jnp.int32 and o.ndim == 1 else VMEM for o in operands],
        out_specs=[VMEM] * len(out),
        out_shape=out_shape,
        scratch_shapes=[pltpu.VMEM(s, d) for s, d in scratch],
        cost_estimate=pl.CostEstimate(flops=flops, bytes_accessed=4 << 20, transcendentals=0),
        compiler_params=pltpu.CompilerParams(vmem_limit_bytes=vmem << 20),
        name=name,
    )(*operands)


def shards(queries, passages, positive):
    count, width = queries.shape
    rows = passages.shape[0]
    scale = 3.0 / math.sqrt(width)
    nz, nx = lax.axis_size("z"), lax.axis_size("x")
    ny = lax.axis_size("yh") * 2
    n_outer = lax.axis_size(OUTER)
    x, c = lax.axis_index("x"), lax.axis_index("c")
    y = lax.axis_index("yh") * 2 + lax.axis_index("yl")
    n = nz * rows
    flops = 2 * n * width * count

    def base_of(yy, cc):
        yy = (yy + ny) & (ny - 1)
        return ((((yy >> 1) * nx + x) * nz * 2 + (yy & 1)) * 2 + cc) * rows

    base = jnp.stack([base_of(y, c), base_of(y, 1 - c), base_of(y + 1 - 2 * c, c), base_of(y - 1 + 2 * c, 1 - c)])
    pos = positive.reshape(1, count)

    copies = jnp.broadcast_to(passages, (nz, rows, width))
    column = lax.all_to_all(copies, "z", split_axis=0, concat_axis=0, tiled=True)
    column = column.reshape(n, width)
    side = to_sides(column, ny)
    column2 = swapped(column)
    st1, mix1, ch1 = call(
        functools.partial(own_kernel, scale, rows),
        [((8, count), F32), ((width, count), F32), ((width, count), BF16)],
        (base, column, column2, queries, pos),
        [((2 * n, count), F32), ((2 * n, count), BF16)],
        6 * flops,
        "own",
    )
    side, st1 = lax.optimization_barrier((side, st1))
    side2 = swapped(side)
    scores, st2 = call(
        functools.partial(side_kernel, scale, rows),
        [((n, count), F32), ((8, count), F32)],
        (base, side, queries, pos),
        (),
        flops,
        "side",
    )
    st, weights, stats = call(
        functools.partial(last_kernel, scale, rows),
        [((8, count), F32), ((2 * n, count), BF16), ((n_outer, 4, count), F32)],
        (base, side2, queries, pos, st1, st2, scores),
        [((n, count), F32)],
        flops,
        "last",
    )
    every = lax.all_to_all(stats, OUTER, split_axis=0, concat_axis=0, tiled=True)
    m, ch = call(
        functools.partial(near_kernel, rows),
        [((width, count), F32), ((width, count), F32)],
        (base, side, side2, weights, pos, st, mix1, ch1),
        (),
        4 * flops,
        "near",
    )
    out, fin = call(
        scale_kernel,
        [((width, count), BF16), ((8, count), F32)],
        (every, st, m, ch),
        (),
        0,
        "scale",
    )
    out = out.reshape(n_outer, width // n_outer, count)
    got = lax.all_to_all(out, OUTER, split_axis=0, concat_axis=0, tiled=True)
    grad = scale * jnp.sum(got.astype(F32), axis=0)
    loss = fin[0] + jnp.log(fin[1]) - fin[2]
    return grad.astype(BF16).T, loss


def solution(mesh):
    devices = mesh.devices
    torus = Mesh(devices.reshape(4, 4, 8, 2, 2), ("yh", "x", "z", "yl", "c"))
    in_specs = (P(INNER, None), P((*OUTER, *INNER), None), P(INNER))
    out_specs = (P(INNER, OUTER), P(INNER))
    return jax.shard_map(
        shards, mesh=torus, in_specs=in_specs, out_specs=out_specs, check_vma=False
    )
```

time: 117 us -> 112 us (0.957)
  the two profiles are of different devices: /device:TPU:8 before, /device:TPU:1 now
where the time goes in v2:
time: 112 us; the launch traced here: 111 us
  blocking collectives  32.4 us (29%)
  waiting for transfers between devices  28.7 us (26%)
  starting transfers between devices  26.7 us (24%)
  local copies, waits for them, and re-layouts  11 us (10%)
  Pallas kernels  9.99 us (9%)
  other arithmetic  1.41 us (1%)
    all_to_all x1, blocking collectives, shards(): lax.all_to_all(copies, 'z', split_axis=0, concat_axis=0, tiled=True)  32.4 us
    all_to_all x1, waiting for transfers between devices, shards(): got = lax.all_to_all(out, OUTER, split_axis=0, concat_axis=0, tiled=True)  21.8 us
    pallas_call x5, Pallas kernels, call(): pl.pallas_call(body, in_specs=[SMEM if o.dtype == jnp.int32 and o.ndim ==...  9.99 us
    unnamed x26, local copies, waits for them, and re-layouts  9.94 us
    all_to_all x1, starting transfers between devices, shards(): lax.all_to_all(stats, OUTER, split_axis=0, concat_axis=0, tiled=True)  8.82 us
    all_to_all x1, starting transfers between devices, shards(): got = lax.all_to_all(out, OUTER, split_axis=0, concat_axis=0, tiled=True)  8.12 us
    ppermute x2, starting transfers between devices, swapped(): return lax.ppermute(x, 'c', [(0, 1), (1, 0)])  6.54 us
    ppermute x1, waiting for transfers between devices, to_sides(): return lax.ppermute(x, LANE, perm)  5.26 us
  transfers between devices with their start and end apart: 5, of which 4 were waited for; matrix products, arithmetic and copies ran while one was open for 1% of the time, Pallas kernels for 7%

profile of v2, /device:TPU:1, one launch (start us, length us, event | category | flops | bytes accessed | tf_op | source)
XLA Modules:
  0.0 110.9 jit_solution(15667618310493438128)
XLA Ops:
  0.6 0.0 copy-start
  0.6 1.0 broadcast_in_dim.3
  1.7 32.4 %all_to_all.15 = bf16[8,64,768]{2,1,0:T(8,128)(2,1)S(1)} all-to-all(bf16[8,64,768]{2,1,0:T(8,128)(2,1)S(1)} %broadcast_in_dim.3), channel_id=1, replica_groups=mesh['yh'=4,'x'=4,'z'=8,'yl'=2,'c'=2] {'z'}, dimensions={0} | all-to-all | bytes 1572864 | tf_op jit(solution)/shard_map/all_to_all | solution.py:157
  34.1 4.2 %collective-permute-start.1 = (bf16[512,768]{1,0:T(8,128)(2,1)S(1)}, bf16[512,768]{1,0:T(8,128)(2,1)S(1)}, u32[]{:S(2)}, u32[]{:S(2)}) collective-permute-start(bf16[512,768]{1,0:T(8,128)(2,1)S(1)} %bitcast.10), channel_id=1, source_target_pairs={{0,1},{1,0},{2,3},{3,2},{4,5},{5,4},{6,7},{7,6},{8,9},{9,8},{10,11... | collective-permute-start | bytes 2359304 | tf_op jit(solution)/shard_map/ppermute | solution.py:21
  38.3 3.2 %collective-permute-start = (bf16[512,768]{1,0:T(8,128)(2,1)S(1)}, bf16[512,768]{1,0:T(8,128)(2,1)S(1)}, u32[]{:S(2)}, u32[]{:S(2)}) collective-permute-start(bf16[512,768]{1,0:T(8,128)(2,1)S(1)} %bitcast.11), channel_id=1, source_target_pairs={{0,386},{1,3},{2,0},{3,129},{128,2},{129,131},{130,128},{131,257},... | collective-permute-start | bytes 2359304 | tf_op jit(solution)/shard_map/ppermute | solution.py:29
  41.5 0.1 pad_add_fusion.base_ref
  41.6 0.0 collective-permute-done.1.b_ref
  41.6 3.8 %own.1 = (f32[8,512]{1,0:T(8,128)S(1)}, f32[768,512]{1,0:T(8,128)S(1)}, bf16[768,512]{1,0:T(8,128)(2,1)S(1)}) custom-call(s32[4]{0:T(128)S(1)} %pad_add_fusion.base_ref, bf16[512,768]{1,0:T(8,128)(2,1)S(1)} %bitcast.12, bf16[512,768]{1,0:T(8,128)(2,1)S(1)} %collective-permute-done.1.b_ref, bf16[512,768]{1,0:T(8,128)(2,1)S(1)} %copy-done, s32[1,512]{1,0:T(1,128)S(1)} %bitcast.14), custom_call_target="tpu_custom_call" | custom-call | flops 2415919104 | bytes 4194304 | tf_op jit(solution)/shard_map/own/pallas_call | solution.py:125
  45.5 1.2 %copy-done.9 = f32[768,512]{1,0:T(8,128)} copy-done((f32[768,512]{1,0:T(8,128)}, f32[768,512]{1,0:T(8,128)S(1)}, u32[]{:S(2)}) %copy-start.9) | copy-done | bytes 1572888
  46.6 0.9 copy-done.11
  47.5 5.3 %collective-permute-done.a_ref = bf16[512,768]{1,0:T(8,128)(2,1)S(1)} collective-permute-done((bf16[512,768]{1,0:T(8,128)(2,1)S(1)}, bf16[512,768]{1,0:T(8,128)(2,1)S(1)}, u32[]{:S(2)}, u32[]{:S(2)}) %collective-permute-start) | collective-permute-done | bytes 786464 | tf_op jit(solution)/shard_map/ppermute | solution.py:29
  52.8 2.3 %collective-permute-start.2 = (bf16[512,768]{1,0:T(8,128)(2,1)S(1)}, bf16[512,768]{1,0:T(8,128)(2,1)S(1)}, u32[]{:S(2)}, u32[]{:S(2)}) collective-permute-start(bf16[512,768]{1,0:T(8,128)(2,1)S(1)} %collective-permute-done.a_ref), channel_id=1, source_target_pairs={{0,1},{1,0},{2,3},{3,2},{4,5},{5,4},{6,7},{7,6},{8,9},{9,8},{10,11... | collective-permute-start | bytes 2359304 | tf_op jit(solution)/shard_map/ppermute | solution.py:21
  55.1 1.2 %side.1 = (f32[512,512]{1,0:T(8,128)S(1)}, f32[8,512]{1,0:T(8,128)S(1)}) custom-call(s32[4]{0:T(128)S(1)} %pad_add_fusion.base_ref, bf16[512,768]{1,0:T(8,128)(2,1)S(1)} %collective-permute-done.a_ref, bf16[512,768]{1,0:T(8,128)(2,1)S(1)} %copy-done, s32[1,512]{1,0:T(1,128)S(1)} %bitcast.15), custom_call_target="tpu_custom_call" | custom-call | flops 402653184 | bytes 4194304 | tf_op jit(solution)/shard_map/side/pallas_call | solution.py:125
  56.3 0.7 collective-permute-done.2.b_ref
  57.0 2.4 %last.1 = (f32[8,512]{1,0:T(8,128)S(1)}, bf16[1024,512]{1,0:T(8,128)(2,1)S(1)}, f32[16,4,512]{2,1,0:T(4,128)}) custom-call(s32[4]{0:T(128)S(1)} %pad_add_fusion.base_ref, bf16[512,768]{1,0:T(8,128)(2,1)S(1)} %collective-permute-done.2.b_ref, bf16[512,768]{1,0:T(8,128)(2,1)S(1)} %copy-done, s32[1,512]{1,0:T(1,128)S(1)} %bitcast.16, ...), custom_call_target="tpu_custom_call" | custom-call | flops 402653184 | bytes 4194304 | tf_op jit(solution)/shard_map/last/pallas_call | solution.py:125
  59.4 0.0 copy-done.1
  59.4 1.0 copy-done.7
  60.4 8.8 %all-to-all-start.1 = ((f32[16,4,512]{2,1,0:T(4,128)}), f32[16,4,512]{2,1,0:T(4,128)S(1)}, u32[]{:S(2)}, u32[]{:S(2)}) async-start(f32[16,4,512]{2,1,0:T(4,128)} %get-tuple-element.21), calls=%async_computation.1 | async-start | bytes 262144 | tf_op jit(solution)/shard_map/all_to_all | solution.py:187
  69.2 1.1 %copy-done.2 = bf16[512,768]{1,0:T(8,128)(2,1)S(1)} copy-done((bf16[512,768]{1,0:T(8,128)(2,1)S(1)}, bf16[512,768]{1,0:T(8,128)(2,1)}, u32[]{:S(2)}) %copy-start.2) | copy-done | bytes 786456
  70.3 1.1 %copy-done.5 = bf16[512,768]{1,0:T(8,128)(2,1)S(1)} copy-done((bf16[512,768]{1,0:T(8,128)(2,1)S(1)}, bf16[512,768]{1,0:T(8,128)(2,1)}, u32[]{:S(2)}) %copy-start.5) | copy-done | bytes 786456
  71.5 1.2 %copy-done.8 = bf16[1024,512]{1,0:T(8,128)(2,1)S(1)} copy-done((bf16[1024,512]{1,0:T(8,128)(2,1)S(1)}, bf16[1024,512]{1,0:T(8,128)(2,1)}, u32[]{:S(2)}) %copy-start.8) | copy-done | bytes 1048600
  72.7 1.4 %copy-done.10 = f32[768,512]{1,0:T(8,128)S(1)} copy-done((f32[768,512]{1,0:T(8,128)S(1)}, f32[768,512]{1,0:T(8,128)}, u32[]{:S(2)}) %copy-start.10) | copy-done | bytes 1572888
  74.1 1.1 %copy-done.12 = bf16[768,512]{1,0:T(8,128)(2,1)S(1)} copy-done((bf16[768,512]{1,0:T(8,128)(2,1)S(1)}, bf16[768,512]{1,0:T(8,128)(2,1)}, u32[]{:S(2)}) %copy-start.12) | copy-done | bytes 786456
  75.2 2.4 %near.1 = (f32[768,512]{1,0:T(8,128)S(1)}, f32[768,512]{1,0:T(8,128)S(1)}) custom-call(s32[4]{0:T(128)S(1)} %pad_add_fusion.base_ref, bf16[512,768]{1,0:T(8,128)(2,1)S(1)} %copy-done.2, bf16[512,768]{1,0:T(8,128)(2,1)S(1)} %copy-done.5, bf16[1024,512]{1,0:T(8,128)(2,1)S(1)} %copy-done.8, s32[1,512]{1,0:T(1,128)S(1)} %bitcast.17, ...), custom_call_target="tpu_custom_call" | custom-call | flops 1610612736 | bytes 4194304 | tf_op jit(solution)/shard_map/near/pallas_call | solution.py:125
  77.6 0.9 all-to-all-done.1.every_ref
  78.5 0.2 scale.1
  78.7 0.9 copy-done.3
  79.6 8.1 %all-to-all-start.2 = ((bf16[16,48,512]{2,1,0:T(8,128)(2,1)}), bf16[16,48,512]{2,1,0:T(8,128)(2,1)S(1)}, u32[]{:S(2)}, u32[]{:S(2)}) async-start(bf16[16,48,512]{2,1,0:T(8,128)(2,1)} %bitcast.13), calls=%async_computation.2 | async-start | bytes 1572864 | tf_op jit(solution)/shard_map/all_to_all | solution.py:205
  87.8 0.6 slice_subtract_fusion
  88.4 21.8 %all-to-all-done.2 = bf16[16,48,512]{2,1,0:T(8,128)(2,1)S(1)} async-done(((bf16[16,48,512]{2,1,0:T(8,128)(2,1)}), bf16[16,48,512]{2,1,0:T(8,128)(2,1)S(1)}, u32[]{:S(2)}, u32[]{:S(2)}) %all-to-all-start.2) | async-done | bytes 786464 | tf_op jit(solution)/shard_map/all_to_all | solution.py:205
  110.2 0.1 convert_reduce_fusion
  110.3 0.6 fusion
  (15 shorter events, 0.0 us)
Async XLA Ops:
  0.6 41.0 %copy-start = (bf16[512,768]{1,0:T(8,128)(2,1)S(1)}, bf16[512,768]{1,0:T(8,128)(2,1)}, u32[]{:S(2)}) copy-start(bf16[512,768]{1,0:T(8,128)(2,1)} %q_ref.5) | copy-start | bytes 2359300
  0.6 41.0 %copy-start.6 = (s32[512]{0:T(512)S(1)}, s32[512]{0:T(512)}, u32[]{:S(2)}) copy-start(s32[512]{0:T(512)} %param.5) | copy-start | bytes 6148
  34.1 7.6 %collective-permute-start.1 = (bf16[512,768]{1,0:T(8,128)(2,1)S(1)}, bf16[512,768]{1,0:T(8,128)(2,1)S(1)}, u32[]{:S(2)}, u32[]{:S(2)}) collective-permute-start(bf16[512,768]{1,0:T(8,128)(2,1)S(1)} %bitcast.10), channel_id=1, source_target_pairs={{0,1},{1,0},{2,3},{3,2},{4,5},{5,4},{6,7},{7,6},{8,9},{9,8},{10,11... | collective-permute-start | bytes 2359304 | tf_op jit(solution)/shard_map/ppermute | solution.py:21
  38.3 14.5 %collective-permute-start = (bf16[512,768]{1,0:T(8,128)(2,1)S(1)}, bf16[512,768]{1,0:T(8,128)(2,1)S(1)}, u32[]{:S(2)}, u32[]{:S(2)}) collective-permute-start(bf16[512,768]{1,0:T(8,128)(2,1)S(1)} %bitcast.11), channel_id=1, source_target_pairs={{0,386},{1,3},{2,0},{3,129},{128,2},{129,131},{130,128},{131,257},... | collective-permute-start | bytes 2359304 | tf_op jit(solution)/shard_map/ppermute | solution.py:29
  45.5 1.2 %copy-start.9 = (f32[768,512]{1,0:T(8,128)}, f32[768,512]{1,0:T(8,128)S(1)}, u32[]{:S(2)}) copy-start(f32[768,512]{1,0:T(8,128)S(1)} %get-tuple-element.24.mix_ref) | copy-start | bytes 4718596
  46.6 0.9 copy-start.11
  52.8 6.6 %copy-start.1 = (bf16[512,768]{1,0:T(8,128)(2,1)}, bf16[512,768]{1,0:T(8,128)(2,1)S(1)}, u32[]{:S(2)}) copy-start(bf16[512,768]{1,0:T(8,128)(2,1)S(1)} %collective-permute-done.a_ref) | copy-start | bytes 2359300
  52.8 4.2 %collective-permute-start.2 = (bf16[512,768]{1,0:T(8,128)(2,1)S(1)}, bf16[512,768]{1,0:T(8,128)(2,1)S(1)}, u32[]{:S(2)}, u32[]{:S(2)}) collective-permute-start(bf16[512,768]{1,0:T(8,128)(2,1)S(1)} %collective-permute-done.a_ref), channel_id=1, source_target_pairs={{0,1},{1,0},{2,3},{3,2},{4,5},{5,4},{6,7},{7,6},{8,9},{9,8},{10,11... | collective-permute-start | bytes 2359304 | tf_op jit(solution)/shard_map/ppermute | solution.py:21
  57.0 2.4 %copy-start.4 = (bf16[512,768]{1,0:T(8,128)(2,1)}, bf16[512,768]{1,0:T(8,128)(2,1)S(1)}, u32[]{:S(2)}) copy-start(bf16[512,768]{1,0:T(8,128)(2,1)S(1)} %collective-permute-done.2.b_ref) | copy-start | bytes 2359300
  59.4 1.0 copy-start.7
  60.4 18.2 %all-to-all-start.1 = ((f32[16,4,512]{2,1,0:T(4,128)}), f32[16,4,512]{2,1,0:T(4,128)S(1)}, u32[]{:S(2)}, u32[]{:S(2)}) async-start(f32[16,4,512]{2,1,0:T(4,128)} %get-tuple-element.21), calls=%async_computation.1 | async-start | bytes 262144 | tf_op jit(solution)/shard_map/all_to_all | solution.py:187
  69.2 1.1 %copy-start.2 = (bf16[512,768]{1,0:T(8,128)(2,1)S(1)}, bf16[512,768]{1,0:T(8,128)(2,1)}, u32[]{:S(2)}) copy-start(bf16[512,768]{1,0:T(8,128)(2,1)} %copy-done.1) | copy-start | bytes 2359300
  70.3 1.1 %copy-start.5 = (bf16[512,768]{1,0:T(8,128)(2,1)S(1)}, bf16[512,768]{1,0:T(8,128)(2,1)}, u32[]{:S(2)}) copy-start(bf16[512,768]{1,0:T(8,128)(2,1)} %copy-done.4) | copy-start | bytes 2359300
  71.5 1.2 %copy-start.8 = (bf16[1024,512]{1,0:T(8,128)(2,1)S(1)}, bf16[1024,512]{1,0:T(8,128)(2,1)}, u32[]{:S(2)}) copy-start(bf16[1024,512]{1,0:T(8,128)(2,1)} %copy-done.7) | copy-start | bytes 3145732
  72.7 1.4 %copy-start.10 = (f32[768,512]{1,0:T(8,128)S(1)}, f32[768,512]{1,0:T(8,128)}, u32[]{:S(2)}) copy-start(f32[768,512]{1,0:T(8,128)} %copy-done.9) | copy-start | bytes 4718596
  74.1 1.1 %copy-start.12 = (bf16[768,512]{1,0:T(8,128)(2,1)S(1)}, bf16[768,512]{1,0:T(8,128)(2,1)}, u32[]{:S(2)}) copy-start(bf16[768,512]{1,0:T(8,128)(2,1)} %copy-done.11) | copy-start | bytes 2359300
  78.7 0.9 copy-start.3
  79.6 30.5 %all-to-all-start.2 = ((bf16[16,48,512]{2,1,0:T(8,128)(2,1)}), bf16[16,48,512]{2,1,0:T(8,128)(2,1)S(1)}, u32[]{:S(2)}, u32[]{:S(2)}) async-start(bf16[16,48,512]{2,1,0:T(8,128)(2,1)} %bitcast.13), calls=%async_computation.2 | async-start | bytes 1572864 | tf_op jit(solution)/shard_map/all_to_all | solution.py:205

commit v3 on v2

--- a/solution.py
+++ b/solution.py
@@ -64,60 +64,103 @@
     return mix, chosen
 
 
+def flash(p_refs, bases, q_ref, pos_ref, s_ref, w_ref, scale, rows):
+    top, ps = statistics(p_refs, bases, q_ref, pos_ref, s_ref, scale, rows)
+    e = jnp.exp(s_ref[...] - top)
+    w_ref[...] = e.astype(BF16)
+    total = jnp.sum(e, axis=0, keepdims=True)
+    mix, chosen = products(p_refs, bases, w_ref, pos_ref, rows)
+    return top, total, ps, mix, chosen
+
+
+def merged(st_ref, mix_ref, ch_ref, part):
+    top, total, ps, mix, chosen = part
+    both = jnp.maximum(st_ref[0:1, :], top)
+    f, g = jnp.exp(st_ref[0:1, :] - both), jnp.exp(top - both)
+    total = st_ref[1:2, :] * f + total * g
+    ps += st_ref[2:3, :]
+    return both, total, ps, mix_ref[...] * f + mix * g, ch_ref[...].astype(F32) + chosen
+
+
+def put(refs, part):
+    st_ref, mix_ref, ch_ref = refs
+    top, total, ps, mix, chosen = part
+    st_ref[0:1, :] = top
+    st_ref[1:2, :] = total
+    st_ref[2:3, :] = ps
+    mix_ref[...] = mix
+    ch_ref[...] = chosen.astype(BF16)
+
+
 def own_kernel(scale, rows, base_ref, a_ref, b_ref, q_ref, pos_ref, st_ref, mix_ref, ch_ref, s_ref, w_ref):
     bases = (base_ref[0], base_ref[1])
-    top, ps = statistics((a_ref, b_ref), bases, q_ref, pos_ref, s_ref, scale, rows)
-    e = jnp.exp(s_ref[...] - top)
-    w_ref[...] = e.astype(BF16)
-    st_ref[0:1, :] = top
-    st_ref[1:2, :] = jnp.sum(e, axis=0, keepdims=True)
-    st_ref[2:3, :] = ps
-    mix, chosen = products((a_ref, b_ref), bases, w_ref, pos_ref, rows)
-    mix_ref[...] = mix
-    ch_ref[...] = chosen.astype(BF16)
-
-
-def side_kernel(scale, rows, base_ref, a_ref, q_ref, pos_ref, s_ref, st_ref):
-    top, ps = statistics((a_ref,), (base_ref[2],), q_ref, pos_ref, s_ref, scale, rows)
-    st_ref[0:1, :] = top
-    st_ref[2:3, :] = ps
-
-
-def last_kernel(scale, rows, base_ref, b_ref, q_ref, pos_ref, st1_ref, st2_ref, sa_ref, st_ref, w_ref, out_ref, s_ref):
-    n = b_ref.shape[0]
-    top3, ps = statistics((b_ref,), (base_ref[3],), q_ref, pos_ref, s_ref, scale, rows)
-    top1 = st1_ref[0:1, :]
-    top = jnp.maximum(jnp.maximum(top1, st2_ref[0:1, :]), top3)
-    f1 = jnp.exp(top1 - top)
-    total = st1_ref[1:2, :] * f1
-    for i, piece in enumerate((sa_ref, s_ref)):
-        e = jnp.exp(piece[...] - top)
-        w_ref[i * n : (i + 1) * n, :] = e.astype(BF16)
-        total += jnp.sum(e, axis=0, keepdims=True)
-    ps += st1_ref[2:3, :] + st2_ref[2:3, :]
-    st_ref[0:1, :] = top
-    st_ref[1:2, :] = f1
-    stats = jnp.concatenate([top, total, ps, ps], axis=0)
-    out_ref[...] = jnp.broadcast_to(stats[None], out_ref.shape)
-
-
-def near_kernel(rows, base_ref, a_ref, b_ref, w_ref, pos_ref, st_ref, mix_ref, ch_ref, m_ref, c_ref):
-    bases = (base_ref[2], base_ref[3])
-    mix, chosen = products((a_ref, b_ref), bases, w_ref, pos_ref, rows)
-    m_ref[...] = mix + mix_ref[...] * st_ref[1:2, :]
-    c_ref[...] = chosen + ch_ref[...].astype(F32)
-
-
-def scale_kernel(every_ref, st_ref, m_ref, c_ref, out_ref, fin_ref):
-    tops = every_ref[:, 0, :]
-    top = jnp.max(tops, axis=0, keepdims=True)
-    total = jnp.sum(every_ref[:, 1, :] * jnp.exp(tops - top), axis=0, keepdims=True)
-    ps = jnp.sum(every_ref[:, 2, :], axis=0, keepdims=True)
-    g = jnp.exp(st_ref[0:1, :] - top) / total
-    out_ref[...] = (m_ref[...] * g - c_ref[...]).astype(BF16)
-    fin_ref[0:1, :] = top
-    fin_ref[1:2, :] = total
-    fin_ref[2:3, :] = ps
+    put((st_ref, mix_ref, ch_ref), flash((a_ref, b_ref), bases, q_ref, pos_ref, s_ref, w_ref, scale, rows))
+
+
+def side_kernel(scale, rows, base_ref, a_ref, q_ref, pos_ref, st0_ref, mix0_ref, ch0_ref, st_ref, mix_ref, ch_ref, s_ref, w_ref):
+    part = flash((a_ref,), (base_ref[2],), q_ref, pos_ref, s_ref, w_ref, scale, rows)
+    put((st_ref, mix_ref, ch_ref), merged(st0_ref, mix0_ref, ch0_ref, part))
+
+
+def split3(v):
+    a = v.astype(BF16).astype(F32)
+    b = (v - a).astype(BF16).astype(F32)
+    return [a, b, v - a - b]
+
+
+def stat_rows(top, total, ps):
+    parts = split3(top) + split3(total) + split3(ps)
+    parts.append(jnp.zeros((16 - len(parts), top.shape[1]), F32))
+    return jnp.concatenate(parts, axis=0).astype(BF16)
+
+
+def last_kernel(scale, rows, nx, base_ref, b_ref, q_ref, pos_ref, st0_ref, mix0_ref, ch0_ref, out_ref, s_ref, w_ref):
+    part = flash((b_ref,), (base_ref[3],), q_ref, pos_ref, s_ref, w_ref, scale, rows)
+    top, total, ps, mix, chosen = merged(st0_ref, mix0_ref, ch0_ref, part)
+    mix, chosen = mix.astype(BF16), chosen.astype(BF16)
+    stats = stat_rows(top, total, ps)
+    width = mix.shape[0] // nx
+    piece = width // 4
+    for x in range(nx):
+        for y in range(4):
+            at = (y * nx + x) * piece
+            out_ref[x, y * piece : (y + 1) * piece, :] = mix[at : at + piece]
+            out_ref[x, width + y * piece : width + (y + 1) * piece, :] = chosen[at : at + piece]
+        out_ref[x, 2 * width :, :] = stats
+
+
+def combined(got_ref):
+    n = got_ref.shape[0]
+    width = (got_ref.shape[1] - 16) // 2
+    stats = [got_ref[i, 2 * width :, :].astype(F32) for i in range(n)]
+    three = [[s[3 * k : 3 * k + 1] + s[3 * k + 1 : 3 * k + 2] + s[3 * k + 2 : 3 * k + 3] for k in range(3)] for s in stats]
+    top = functools.reduce(jnp.maximum, [t[0] for t in three])
+    total = ps = mix = chosen = 0.0
+    for i in range(n):
+        f = jnp.exp(three[i][0] - top)
+        total += three[i][1] * f
+        ps += three[i][2]
+        mix += got_ref[i, :width, :].astype(F32) * f
+        chosen += got_ref[i, width : 2 * width, :].astype(F32)
+    return top, total, ps, mix, chosen
+
+
+def middle_kernel(got_ref, out_ref):
+    top, total, ps, mix, chosen = combined(got_ref)
+    mix, chosen = mix.astype(BF16), chosen.astype(BF16)
+    stats = stat_rows(top, total, ps)
+    n = out_ref.shape[0]
+    piece = mix.shape[0] // n
+    for y in range(n):
+        out_ref[y, :piece, :] = mix[y * piece : (y + 1) * piece]
+        out_ref[y, piece : 2 * piece, :] = chosen[y * piece : (y + 1) * piece]
+        out_ref[y, 2 * piece :, :] = stats
+
+
+def final_kernel(scale, got_ref, grad_ref, loss_ref):
+    top, total, ps, mix, chosen = combined(got_ref)
+    grad_ref[...] = (scale * (mix / total - chosen)).astype(BF16)
+    loss_ref[...] = top + jnp.log(total) - ps
 
 
 def call(body, out, operands, scratch=(), flops=0, name=None, vmem=20):
@@ -140,7 +183,6 @@
     scale = 3.0 / math.sqrt(width)
     nz, nx = lax.axis_size("z"), lax.axis_size("x")
     ny = lax.axis_size("yh") * 2
-    n_outer = lax.axis_size(OUTER)
     x, c = lax.axis_index("x"), lax.axis_index("c")
     y = lax.axis_index("yh") * 2 + lax.axis_index("yl")
     n = nz * rows
@@ -168,44 +210,34 @@
     )
     side, st1 = lax.optimization_barrier((side, st1))
     side2 = swapped(side)
-    scores, st2 = call(
+    st2, mix2, ch2 = call(
         functools.partial(side_kernel, scale, rows),
-        [((n, count), F32), ((8, count), F32)],
-        (base, side, queries, pos),
-        (),
-        flops,
+        [((8, count), F32), ((width, count), F32), ((width, count), BF16)],
+        (base, side, queries, pos, st1, mix1, ch1),
+        [((n, count), F32), ((n, count), BF16)],
+        3 * flops,
         "side",
     )
-    st, weights, stats = call(
-        functools.partial(last_kernel, scale, rows),
-        [((8, count), F32), ((2 * n, count), BF16), ((n_outer, 4, count), F32)],
-        (base, side2, queries, pos, st1, st2, scores),
-        [((n, count), F32)],
-        flops,
+    nyh = ny // 2
+    (out,) = call(
+        functools.partial(last_kernel, scale, rows, nx),
+        [((nx, 2 * width // nx + 16, count), BF16)],
+        (base, side2, queries, pos, st2, mix2, ch2),
+        [((n, count), F32), ((n, count), BF16)],
+        3 * flops,
         "last",
     )
-    every = lax.all_to_all(stats, OUTER, split_axis=0, concat_axis=0, tiled=True)
-    m, ch = call(
-        functools.partial(near_kernel, rows),
-        [((width, count), F32), ((width, count), F32)],
-        (base, side, side2, weights, pos, st, mix1, ch1),
-        (),
-        4 * flops,
-        "near",
-    )
-    out, fin = call(
-        scale_kernel,
-        [((width, count), BF16), ((8, count), F32)],
-        (every, st, m, ch),
-        (),
-        0,
-        "scale",
-    )
-    out = out.reshape(n_outer, width // n_outer, count)
-    got = lax.all_to_all(out, OUTER, split_axis=0, concat_axis=0, tiled=True)
-    grad = scale * jnp.sum(got.astype(F32), axis=0)
-    loss = fin[0] + jnp.log(fin[1]) - fin[2]
-    return grad.astype(BF16).T, loss
+    got = lax.all_to_all(out, "x", split_axis=0, concat_axis=0, tiled=True)
+    piece = width // (nx * nyh)
+    (out,) = call(middle_kernel, [((nyh, 2 * piece + 16, count), BF16)], (got,), name="middle")
+    got = lax.all_to_all(out, "yh", split_axis=0, concat_axis=0, tiled=True)
+    grad, loss = call(
+        functools.partial(final_kernel, scale),
+        [((piece, count), BF16), ((1, count), F32)],
+        (got,),
+        name="final",
+    )
+    return grad.T, loss.reshape(count)
 
 
 def solution(mesh):

time: 112 us -> 106 us (0.946)
  the two profiles are of different devices: /device:TPU:1 before, /device:TPU:8 now
where the time goes in v3:
time: 106 us
  blocking collectives  80.3 us (76%)
  Pallas kernels  9.69 us (9%)
  waiting for transfers between devices  7.56 us (7%)
  starting transfers between devices  6.18 us (6%)
    all_to_all x1, blocking collectives, shards(): lax.all_to_all(copies, 'z', split_axis=0, concat_axis=0, tiled=True)  33.2 us
    all_to_all x1, blocking collectives, shards(): got = lax.all_to_all(out, 'x', split_axis=0, concat_axis=0, tiled=True)  26.2 us
    all_to_all x1, blocking collectives, shards(): got = lax.all_to_all(out, 'yh', split_axis=0, concat_axis=0, tiled=True)  20.9 us
    pallas_call x5, Pallas kernels, call(): pl.pallas_call(body, in_specs=[SMEM if o.dtype == jnp.int32 and o.ndim ==...  9.69 us
    ppermute x1, waiting for transfers between devices, to_sides(): return lax.ppermute(x, LANE, perm)  7.55 us
    ppermute x2, starting transfers between devices, swapped(): return lax.ppermute(x, 'c', [(0, 1), (1, 0)])  3.82 us
    ppermute x1, starting transfers between devices, to_sides(): return lax.ppermute(x, LANE, perm)  2.36 us
  transfers between devices with their start and end apart: 3, of which 1 were waited for; matrix products, arithmetic and copies ran while one was open for 0% of the time, Pallas kernels for 6%

profile of v3, /device:TPU:8, one launch (start us, length us, event | category | flops | bytes accessed | tf_op | source)
XLA Modules:
  0.0 105.6 jit_solution(14779984099611753140)
XLA Ops:
  0.6 0.0 copy-start
  0.6 0.0 copy-start.1
  0.6 1.0 broadcast_in_dim.3
  1.7 33.2 %all_to_all.15 = bf16[8,64,768]{2,1,0:T(8,128)(2,1)S(1)} all-to-all(bf16[8,64,768]{2,1,0:T(8,128)(2,1)S(1)} %broadcast_in_dim.3), channel_id=1, replica_groups=mesh['yh'=4,'x'=4,'z'=8,'yl'=2,'c'=2] {'z'}, dimensions={0} | all-to-all | bytes 1572864 | tf_op jit(solution)/shard_map/all_to_all | solution.py:199
  34.9 1.9 %collective-permute-start.1 = (bf16[512,768]{1,0:T(8,128)(2,1)S(1)}, bf16[512,768]{1,0:T(8,128)(2,1)S(1)}, u32[]{:S(2)}, u32[]{:S(2)}) collective-permute-start(bf16[512,768]{1,0:T(8,128)(2,1)S(1)} %bitcast.8), channel_id=1, source_target_pairs={{0,1},{1,0},{2,3},{3,2},{4,5},{5,4},{6,7},{7,6},{8,9},{9,8},{10,11... | collective-permute-start | bytes 2359304 | tf_op jit(solution)/shard_map/ppermute | solution.py:21
  36.8 2.4 %collective-permute-start = (bf16[512,768]{1,0:T(8,128)(2,1)S(1)}, bf16[512,768]{1,0:T(8,128)(2,1)S(1)}, u32[]{:S(2)}, u32[]{:S(2)}) collective-permute-start(bf16[512,768]{1,0:T(8,128)(2,1)S(1)} %bitcast.9), channel_id=1, source_target_pairs={{0,386},{1,3},{2,0},{3,129},{128,2},{129,131},{130,128},{131,257},... | collective-permute-start | bytes 2359304 | tf_op jit(solution)/shard_map/ppermute | solution.py:29
  39.2 0.1 pad_add_fusion.base_ref
  39.3 0.0 collective-permute-done.1.b_ref
  39.3 0.0 copy-done
  39.3 0.0 copy-done.1
  39.3 3.8 %own.1 = (f32[8,512]{1,0:T(8,128)S(1)}, f32[768,512]{1,0:T(8,128)S(1)}, bf16[768,512]{1,0:T(8,128)(2,1)S(1)}) custom-call(s32[4]{0:T(128)S(1)} %pad_add_fusion.base_ref, bf16[512,768]{1,0:T(8,128)(2,1)S(1)} %bitcast.10, bf16[512,768]{1,0:T(8,128)(2,1)S(1)} %collective-permute-done.1.b_ref, bf16[512,768]{1,0:T(8,128)(2,1)S(1)} %copy-done, s32[1,512]{1,0:T(1,128)S(1)} %bitcast.11), custom_call_target="tpu_custom_call" | custom-call | flops 2415919104 | bytes 4194304 | tf_op jit(solution)/shard_map/own/pallas_call | solution.py:168
  43.1 7.6 %collective-permute-done.a_ref = bf16[512,768]{1,0:T(8,128)(2,1)S(1)} collective-permute-done((bf16[512,768]{1,0:T(8,128)(2,1)S(1)}, bf16[512,768]{1,0:T(8,128)(2,1)S(1)}, u32[]{:S(2)}, u32[]{:S(2)}) %collective-permute-start) | collective-permute-done | bytes 786464 | tf_op jit(solution)/shard_map/ppermute | solution.py:29
  50.7 1.9 %collective-permute-start.2 = (bf16[512,768]{1,0:T(8,128)(2,1)S(1)}, bf16[512,768]{1,0:T(8,128)(2,1)S(1)}, u32[]{:S(2)}, u32[]{:S(2)}) collective-permute-start(bf16[512,768]{1,0:T(8,128)(2,1)S(1)} %collective-permute-done.a_ref), channel_id=1, source_target_pairs={{0,1},{1,0},{2,3},{3,2},{4,5},{5,4},{6,7},{7,6},{8,9},{9,8},{10,11... | collective-permute-start | bytes 2359304 | tf_op jit(solution)/shard_map/ppermute | solution.py:21
  52.6 2.4 %side.1 = (f32[8,512]{1,0:T(8,128)S(1)}, f32[768,512]{1,0:T(8,128)S(1)}, bf16[768,512]{1,0:T(8,128)(2,1)S(1)}) custom-call(s32[4]{0:T(128)S(1)} %pad_add_fusion.base_ref, bf16[512,768]{1,0:T(8,128)(2,1)S(1)} %collective-permute-done.a_ref, bf16[512,768]{1,0:T(8,128)(2,1)S(1)} %copy-done, s32[1,512]{1,0:T(1,128)S(1)} %bitcast.12, ...), custom_call_target="tpu_custom_call" | custom-call | flops 1207959552 | bytes 4194304 | tf_op jit(solution)/shard_map/side/pallas_call | solution.py:168
  55.0 0.0 collective-permute-done.2.b_ref
  55.0 2.4 %last.1 = bf16[4,400,512]{2,1,0:T(8,128)(2,1)S(1)} custom-call(s32[4]{0:T(128)S(1)} %pad_add_fusion.base_ref, bf16[512,768]{1,0:T(8,128)(2,1)S(1)} %collective-permute-done.2.b_ref, bf16[512,768]{1,0:T(8,128)(2,1)S(1)} %copy-done, s32[1,512]{1,0:T(1,128)S(1)} %bitcast.13, f32[8,512]{1,0:T(8,128)S(1)} %get-tuple-element.17.st0_ref, ...), custom_call_target="tpu_custom_call" | custom-call | flops 1207959552 | bytes 4194304 | tf_op jit(solution)/shard_map/last/pallas_call | solution.py:168
  57.5 26.2 %all_to_all.16.got_ref = bf16[4,400,512]{2,1,0:T(8,128)(2,1)S(1)} all-to-all(bf16[4,400,512]{2,1,0:T(8,128)(2,1)S(1)} %last.1), channel_id=1, replica_groups=mesh['yh'=4,'x'=4,'z'=8,'yl'=2,'c'=2] {'x'}, dimensions={0} | all-to-all | bytes 3276800 | tf_op jit(solution)/shard_map/all_to_all | solution.py:230
  83.6 0.3 middle.1
  83.9 20.9 %all_to_all.17.got_ref = bf16[4,112,512]{2,1,0:T(8,128)(2,1)S(1)} all-to-all(bf16[4,112,512]{2,1,0:T(8,128)(2,1)S(1)} %middle.1), channel_id=1, replica_groups=mesh['yh'=4,'x'=4,'z'=8,'yl'=2,'c'=2] {'yh'}, dimensions={0} | all-to-all | bytes 917504 | tf_op jit(solution)/shard_map/all_to_all | solution.py:233
  104.8 0.7 final.1
Async XLA Ops:
  0.6 38.7 %copy-start = (bf16[512,768]{1,0:T(8,128)(2,1)S(1)}, bf16[512,768]{1,0:T(8,128)(2,1)}, u32[]{:S(2)}) copy-start(bf16[512,768]{1,0:T(8,128)(2,1)} %q_ref.5) | copy-start | bytes 2359300
  0.6 38.7 %copy-start.1 = (s32[512]{0:T(512)S(1)}, s32[512]{0:T(512)}, u32[]{:S(2)}) copy-start(s32[512]{0:T(512)} %param.5) | copy-start | bytes 6148
  34.9 4.4 %collective-permute-start.1 = (bf16[512,768]{1,0:T(8,128)(2,1)S(1)}, bf16[512,768]{1,0:T(8,128)(2,1)S(1)}, u32[]{:S(2)}, u32[]{:S(2)}) collective-permute-start(bf16[512,768]{1,0:T(8,128)(2,1)S(1)} %bitcast.8), channel_id=1, source_target_pairs={{0,1},{1,0},{2,3},{3,2},{4,5},{5,4},{6,7},{7,6},{8,9},{9,8},{10,11... | collective-permute-start | bytes 2359304 | tf_op jit(solution)/shard_map/ppermute | solution.py:21
  36.8 13.9 %collective-permute-start = (bf16[512,768]{1,0:T(8,128)(2,1)S(1)}, bf16[512,768]{1,0:T(8,128)(2,1)S(1)}, u32[]{:S(2)}, u32[]{:S(2)}) collective-permute-start(bf16[512,768]{1,0:T(8,128)(2,1)S(1)} %bitcast.9), channel_id=1, source_target_pairs={{0,386},{1,3},{2,0},{3,129},{128,2},{129,131},{130,128},{131,257},... | collective-permute-start | bytes 2359304 | tf_op jit(solution)/shard_map/ppermute | solution.py:29
  50.7 4.3 %collective-permute-start.2 = (bf16[512,768]{1,0:T(8,128)(2,1)S(1)}, bf16[512,768]{1,0:T(8,128)(2,1)S(1)}, u32[]{:S(2)}, u32[]{:S(2)}) collective-permute-start(bf16[512,768]{1,0:T(8,128)(2,1)S(1)} %collective-permute-done.a_ref), channel_id=1, source_target_pairs={{0,1},{1,0},{2,3},{3,2},{4,5},{5,4},{6,7},{7,6},{8,9},{9,8},{10,11... | collective-permute-start | bytes 2359304 | tf_op jit(solution)/shard_map/ppermute | solution.py:21

commit v4 on v2

v4 whole, which is shorter than its diff:
```python
import functools
import math

import jax
import jax.numpy as jnp
from jax import lax
from jax.experimental import pallas as pl
from jax.experimental.pallas import tpu as pltpu
from jax.sharding import Mesh
from jax.sharding import PartitionSpec as P


INNER = ("z", "yl", "c")
OUTER = ("yh", "x")
LANE = ("yh", "yl", "c")
F32, BF16 = jnp.float32, jnp.bfloat16
VMEM = pl.BlockSpec(memory_space=pltpu.VMEM)
SMEM = pl.BlockSpec(memory_space=pltpu.SMEM)


def swapped(x):
    return lax.ppermute(x, "c", [(0, 1), (1, 0)])


def to_sides(x, ny):
    perm = []
    for y in range(ny):
        perm.append((2 * y, 2 * ((y - 1) % ny)))
        perm.append((2 * y + 1, 2 * ((y + 1) % ny) + 1))
    return lax.ppermute(x, LANE, perm)


def dot(a, b, dims):
    return lax.dot_general(a, b, (dims, ((), ())), preferred_element_type=F32)


def hits_of(pos_ref, base, count, rows):
    j = lax.broadcasted_iota(jnp.int32, (count, 1), 0)
    return (j // rows) * (4 * rows) + j % rows == pos_ref[...] - base


def statistics(p_refs, bases, q_ref, pos_ref, s_ref, scale, rows):
    q = q_ref[...]
    top = ps = None
    for i, p_ref in enumerate(p_refs):
        n = p_ref.shape[0]
        s = dot(p_ref[...], q, ((1,), (1,))) * scale
        s_ref[i * n : (i + 1) * n, :] = s
        hit = hits_of(pos_ref, bases[i], n, rows)
        t = jnp.max(s, axis=0, keepdims=True)
        u = jnp.sum(jnp.where(hit, s, 0.0), axis=0, keepdims=True)
        top = t if top is None else jnp.maximum(top, t)
        ps = u if ps is None else ps + u
    return top, ps


def products(p_refs, bases, w_ref, pos_ref, rows):
    mix = chosen = 0.0
    for i, p_ref in enumerate(p_refs):
        n = p_ref.shape[0]
        p = p_ref[...]
        hit = hits_of(pos_ref, bases[i], n, rows).astype(F32).astype(BF16)
        mix += dot(p, w_ref[i * n : (i + 1) * n, :], ((0,), (0,)))
        chosen += dot(p, hit, ((0,), (0,)))
    return mix, chosen


def stat_kernel(scale, rows, base_ref, a_ref, b_ref, q_ref, pos_ref, qf_ref, posf_ref, st_ref, w_ref, out_ref, s_ref):
    bases = (base_ref[0], base_ref[1])
    pieces = []
    for qq, pp in ((qf_ref, posf_ref), (q_ref, pos_ref)):
        top, ps = statistics((a_ref, b_ref), bases, qq, pp, s_ref, scale, rows)
        e = jnp.exp(s_ref[...] - top)
        total = jnp.sum(e, axis=0, keepdims=True)
        pieces.append(jnp.concatenate([top, total, ps, ps], axis=0))
    st_ref[0:1, :] = top
    w_ref[...] = e.astype(BF16)
    theirs, own = pieces
    lower = base_ref[4] == 0
    half = out_ref.shape[0] // 2
    shape = (half, *own.shape)
    out_ref[:half] = jnp.broadcast_to(jnp.where(lower, own, theirs)[None], shape)
    out_ref[half:] = jnp.broadcast_to(jnp.where(lower, theirs, own)[None], shape)


def own_kernel(rows, base_ref, a_ref, b_ref, w_ref, pos_ref, mix_ref, ch_ref):
    mix, chosen = products((a_ref, b_ref), (base_ref[0], base_ref[1]), w_ref, pos_ref, rows)
    mix_ref[...] = mix
    ch_ref[...] = chosen.astype(BF16)


def near_kernel(scale, rows, base_ref, a_ref, b_ref, q_ref, pos_ref, st0_ref, mix0_ref, ch0_ref, st_ref, m_ref, c_ref, s_ref, w_ref):
    bases = (base_ref[2], base_ref[3])
    top, _ = statistics((a_ref, b_ref), bases, q_ref, pos_ref, s_ref, scale, rows)
    top0 = st0_ref[0:1, :]
    top = jnp.maximum(top, top0)
    w_ref[...] = jnp.exp(s_ref[...] - top).astype(BF16)
    mix, chosen = products((a_ref, b_ref), bases, w_ref, pos_ref, rows)
    st_ref[0:1, :] = top
    m_ref[...] = mix + mix0_ref[...] * jnp.exp(top0 - top)
    c_ref[...] = (chosen + ch0_ref[...].astype(F32)).astype(BF16)


def scale_kernel(every_ref, st_ref, m_ref, c_ref, out_ref, loss_ref):
    tops = every_ref[:, 0, :]
    top = jnp.max(tops, axis=0, keepdims=True)
    total = jnp.sum(every_ref[:, 1, :] * jnp.exp(tops - top), axis=0, keepdims=True)
    ps = jnp.sum(every_ref[:, 2, :], axis=0, keepdims=True)
    g = jnp.exp(st_ref[0:1, :] - top) / total
    out_ref[...] = (m_ref[...] * g - c_ref[...].astype(F32)).astype(BF16)
    loss_ref[...] = top + jnp.log(total) - ps


def final_kernel(scale, got_ref, grad_ref):
    total = got_ref[0].astype(F32)
    for i in range(1, got_ref.shape[0]):
        total += got_ref[i].astype(F32)
    grad_ref[...] = (scale * total).astype(BF16)


def call(body, out, operands, scratch=(), flops=0, vmem=20):
    out_shape = [jax.ShapeDtypeStruct(s, d) for s, d in out]
    return pl.pallas_call(
        body,
        in_specs=[SMEM if o.dtype == jnp.int32 and o.ndim == 1 else VMEM for o in operands],
        out_specs=[VMEM] * len(out),
        out_shape=out_shape,
        scratch_shapes=[pltpu.VMEM(s, d) for s, d in scratch],
        cost_estimate=pl.CostEstimate(flops=flops, bytes_accessed=4 << 20, transcendentals=0),
        compiler_params=pltpu.CompilerParams(vmem_limit_bytes=vmem << 20),
    )(*operands)


def shards(queries, passages, positive):
    count, width = queries.shape
    rows = passages.shape[0]
    scale = 3.0 / math.sqrt(width)
    nz, nx = lax.axis_size("z"), lax.axis_size("x")
    ny = lax.axis_size("yh") * 2
    x, c = lax.axis_index("x"), lax.axis_index("c")
    y = lax.axis_index("yh") * 2 + lax.axis_index("yl")
    n = nz * rows
    flops = 2 * n * width * count

    def base_of(yy, cc):
        yy = (yy + ny) & (ny - 1)
        return ((((yy >> 1) * nx + x) * nz * 2 + (yy & 1)) * 2 + cc) * rows

    base = jnp.stack(
        [base_of(y, c), base_of(y, 1 - c), base_of(y + 1 - 2 * c, c), base_of(y - 1 + 2 * c, 1 - c), y & 1]
    )
    pos = positive.reshape(1, count)

    theirs = to_sides(queries, ny)
    pos_theirs = to_sides(pos, ny)
    copies = jnp.broadcast_to(passages, (nz, rows, width))
    column = lax.all_to_all(copies, "z", split_axis=0, concat_axis=0, tiled=True)
    column, theirs, pos_theirs = lax.optimization_barrier((column, theirs, pos_theirs))
    column = column.reshape(n, width)
    side = to_sides(column, ny)
    column2 = swapped(column)
    members = ny * nx
    st1, weights, stats = call(
        functools.partial(stat_kernel, scale, rows),
        [((8, count), F32), ((2 * n, count), BF16), ((members, 4, count), F32)],
        (base, column, column2, queries, pos, theirs, pos_theirs),
        [((2 * n, count), F32)],
        4 * flops,
    )
    every = lax.all_to_all(stats, ("yl", *OUTER), split_axis=0, concat_axis=0, tiled=True)
    mix1, ch1 = call(
        functools.partial(own_kernel, rows),
        [((width, count), F32), ((width, count), BF16)],
        (base, column, column2, weights, pos),
        (),
        4 * flops,
    )
    side2 = swapped(side)
    st, m, ch = call(
        functools.partial(near_kernel, scale, rows),
        [((8, count), F32), ((width, count), F32), ((width, count), BF16)],
        (base, side, side2, queries, pos, st1, mix1, ch1),
        [((2 * n, count), F32), ((2 * n, count), BF16)],
        6 * flops,
    )
    out, loss = call(scale_kernel, [((width, count), BF16), ((1, count), F32)], (every, st, m, ch))
    n_outer = members // 2
    out = out.reshape(n_outer, width // n_outer, count)
    got = lax.all_to_all(out, OUTER, split_axis=0, concat_axis=0, tiled=True)
    (grad,) = call(
        functools.partial(final_kernel, scale), [((width // n_outer, count), BF16)], (got,)
    )
    return grad.T, loss.reshape(count)


def solution(mesh):
    devices = mesh.devices
    torus = Mesh(devices.reshape(4, 4, 8, 2, 2), ("yh", "x", "z", "yl", "c"))
    in_specs = (P(INNER, None), P((*OUTER, *INNER), None), P(INNER))
    out_specs = (P(INNER, OUTER), P(INNER))
    return jax.shard_map(
        shards, mesh=torus, in_specs=in_specs, out_specs=out_specs, check_vma=False
    )
```

time: 112 us -> 110 us (0.982)
  the two profiles are of different devices: /device:TPU:1 before, /device:TPU:16 now
where the time goes in v4:
time: 110 us
  starting transfers between devices  32.2 us (29%)
  waiting for transfers between devices  30.8 us (28%)
  blocking collectives  28.4 us (26%)
  Pallas kernels  13.3 us (12%)
  local copies, waits for them, and re-layouts  4.21 us (4%)
    all_to_all x1, blocking collectives, shards(): got = lax.all_to_all(out, OUTER, split_axis=0, concat_axis=0, tiled=True)  28.4 us
    ppermute x3, waiting for transfers between devices, to_sides(): return lax.ppermute(x, LANE, perm)  17.9 us
    pallas_call x5, Pallas kernels, call(): pl.pallas_call(body, in_specs=[SMEM if o.dtype == jnp.int32 and o.ndim ==...  13.3 us
    all_to_all x1, starting transfers between devices, shards(): lax.all_to_all(copies, 'z', split_axis=0, concat_axis=0, tiled=True)  10.3 us
    all_to_all x1, starting transfers between devices, shards(): lax.all_to_all(stats, ('yl', *OUTER), split_axis=0, concat_axis=0, tiled=...  10.1 us
    all_to_all x1, waiting for transfers between devices, shards(): lax.all_to_all(copies, 'z', split_axis=0, concat_axis=0, tiled=True)  9.2 us
    ppermute x3, starting transfers between devices, to_sides(): return lax.ppermute(x, LANE, perm)  7.06 us
    ppermute x2, starting transfers between devices, swapped(): return lax.ppermute(x, 'c', [(0, 1), (1, 0)])  4.68 us
  transfers between devices with their start and end apart: 7, of which 4 were waited for; matrix products, arithmetic and copies ran while one was open for 0% of the time, Pallas kernels for 11%

profile of v4, /device:TPU:16, one launch (start us, length us, event | category | flops | bytes accessed | tf_op | source)
XLA Modules:
  0.0 109.7 jit_solution(14418726775917859711)
XLA Ops:
  0.6 0.0 copy-start
  0.6 0.0 copy-start.3
  0.6 1.9 %broadcast_in_dim.3 = bf16[8,64,768]{2,1,0:T(8,128)(2,1)} broadcast(bf16[64,768]{1,0:T(8,128)(2,1)} %param.4), dimensions={1,2} | broadcast | bytes 884736 | tf_op jit(solution)/shard_map/broadcast_in_dim | solution.py:156
  2.6 10.3 %all-to-all-start = ((bf16[8,64,768]{2,1,0:T(8,128)(2,1)}), bf16[8,64,768]{2,1,0:T(8,128)(2,1)S(1)}, u32[]{:S(2)}, u32[]{:S(2)}) async-start(bf16[8,64,768]{2,1,0:T(8,128)(2,1)} %broadcast_in_dim.3), calls=%async_computation | async-start | bytes 1572864 | tf_op jit(solution)/shard_map/all_to_all | solution.py:157
  12.9 0.0 copy-done
  12.9 2.4 %collective-permute-start = (bf16[512,768]{1,0:T(8,128)(2,1)S(1)}, bf16[512,768]{1,0:T(8,128)(2,1)S(1)}, u32[]{:S(2)}, u32[]{:S(2)}) collective-permute-start(bf16[512,768]{1,0:T(8,128)(2,1)S(1)} %copy-done), channel_id=1, source_target_pairs={{0,386},{1,3},{2,0},{3,129},{128,2},{129,131},{130,128},{131,257},... | collective-permute-start | bytes 2359304 | tf_op jit(solution)/shard_map/ppermute | solution.py:30
  15.2 0.0 copy-done.3
  15.3 2.4 %collective-permute-start.1 = (s32[1,512]{1,0:T(1,128)S(1)}, s32[1,512]{1,0:T(1,128)S(1)}, u32[]{:S(2)}, u32[]{:S(2)}) collective-permute-start(s32[1,512]{1,0:T(1,128)S(1)} %bitcast.15), channel_id=1, source_target_pairs={{0,386},{1,3},{2,0},{3,129},{128,2},{129,131},{130,128},{131,257},... | collective-permute-start | bytes 6152 | tf_op jit(solution)/shard_map/ppermute | solution.py:30
  17.6 9.2 %collective-permute-done.1.posf_ref = s32[1,512]{1,0:T(1,128)S(1)} collective-permute-done((s32[1,512]{1,0:T(1,128)S(1)}, s32[1,512]{1,0:T(1,128)S(1)}, u32[]{:S(2)}, u32[]{:S(2)}) %collective-permute-start.1) | collective-permute-done | bytes 2080 | tf_op jit(solution)/shard_map/ppermute | solution.py:30
  26.8 0.0 collective-permute-done.qf_ref
  26.8 9.2 %all-to-all-done = bf16[8,64,768]{2,1,0:T(8,128)(2,1)S(1)} async-done(((bf16[8,64,768]{2,1,0:T(8,128)(2,1)}), bf16[8,64,768]{2,1,0:T(8,128)(2,1)S(1)}, u32[]{:S(2)}, u32[]{:S(2)}) %all-to-all-start) | async-done | bytes 786464 | tf_op jit(solution)/shard_map/all_to_all | solution.py:157
  36.0 2.3 %collective-permute-start.3 = (bf16[512,768]{1,0:T(8,128)(2,1)S(1)}, bf16[512,768]{1,0:T(8,128)(2,1)S(1)}, u32[]{:S(2)}, u32[]{:S(2)}) collective-permute-start(bf16[512,768]{1,0:T(8,128)(2,1)S(1)} %bitcast.10), channel_id=1, source_target_pairs={{0,386},{1,3},{2,0},{3,129},{128,2},{129,131},{130,128},{131,257},... | collective-permute-start | bytes 2359304 | tf_op jit(solution)/shard_map/ppermute | solution.py:30
  38.3 2.8 %collective-permute-start.2 = (bf16[512,768]{1,0:T(8,128)(2,1)S(1)}, bf16[512,768]{1,0:T(8,128)(2,1)}, u32[]{:S(2)}, u32[]{:S(2)}) collective-permute-start(bf16[512,768]{1,0:T(8,128)(2,1)S(1)} %bitcast.11), channel_id=1, source_target_pairs={{0,1},{1,0},{2,3},{3,2},{4,5},{5,4},{6,7},{7,6},{8,9},{9,8},{10,11... | collective-permute-start | bytes 2359304 | tf_op jit(solution)/shard_map/ppermute | solution.py:22
  41.1 8.7 %collective-permute-done.3.a_ref = bf16[512,768]{1,0:T(8,128)(2,1)S(1)} collective-permute-done((bf16[512,768]{1,0:T(8,128)(2,1)S(1)}, bf16[512,768]{1,0:T(8,128)(2,1)S(1)}, u32[]{:S(2)}, u32[]{:S(2)}) %collective-permute-start.3) | collective-permute-done | bytes 786464 | tf_op jit(solution)/shard_map/ppermute | solution.py:30
  49.9 0.0 copy-start.1
  49.9 1.9 %collective-permute-start.4 = (bf16[512,768]{1,0:T(8,128)(2,1)S(1)}, bf16[512,768]{1,0:T(8,128)(2,1)}, u32[]{:S(2)}, u32[]{:S(2)}) collective-permute-start(bf16[512,768]{1,0:T(8,128)(2,1)S(1)} %collective-permute-done.3.a_ref), channel_id=1, source_target_pairs={{0,1},{1,0},{2,3},{3,2},{4,5},{5,4},{6,7},{7,6},{8,9},{9,8},{10,11... | collective-permute-start | bytes 2359304 | tf_op jit(solution)/shard_map/ppermute | solution.py:22
  51.8 0.1 stack.23.base_ref
  51.9 0.0 collective-permute-done.2.b_ref
  51.9 4.7 %shard_map.50 = (f32[8,512]{1,0:T(8,128)S(1)}, bf16[1024,512]{1,0:T(8,128)(2,1)S(1)}, f32[32,4,512]{2,1,0:T(4,128)}) custom-call(s32[5]{0:T(128)S(1)} %stack.23.base_ref, bf16[512,768]{1,0:T(8,128)(2,1)S(1)} %bitcast.12, bf16[512,768]{1,0:T(8,128)(2,1)} %collective-permute-done.2.b_ref, bf16[512,768]{1,0:T(8,128)(2,1)S(1)} %copy-done, ...), custom_call_target="tpu_custom_call" | custom-call | flops 1610612736 | bytes 4194304 | tf_op jit(solution)/shard_map/pallas_call | solution.py:123
  56.7 0.0 copy-done.1
  56.7 1.0 copy-done.4
  57.6 10.1 %all-to-all-start.1 = ((f32[32,4,512]{2,1,0:T(4,128)}), f32[32,4,512]{2,1,0:T(4,128)S(1)}, u32[]{:S(2)}, u32[]{:S(2)}) async-start(f32[32,4,512]{2,1,0:T(4,128)} %get-tuple-element.18), calls=%async_computation.1 | async-start | bytes 524288 | tf_op jit(solution)/shard_map/all_to_all | solution.py:170
  67.8 0.0 copy-start.5
  67.8 1.2 %copy-done.5 = bf16[1024,512]{1,0:T(8,128)(2,1)S(1)} copy-done((bf16[1024,512]{1,0:T(8,128)(2,1)S(1)}, bf16[1024,512]{1,0:T(8,128)(2,1)}, u32[]{:S(2)}) %copy-start.5) | copy-done | bytes 1048600
  69.0 3.0 %shard_map.51 = (f32[768,512]{1,0:T(8,128)S(1)}, bf16[768,512]{1,0:T(8,128)(2,1)S(1)}) custom-call(s32[5]{0:T(128)S(1)} %stack.23.base_ref, bf16[512,768]{1,0:T(8,128)(2,1)S(1)} %bitcast.13, bf16[512,768]{1,0:T(8,128)(2,1)} %collective-permute-done.2.b_ref, bf16[1024,512]{1,0:T(8,128)(2,1)S(1)} %copy-done.5, s32[1,512]{1,0:T(1,128)S(1)} %bitcast.17), custom_call_target="tpu_custom_call" | custom-call | flops 1610612736 | bytes 4194304 | tf_op jit(solution)/shard_map/pallas_call | solution.py:123
  72.0 0.0 collective-permute-done.4.b_ref
  72.0 0.0 copy-done.2
  72.0 4.2 %shard_map.52 = (f32[8,512]{1,0:T(8,128)S(1)}, f32[768,512]{1,0:T(8,128)S(1)}, bf16[768,512]{1,0:T(8,128)(2,1)S(1)}) custom-call(s32[5]{0:T(128)S(1)} %stack.23.base_ref, bf16[512,768]{1,0:T(8,128)(2,1)S(1)} %copy-done.2, bf16[512,768]{1,0:T(8,128)(2,1)} %collective-permute-done.4.b_ref, bf16[512,768]{1,0:T(8,128)(2,1)S(1)} %copy-done, ...), custom_call_target="tpu_custom_call" | custom-call | flops 2415919104 | bytes 4194304 | tf_op jit(solution)/shard_map/pallas_call | solution.py:123
  76.2 3.7 %all-to-all-done.1.every_ref = f32[32,4,512]{2,1,0:T(4,128)S(1)} async-done(((f32[32,4,512]{2,1,0:T(4,128)}), f32[32,4,512]{2,1,0:T(4,128)S(1)}, u32[]{:S(2)}, u32[]{:S(2)}) %all-to-all-start.1) | async-done | bytes 262176 | tf_op jit(solution)/shard_map/all_to_all | solution.py:170
  79.9 0.7 shard_map.53
  80.6 28.4 %all_to_all.15.got_ref = bf16[16,48,512]{2,1,0:T(8,128)(2,1)S(1)} all-to-all(bf16[16,48,512]{2,1,0:T(8,128)(2,1)S(1)} %bitcast.14), channel_id=1, replica_groups=mesh['yh'=4,'x'=4,'z'=8,'yl'=2,'c'=2] {'yh','x'}, dimensions={0} | all-to-all | bytes 1572864 | tf_op jit(solution)/shard_map/all_to_all | solution.py:189
  109.0 0.7 shard_map.54
  (2 shorter events, 0.0 us)
Async XLA Ops:
  0.6 12.2 %copy-start = (bf16[512,768]{1,0:T(8,128)(2,1)S(1)}, bf16[512,768]{1,0:T(8,128)(2,1)}, u32[]{:S(2)}) copy-start(bf16[512,768]{1,0:T(8,128)(2,1)} %q_ref.3) | copy-start | bytes 2359300
  0.6 14.6 %copy-start.3 = (s32[512]{0:T(512)S(1)}, s32[512]{0:T(512)}, u32[]{:S(2)}) copy-start(s32[512]{0:T(512)} %param.5) | copy-start | bytes 6148
  2.6 33.4 %all-to-all-start = ((bf16[8,64,768]{2,1,0:T(8,128)(2,1)}), bf16[8,64,768]{2,1,0:T(8,128)(2,1)S(1)}, u32[]{:S(2)}, u32[]{:S(2)}) async-start(bf16[8,64,768]{2,1,0:T(8,128)(2,1)} %broadcast_in_dim.3), calls=%async_computation | async-start | bytes 1572864 | tf_op jit(solution)/shard_map/all_to_all | solution.py:157
  12.9 13.9 %collective-permute-start = (bf16[512,768]{1,0:T(8,128)(2,1)S(1)}, bf16[512,768]{1,0:T(8,128)(2,1)S(1)}, u32[]{:S(2)}, u32[]{:S(2)}) collective-permute-start(bf16[512,768]{1,0:T(8,128)(2,1)S(1)} %copy-done), channel_id=1, source_target_pairs={{0,386},{1,3},{2,0},{3,129},{128,2},{129,131},{130,128},{131,257},... | collective-permute-start | bytes 2359304 | tf_op jit(solution)/shard_map/ppermute | solution.py:30
  15.3 11.5 %collective-permute-start.1 = (s32[1,512]{1,0:T(1,128)S(1)}, s32[1,512]{1,0:T(1,128)S(1)}, u32[]{:S(2)}, u32[]{:S(2)}) collective-permute-start(s32[1,512]{1,0:T(1,128)S(1)} %bitcast.15), channel_id=1, source_target_pairs={{0,386},{1,3},{2,0},{3,129},{128,2},{129,131},{130,128},{131,257},... | collective-permute-start | bytes 6152 | tf_op jit(solution)/shard_map/ppermute | solution.py:30
  36.0 13.9 %collective-permute-start.3 = (bf16[512,768]{1,0:T(8,128)(2,1)S(1)}, bf16[512,768]{1,0:T(8,128)(2,1)S(1)}, u32[]{:S(2)}, u32[]{:S(2)}) collective-permute-start(bf16[512,768]{1,0:T(8,128)(2,1)S(1)} %bitcast.10), channel_id=1, source_target_pairs={{0,386},{1,3},{2,0},{3,129},{128,2},{129,131},{130,128},{131,257},... | collective-permute-start | bytes 2359304 | tf_op jit(solution)/shard_map/ppermute | solution.py:30
  38.3 13.6 %collective-permute-start.2 = (bf16[512,768]{1,0:T(8,128)(2,1)S(1)}, bf16[512,768]{1,0:T(8,128)(2,1)}, u32[]{:S(2)}, u32[]{:S(2)}) collective-permute-start(bf16[512,768]{1,0:T(8,128)(2,1)S(1)} %bitcast.11), channel_id=1, source_target_pairs={{0,1},{1,0},{2,3},{3,2},{4,5},{5,4},{6,7},{7,6},{8,9},{9,8},{10,11... | collective-permute-start | bytes 2359304 | tf_op jit(solution)/shard_map/ppermute | solution.py:22
  49.9 6.8 %copy-start.1 = (bf16[512,768]{1,0:T(8,128)(2,1)}, bf16[512,768]{1,0:T(8,128)(2,1)S(1)}, u32[]{:S(2)}) copy-start(bf16[512,768]{1,0:T(8,128)(2,1)S(1)} %collective-permute-done.3.a_ref) | copy-start | bytes 2359300
  49.9 22.2 %collective-permute-start.4 = (bf16[512,768]{1,0:T(8,128)(2,1)S(1)}, bf16[512,768]{1,0:T(8,128)(2,1)}, u32[]{:S(2)}, u32[]{:S(2)}) collective-permute-start(bf16[512,768]{1,0:T(8,128)(2,1)S(1)} %collective-permute-done.3.a_ref), channel_id=1, source_target_pairs={{0,1},{1,0},{2,3},{3,2},{4,5},{5,4},{6,7},{7,6},{8,9},{9,8},{10,11... | collective-permute-start | bytes 2359304 | tf_op jit(solution)/shard_map/ppermute | solution.py:22
  56.7 1.0 copy-start.4
  57.6 22.3 %all-to-all-start.1 = ((f32[32,4,512]{2,1,0:T(4,128)}), f32[32,4,512]{2,1,0:T(4,128)S(1)}, u32[]{:S(2)}, u32[]{:S(2)}) async-start(f32[32,4,512]{2,1,0:T(4,128)} %get-tuple-element.18), calls=%async_computation.1 | async-start | bytes 524288 | tf_op jit(solution)/shard_map/all_to_all | solution.py:170
  67.8 1.2 %copy-start.5 = (bf16[1024,512]{1,0:T(8,128)(2,1)S(1)}, bf16[1024,512]{1,0:T(8,128)(2,1)}, u32[]{:S(2)}) copy-start(bf16[1024,512]{1,0:T(8,128)(2,1)} %copy-done.4) | copy-start | bytes 3145732
  69.0 3.0 %copy-start.2 = (bf16[512,768]{1,0:T(8,128)(2,1)S(1)}, bf16[512,768]{1,0:T(8,128)(2,1)}, u32[]{:S(2)}) copy-start(bf16[512,768]{1,0:T(8,128)(2,1)} %copy-done.1) | copy-start | bytes 2359300

commit v5 on v4

--- a/solution.py
+++ b/solution.py
@@ -16,6 +16,7 @@
 F32, BF16 = jnp.float32, jnp.bfloat16
 VMEM = pl.BlockSpec(memory_space=pltpu.VMEM)
 SMEM = pl.BlockSpec(memory_space=pltpu.SMEM)
+HBM = pl.BlockSpec(memory_space=pltpu.HBM)
 
 
 def swapped(x):
@@ -65,37 +66,57 @@
     return mix, chosen
 
 
-def stat_kernel(scale, rows, base_ref, a_ref, b_ref, q_ref, pos_ref, qf_ref, posf_ref, st_ref, w_ref, out_ref, s_ref):
+def stat_kernel(scale, rows, base_ref, a_ref, b_ref, q_ref, pos_ref, qf_ref, posf_ref, st_ref, w_hbm, out_ref, s_ref, w_ref, sem):
     bases = (base_ref[0], base_ref[1])
     pieces = []
-    for qq, pp in ((qf_ref, posf_ref), (q_ref, pos_ref)):
+    for qq, pp in ((q_ref, pos_ref), (qf_ref, posf_ref)):
         top, ps = statistics((a_ref, b_ref), bases, qq, pp, s_ref, scale, rows)
         e = jnp.exp(s_ref[...] - top)
         total = jnp.sum(e, axis=0, keepdims=True)
+        if not pieces:
+            w_ref[...] = e.astype(BF16)
+            copy = pltpu.make_async_copy(w_ref, w_hbm, sem)
+            copy.start()
+            st_ref[0:1, :] = top
         pieces.append(jnp.concatenate([top, total, ps, ps], axis=0))
-    st_ref[0:1, :] = top
-    w_ref[...] = e.astype(BF16)
-    theirs, own = pieces
+    own, theirs = pieces
     lower = base_ref[4] == 0
     half = out_ref.shape[0] // 2
     shape = (half, *own.shape)
     out_ref[:half] = jnp.broadcast_to(jnp.where(lower, own, theirs)[None], shape)
     out_ref[half:] = jnp.broadcast_to(jnp.where(lower, theirs, own)[None], shape)
-
-
-def own_kernel(rows, base_ref, a_ref, b_ref, w_ref, pos_ref, mix_ref, ch_ref):
-    mix, chosen = products((a_ref, b_ref), (base_ref[0], base_ref[1]), w_ref, pos_ref, rows)
-    mix_ref[...] = mix
+    copy.wait()
+
+
+def own_kernel(rows, base_ref, a_hbm, b_hbm, w_hbm, pos_ref, mix_ref, ch_ref, a_ref, b_ref, w_ref, sems):
+    pairs = ((a_hbm, a_ref), (b_hbm, b_ref), (w_hbm, w_ref))
+    copies = [pltpu.make_async_copy(src, dst, sems.at[i]) for i, (src, dst) in enumerate(pairs)]
+    for copy in copies:
+        copy.start()
+    n = a_ref.shape[0]
+    chosen = 0.0
+    for i, p_ref in enumerate((a_ref, b_ref)):
+        hit = hits_of(pos_ref, base_ref[i], n, rows).astype(F32).astype(BF16)
+        copies[i].wait()
+        chosen += dot(p_ref[...], hit, ((0,), (0,)))
     ch_ref[...] = chosen.astype(BF16)
-
-
-def near_kernel(scale, rows, base_ref, a_ref, b_ref, q_ref, pos_ref, st0_ref, mix0_ref, ch0_ref, st_ref, m_ref, c_ref, s_ref, w_ref):
-    bases = (base_ref[2], base_ref[3])
-    top, _ = statistics((a_ref, b_ref), bases, q_ref, pos_ref, s_ref, scale, rows)
+    copies[2].wait()
+    mix_ref[...] = dot(a_ref[...], w_ref[:n, :], ((0,), (0,))) + dot(b_ref[...], w_ref[n:, :], ((0,), (0,)))
+
+
+def near_kernel(scale, rows, base_ref, a_hbm, b_ref, q_ref, pos_ref, st0_ref, mix0_ref, ch0_ref, st_ref, m_ref, c_ref, s_ref, w_ref, a_ref, sem):
+    copy = pltpu.make_async_copy(a_hbm, a_ref, sem)
+    copy.start()
+    bases = (base_ref[3], base_ref[2])
+    q = q_ref[...]
+    n = b_ref.shape[0]
+    s_ref[:n, :] = dot(b_ref[...], q, ((1,), (1,))) * scale
+    copy.wait()
+    s_ref[n:, :] = dot(a_ref[...], q, ((1,), (1,))) * scale
     top0 = st0_ref[0:1, :]
-    top = jnp.maximum(top, top0)
+    top = jnp.maximum(jnp.max(s_ref[...], axis=0, keepdims=True), top0)
     w_ref[...] = jnp.exp(s_ref[...] - top).astype(BF16)
-    mix, chosen = products((a_ref, b_ref), bases, w_ref, pos_ref, rows)
+    mix, chosen = products((b_ref, a_ref), bases, w_ref, pos_ref, rows)
     st_ref[0:1, :] = top
     m_ref[...] = mix + mix0_ref[...] * jnp.exp(top0 - top)
     c_ref[...] = (chosen + ch0_ref[...].astype(F32)).astype(BF16)
@@ -118,17 +139,23 @@
     grad_ref[...] = (scale * total).astype(BF16)
 
 
-def call(body, out, operands, scratch=(), flops=0, vmem=20):
-    out_shape = [jax.ShapeDtypeStruct(s, d) for s, d in out]
-    return pl.pallas_call(
+def call(body, out, operands, scratch=(), flops=0, vmem=12, hbm_in=(), hbm_out=()):
+    def spec(i, o):
+        if i in hbm_in:
+            return HBM
+        return SMEM if o.dtype == jnp.int32 and o.ndim == 1 else VMEM
+
+    kernel = pl.pallas_call(
         body,
-        in_specs=[SMEM if o.dtype == jnp.int32 and o.ndim == 1 else VMEM for o in operands],
-        out_specs=[VMEM] * len(out),
-        out_shape=out_shape,
-        scratch_shapes=[pltpu.VMEM(s, d) for s, d in scratch],
+        in_specs=[spec(i, o) for i, o in enumerate(operands)],
+        out_specs=[HBM if i in hbm_out else VMEM for i in range(len(out))],
+        out_shape=[pltpu.HBM(s, d) if i in hbm_out else jax.ShapeDtypeStruct(s, d) for i, (s, d) in enumerate(out)],
+        scratch_shapes=[s if not isinstance(s, tuple) else pltpu.VMEM(*s) for s in scratch],
         cost_estimate=pl.CostEstimate(flops=flops, bytes_accessed=4 << 20, transcendentals=0),
         compiler_params=pltpu.CompilerParams(vmem_limit_bytes=vmem << 20),
-    )(*operands)
+    )
+    operands = [pltpu.with_memory_space_constraint(o, pltpu.HBM) if i in hbm_in else o for i, o in enumerate(operands)]
+    return kernel(*operands)
 
 
 def shards(queries, passages, positive):
@@ -164,32 +191,33 @@
         functools.partial(stat_kernel, scale, rows),
         [((8, count), F32), ((2 * n, count), BF16), ((members, 4, count), F32)],
         (base, column, column2, queries, pos, theirs, pos_theirs),
-        [((2 * n, count), F32)],
+        [((2 * n, count), F32), ((2 * n, count), BF16), pltpu.SemaphoreType.DMA],
         4 * flops,
+        hbm_out=(1,),
     )
     every = lax.all_to_all(stats, ("yl", *OUTER), split_axis=0, concat_axis=0, tiled=True)
     mix1, ch1 = call(
         functools.partial(own_kernel, rows),
         [((width, count), F32), ((width, count), BF16)],
         (base, column, column2, weights, pos),
-        (),
+        [((n, width), BF16), ((n, width), BF16), ((2 * n, count), BF16), pltpu.SemaphoreType.DMA((3,))],
         4 * flops,
+        hbm_in=(1, 2, 3),
     )
     side2 = swapped(side)
     st, m, ch = call(
         functools.partial(near_kernel, scale, rows),
         [((8, count), F32), ((width, count), F32), ((width, count), BF16)],
         (base, side, side2, queries, pos, st1, mix1, ch1),
-        [((2 * n, count), F32), ((2 * n, count), BF16)],
+        [((2 * n, count), F32), ((2 * n, count), BF16), ((n, width), BF16), pltpu.SemaphoreType.DMA],
         6 * flops,
+        hbm_in=(1,),
     )
     out, loss = call(scale_kernel, [((width, count), BF16), ((1, count), F32)], (every, st, m, ch))
     n_outer = members // 2
     out = out.reshape(n_outer, width // n_outer, count)
     got = lax.all_to_all(out, OUTER, split_axis=0, concat_axis=0, tiled=True)
-    (grad,) = call(
-        functools.partial(final_kernel, scale), [((width // n_outer, count), BF16)], (got,)
-    )
+    (grad,) = call(functools.partial(final_kernel, scale), [((width // n_outer, count), BF16)], (got,))
     return grad.T, loss.reshape(count)
 
 
@@ -198,6 +226,4 @@
     torus = Mesh(devices.reshape(4, 4, 8, 2, 2), ("yh", "x", "z", "yl", "c"))
     in_specs = (P(INNER, None), P((*OUTER, *INNER), None), P(INNER))
     out_specs = (P(INNER, OUTER), P(INNER))
-    return jax.shard_map(
-        shards, mesh=torus, in_specs=in_specs, out_specs=out_specs, check_vma=False
-    )
+    return jax.shard_map(shards, mesh=torus, in_specs=in_specs, out_specs=out_specs, check_vma=False)

time: 110 us -> 111 us (level)
  blocking collectives: 28.4 us -> 30.3 us
  waiting for transfers between devices: 30.8 us -> 29.1 us
    all_to_all x1, blocking collectives: 28.4 us -> 30.3 us  [shards(): got = lax.all_to_all(out, OUTER, split_axis=0, concat_axis=0, tiled=True)]
    all_to_all x1, waiting for transfers between devices: 3.7 us -> 1.86 us  [shards(): lax.all_to_all(stats, ('yl', *OUTER), split_axis=0, concat_axis=0, tiled=...]
  transfers between devices with their start and end apart: 7 -> 7, of which waited for: 4 -> 4; matrix products, arithmetic and copies ran while one was open for 0% -> 0% of each run, Pallas kernels for 11% -> 12%
where the time goes in v5:
time: 111 us
  starting transfers between devices  32.2 us (29%)
  blocking collectives  30.3 us (27%)
  waiting for transfers between devices  29.1 us (26%)
  Pallas kernels  14.4 us (13%)
  local copies, waits for them, and re-layouts  4.04 us (4%)
    all_to_all x1, blocking collectives, shards(): got = lax.all_to_all(out, OUTER, split_axis=0, concat_axis=0, tiled=True)  30.3 us
    ppermute x3, waiting for transfers between devices, to_sides(): return lax.ppermute(x, LANE, perm)  18 us
    pallas_call x5, Pallas kernels, call(): return kernel(*operands)  14.4 us
    all_to_all x1, starting transfers between devices, shards(): lax.all_to_all(copies, 'z', split_axis=0, concat_axis=0, tiled=True)  10.3 us
    all_to_all x1, starting transfers between devices, shards(): lax.all_to_all(stats, ('yl', *OUTER), split_axis=0, concat_axis=0, tiled=...  10.1 us
    all_to_all x1, waiting for transfers between devices, shards(): lax.all_to_all(copies, 'z', split_axis=0, concat_axis=0, tiled=True)  9.2 us
    ppermute x3, starting transfers between devices, to_sides(): return lax.ppermute(x, LANE, perm)  7.06 us
    ppermute x2, starting transfers between devices, swapped(): return lax.ppermute(x, 'c', [(0, 1), (1, 0)])  4.68 us
  transfers between devices with their start and end apart: 7, of which 4 were waited for; matrix products, arithmetic and copies ran while one was open for 0% of the time, Pallas kernels for 12%

profile of v5, /device:TPU:16, one launch (start us, length us, event | category | flops | bytes accessed | tf_op | source)
XLA Modules:
  0.0 110.8 jit_solution(3826130463136171427)
XLA Ops:
  0.6 0.0 copy-start.1
  0.6 0.0 copy-start.4
  0.6 1.9 %broadcast_in_dim.3 = bf16[8,64,768]{2,1,0:T(8,128)(2,1)} broadcast(bf16[64,768]{1,0:T(8,128)(2,1)} %param.4), dimensions={1,2} | broadcast | bytes 884736 | tf_op jit(solution)/shard_map/broadcast_in_dim | solution.py:183
  2.6 10.3 %all-to-all-start = ((bf16[8,64,768]{2,1,0:T(8,128)(2,1)}), bf16[8,64,768]{2,1,0:T(8,128)(2,1)S(1)}, u32[]{:S(2)}, u32[]{:S(2)}) async-start(bf16[8,64,768]{2,1,0:T(8,128)(2,1)} %broadcast_in_dim.3), calls=%async_computation | async-start | bytes 1572864 | tf_op jit(solution)/shard_map/all_to_all | solution.py:184
  12.9 0.0 copy-done.1
  12.9 2.4 %collective-permute-start = (bf16[512,768]{1,0:T(8,128)(2,1)S(1)}, bf16[512,768]{1,0:T(8,128)(2,1)S(1)}, u32[]{:S(2)}, u32[]{:S(2)}) collective-permute-start(bf16[512,768]{1,0:T(8,128)(2,1)S(1)} %copy-done.1), channel_id=1, source_target_pairs={{0,386},{1,3},{2,0},{3,129},{128,2},{129,131},{130,128},{131,257},... | collective-permute-start | bytes 2359304 | tf_op jit(solution)/shard_map/ppermute | solution.py:31
  15.3 0.0 copy-done.4
  15.3 2.4 %collective-permute-start.1 = (s32[1,512]{1,0:T(1,128)S(1)}, s32[1,512]{1,0:T(1,128)S(1)}, u32[]{:S(2)}, u32[]{:S(2)}) collective-permute-start(s32[1,512]{1,0:T(1,128)S(1)} %bitcast.15), channel_id=1, source_target_pairs={{0,386},{1,3},{2,0},{3,129},{128,2},{129,131},{130,128},{131,257},... | collective-permute-start | bytes 6152 | tf_op jit(solution)/shard_map/ppermute | solution.py:31
  17.6 9.2 %collective-permute-done.1.posf_ref = s32[1,512]{1,0:T(1,128)S(1)} collective-permute-done((s32[1,512]{1,0:T(1,128)S(1)}, s32[1,512]{1,0:T(1,128)S(1)}, u32[]{:S(2)}, u32[]{:S(2)}) %collective-permute-start.1) | collective-permute-done | bytes 2080 | tf_op jit(solution)/shard_map/ppermute | solution.py:31
  26.8 0.0 collective-permute-done.qf_ref
  26.8 9.2 %all-to-all-done = bf16[8,64,768]{2,1,0:T(8,128)(2,1)S(1)} async-done(((bf16[8,64,768]{2,1,0:T(8,128)(2,1)}), bf16[8,64,768]{2,1,0:T(8,128)(2,1)S(1)}, u32[]{:S(2)}, u32[]{:S(2)}) %all-to-all-start) | async-done | bytes 786464 | tf_op jit(solution)/shard_map/all_to_all | solution.py:184
  36.0 0.0 copy-start
  36.0 2.3 %collective-permute-start.3 = (bf16[512,768]{1,0:T(8,128)(2,1)S(1)}, bf16[512,768]{1,0:T(8,128)(2,1)}, u32[]{:S(2)}, u32[]{:S(2)}) collective-permute-start(bf16[512,768]{1,0:T(8,128)(2,1)S(1)} %bitcast.10), channel_id=1, source_target_pairs={{0,386},{1,3},{2,0},{3,129},{128,2},{129,131},{130,128},{131,257},... | collective-permute-start | bytes 2359304 | tf_op jit(solution)/shard_map/ppermute | solution.py:31
  38.4 2.8 %collective-permute-start.2 = (bf16[512,768]{1,0:T(8,128)(2,1)S(1)}, bf16[512,768]{1,0:T(8,128)(2,1)}, u32[]{:S(2)}, u32[]{:S(2)}) collective-permute-start(bf16[512,768]{1,0:T(8,128)(2,1)S(1)} %bitcast.11), channel_id=1, source_target_pairs={{0,1},{1,0},{2,3},{3,2},{4,5},{5,4},{6,7},{7,6},{8,9},{9,8},{10,11... | collective-permute-start | bytes 2359304 | tf_op jit(solution)/shard_map/ppermute | solution.py:23
  41.1 8.8 %collective-permute-done.3.a_hbm = bf16[512,768]{1,0:T(8,128)(2,1)} collective-permute-done((bf16[512,768]{1,0:T(8,128)(2,1)S(1)}, bf16[512,768]{1,0:T(8,128)(2,1)}, u32[]{:S(2)}, u32[]{:S(2)}) %collective-permute-start.3) | collective-permute-done | bytes 786464 | tf_op jit(solution)/shard_map/ppermute | solution.py:31
  50.0 1.9 %collective-permute-start.4 = (bf16[512,768]{1,0:T(8,128)(2,1)}, bf16[512,768]{1,0:T(8,128)(2,1)S(1)}, u32[]{:S(2)}, u32[]{:S(2)}) collective-permute-start(bf16[512,768]{1,0:T(8,128)(2,1)} %collective-permute-done.3.a_hbm), channel_id=1, source_target_pairs={{0,1},{1,0},{2,3},{3,2},{4,5},{5,4},{6,7},{7,6},{8,9},{9,8},{10,11... | collective-permute-start | bytes 2359304 | tf_op jit(solution)/shard_map/ppermute | solution.py:23
  51.9 0.1 stack.23.base_ref
  52.0 0.0 collective-permute-done.2.b_ref.b_hbm
  52.0 4.8 %shard_map.50 = (f32[8,512]{1,0:T(8,128)S(1)}, bf16[1024,512]{1,0:T(8,128)(2,1)}, f32[32,4,512]{2,1,0:T(4,128)}) custom-call(s32[5]{0:T(128)S(1)} %stack.23.base_ref, bf16[512,768]{1,0:T(8,128)(2,1)S(1)} %bitcast.12, bf16[512,768]{1,0:T(8,128)(2,1)} %collective-permute-done.2.b_ref.b_hbm, bf16[512,768]{1,0:T(8,128)(2,1)S(1)} %copy-done.1, ...), custom_call_target="tpu_custom_call" | custom-call | flops 1610612736 | bytes 4194304 | tf_op jit(solution)/shard_map/pallas_call | solution.py:158
  56.8 0.0 copy-done
  56.8 10.1 %all-to-all-start.1 = ((f32[32,4,512]{2,1,0:T(4,128)}), f32[32,4,512]{2,1,0:T(4,128)S(1)}, u32[]{:S(2)}, u32[]{:S(2)}) async-start(f32[32,4,512]{2,1,0:T(4,128)} %get-tuple-element.18), calls=%async_computation.1 | async-start | bytes 524288 | tf_op jit(solution)/shard_map/all_to_all | solution.py:198
  67.0 4.0 %shard_map.51 = (f32[768,512]{1,0:T(8,128)S(1)}, bf16[768,512]{1,0:T(8,128)(2,1)S(1)}) custom-call(s32[5]{0:T(128)S(1)} %stack.23.base_ref, bf16[512,768]{1,0:T(8,128)(2,1)} %bitcast.13, bf16[512,768]{1,0:T(8,128)(2,1)} %collective-permute-done.2.b_ref.b_hbm, bf16[1024,512]{1,0:T(8,128)(2,1)} %get-tuple-element.20.w_hbm, s32[1,512]{1,0:T(1,128)S(1)} %bitcast.17), custom_call_target="tpu_custom_call" | custom-call | flops 1610612736 | bytes 4194304 | tf_op jit(solution)/shard_map/pallas_call | solution.py:158
  70.9 0.0 collective-permute-done.4.b_ref
  70.9 0.0 copy-start.2
  70.9 0.9 copy-done.2
  71.8 0.0 copy-start.3
  71.8 1.1 %copy-done.3 = bf16[512,768]{1,0:T(8,128)(2,1)S(1)} copy-done((bf16[512,768]{1,0:T(8,128)(2,1)S(1)}, bf16[512,768]{1,0:T(8,128)(2,1)}, u32[]{:S(2)}) %copy-start.3) | copy-done | bytes 786456
  73.0 4.3 %shard_map.52 = (f32[8,512]{1,0:T(8,128)S(1)}, f32[768,512]{1,0:T(8,128)S(1)}, bf16[768,512]{1,0:T(8,128)(2,1)S(1)}) custom-call(s32[5]{0:T(128)S(1)} %stack.23.base_ref, bf16[512,768]{1,0:T(8,128)(2,1)} %collective-permute-done.3.a_hbm, bf16[512,768]{1,0:T(8,128)(2,1)S(1)} %copy-done.3, bf16[512,768]{1,0:T(8,128)(2,1)S(1)} %copy-done.1, ...), custom_call_target="tpu_custom_call" | custom-call | flops 2415919104 | bytes 4194304 | tf_op jit(solution)/shard_map/pallas_call | solution.py:158
  77.3 1.9 %all-to-all-done.1.every_ref = f32[32,4,512]{2,1,0:T(4,128)S(1)} async-done(((f32[32,4,512]{2,1,0:T(4,128)}), f32[32,4,512]{2,1,0:T(4,128)S(1)}, u32[]{:S(2)}, u32[]{:S(2)}) %all-to-all-start.1) | async-done | bytes 262176 | tf_op jit(solution)/shard_map/all_to_all | solution.py:198
  79.1 0.7 shard_map.53
  79.8 30.3 %all_to_all.15.got_ref = bf16[16,48,512]{2,1,0:T(8,128)(2,1)S(1)} all-to-all(bf16[16,48,512]{2,1,0:T(8,128)(2,1)S(1)} %bitcast.14), channel_id=1, replica_groups=mesh['yh'=4,'x'=4,'z'=8,'yl'=2,'c'=2] {'yh','x'}, dimensions={0} | all-to-all | bytes 1572864 | tf_op jit(solution)/shard_map/all_to_all | solution.py:219
  110.1 0.7 shard_map.54
Async XLA Ops:
  0.6 12.3 %copy-start.1 = (bf16[512,768]{1,0:T(8,128)(2,1)S(1)}, bf16[512,768]{1,0:T(8,128)(2,1)}, u32[]{:S(2)}) copy-start(bf16[512,768]{1,0:T(8,128)(2,1)} %q_ref.3) | copy-start | bytes 2359300
  0.6 14.6 %copy-start.4 = (s32[512]{0:T(512)S(1)}, s32[512]{0:T(512)}, u32[]{:S(2)}) copy-start(s32[512]{0:T(512)} %param.5) | copy-start | bytes 6148
  2.6 33.4 %all-to-all-start = ((bf16[8,64,768]{2,1,0:T(8,128)(2,1)}), bf16[8,64,768]{2,1,0:T(8,128)(2,1)S(1)}, u32[]{:S(2)}, u32[]{:S(2)}) async-start(bf16[8,64,768]{2,1,0:T(8,128)(2,1)} %broadcast_in_dim.3), calls=%async_computation | async-start | bytes 1572864 | tf_op jit(solution)/shard_map/all_to_all | solution.py:184
  12.9 13.9 %collective-permute-start = (bf16[512,768]{1,0:T(8,128)(2,1)S(1)}, bf16[512,768]{1,0:T(8,128)(2,1)S(1)}, u32[]{:S(2)}, u32[]{:S(2)}) collective-permute-start(bf16[512,768]{1,0:T(8,128)(2,1)S(1)} %copy-done.1), channel_id=1, source_target_pairs={{0,386},{1,3},{2,0},{3,129},{128,2},{129,131},{130,128},{131,257},... | collective-permute-start | bytes 2359304 | tf_op jit(solution)/shard_map/ppermute | solution.py:31
  15.3 11.5 %collective-permute-start.1 = (s32[1,512]{1,0:T(1,128)S(1)}, s32[1,512]{1,0:T(1,128)S(1)}, u32[]{:S(2)}, u32[]{:S(2)}) collective-permute-start(s32[1,512]{1,0:T(1,128)S(1)} %bitcast.15), channel_id=1, source_target_pairs={{0,386},{1,3},{2,0},{3,129},{128,2},{129,131},{130,128},{131,257},... | collective-permute-start | bytes 6152 | tf_op jit(solution)/shard_map/ppermute | solution.py:31
  36.0 20.8 %copy-start = (bf16[8,64,768]{2,1,0:T(8,128)(2,1)}, bf16[8,64,768]{2,1,0:T(8,128)(2,1)S(1)}, u32[]{:S(2)}) copy-start(bf16[8,64,768]{2,1,0:T(8,128)(2,1)S(1)} %all-to-all-done) | copy-start | bytes 2359300
  36.0 14.0 %collective-permute-start.3 = (bf16[512,768]{1,0:T(8,128)(2,1)S(1)}, bf16[512,768]{1,0:T(8,128)(2,1)}, u32[]{:S(2)}, u32[]{:S(2)}) collective-permute-start(bf16[512,768]{1,0:T(8,128)(2,1)S(1)} %bitcast.10), channel_id=1, source_target_pairs={{0,386},{1,3},{2,0},{3,129},{128,2},{129,131},{130,128},{131,257},... | collective-permute-start | bytes 2359304 | tf_op jit(solution)/shard_map/ppermute | solution.py:31
  38.4 13.7 %collective-permute-start.2 = (bf16[512,768]{1,0:T(8,128)(2,1)S(1)}, bf16[512,768]{1,0:T(8,128)(2,1)}, u32[]{:S(2)}, u32[]{:S(2)}) collective-permute-start(bf16[512,768]{1,0:T(8,128)(2,1)S(1)} %bitcast.11), channel_id=1, source_target_pairs={{0,1},{1,0},{2,3},{3,2},{4,5},{5,4},{6,7},{7,6},{8,9},{9,8},{10,11... | collective-permute-start | bytes 2359304 | tf_op jit(solution)/shard_map/ppermute | solution.py:23
  50.0 21.0 %collective-permute-start.4 = (bf16[512,768]{1,0:T(8,128)(2,1)}, bf16[512,768]{1,0:T(8,128)(2,1)S(1)}, u32[]{:S(2)}, u32[]{:S(2)}) collective-permute-start(bf16[512,768]{1,0:T(8,128)(2,1)} %collective-permute-done.3.a_hbm), channel_id=1, source_target_pairs={{0,1},{1,0},{2,3},{3,2},{4,5},{5,4},{6,7},{7,6},{8,9},{9,8},{10,11... | collective-permute-start | bytes 2359304 | tf_op jit(solution)/shard_map/ppermute | solution.py:23
  56.8 22.3 %all-to-all-start.1 = ((f32[32,4,512]{2,1,0:T(4,128)}), f32[32,4,512]{2,1,0:T(4,128)S(1)}, u32[]{:S(2)}, u32[]{:S(2)}) async-start(f32[32,4,512]{2,1,0:T(4,128)} %get-tuple-element.18), calls=%async_computation.1 | async-start | bytes 524288 | tf_op jit(solution)/shard_map/all_to_all | solution.py:198
  70.9 0.9 copy-start.2
  71.8 1.1 %copy-start.3 = (bf16[512,768]{1,0:T(8,128)(2,1)S(1)}, bf16[512,768]{1,0:T(8,128)(2,1)}, u32[]{:S(2)}) copy-start(bf16[512,768]{1,0:T(8,128)(2,1)} %copy-done.2) | copy-start | bytes 2359300

commit v6 on v5

--- a/solution.py
+++ b/solution.py
@@ -14,6 +14,7 @@
 OUTER = ("yh", "x")
 LANE = ("yh", "yl", "c")
 F32, BF16 = jnp.float32, jnp.bfloat16
+LOG2E = math.log2(math.e)
 VMEM = pl.BlockSpec(memory_space=pltpu.VMEM)
 SMEM = pl.BlockSpec(memory_space=pltpu.SMEM)
 HBM = pl.BlockSpec(memory_space=pltpu.HBM)
@@ -40,12 +41,12 @@
     return (j // rows) * (4 * rows) + j % rows == pos_ref[...] - base
 
 
-def statistics(p_refs, bases, q_ref, pos_ref, s_ref, scale, rows):
+def statistics(p_refs, bases, q_ref, pos_ref, s_ref, rows):
     q = q_ref[...]
     top = ps = None
     for i, p_ref in enumerate(p_refs):
         n = p_ref.shape[0]
-        s = dot(p_ref[...], q, ((1,), (1,))) * scale
+        s = dot(p_ref[...], q, ((1,), (1,)))
         s_ref[i * n : (i + 1) * n, :] = s
         hit = hits_of(pos_ref, bases[i], n, rows)
         t = jnp.max(s, axis=0, keepdims=True)
@@ -70,15 +71,15 @@
     bases = (base_ref[0], base_ref[1])
     pieces = []
     for qq, pp in ((q_ref, pos_ref), (qf_ref, posf_ref)):
-        top, ps = statistics((a_ref, b_ref), bases, qq, pp, s_ref, scale, rows)
-        e = jnp.exp(s_ref[...] - top)
+        top, ps = statistics((a_ref, b_ref), bases, qq, pp, s_ref, rows)
+        e = jnp.exp2((s_ref[...] - top) * (scale * LOG2E))
         total = jnp.sum(e, axis=0, keepdims=True)
         if not pieces:
             w_ref[...] = e.astype(BF16)
             copy = pltpu.make_async_copy(w_ref, w_hbm, sem)
             copy.start()
             st_ref[0:1, :] = top
-        pieces.append(jnp.concatenate([top, total, ps, ps], axis=0))
+        pieces.append(jnp.concatenate([top * scale + jnp.log(total), ps * scale], axis=1))
     own, theirs = pieces
     lower = base_ref[4] == 0
     half = out_ref.shape[0] // 2
@@ -110,26 +111,36 @@
     bases = (base_ref[3], base_ref[2])
     q = q_ref[...]
     n = b_ref.shape[0]
-    s_ref[:n, :] = dot(b_ref[...], q, ((1,), (1,))) * scale
+    s_ref[:n, :] = dot(b_ref[...], q, ((1,), (1,)))
     copy.wait()
-    s_ref[n:, :] = dot(a_ref[...], q, ((1,), (1,))) * scale
+    s_ref[n:, :] = dot(a_ref[...], q, ((1,), (1,)))
     top0 = st0_ref[0:1, :]
     top = jnp.maximum(jnp.max(s_ref[...], axis=0, keepdims=True), top0)
-    w_ref[...] = jnp.exp(s_ref[...] - top).astype(BF16)
+    w_ref[...] = jnp.exp2((s_ref[...] - top) * (scale * LOG2E)).astype(BF16)
     mix, chosen = products((b_ref, a_ref), bases, w_ref, pos_ref, rows)
     st_ref[0:1, :] = top
-    m_ref[...] = mix + mix0_ref[...] * jnp.exp(top0 - top)
+    m_ref[...] = mix + mix0_ref[...] * jnp.exp2((top0 - top) * (scale * LOG2E))
     c_ref[...] = (chosen + ch0_ref[...].astype(F32)).astype(BF16)
 
 
-def scale_kernel(every_ref, st_ref, m_ref, c_ref, out_ref, loss_ref):
-    tops = every_ref[:, 0, :]
-    top = jnp.max(tops, axis=0, keepdims=True)
-    total = jnp.sum(every_ref[:, 1, :] * jnp.exp(tops - top), axis=0, keepdims=True)
-    ps = jnp.sum(every_ref[:, 2, :], axis=0, keepdims=True)
-    g = jnp.exp(st_ref[0:1, :] - top) / total
+def scale_kernel(scale, every_ref, st_ref, m_ref, c_ref, out_ref, loss_ref):
+    count = m_ref.shape[1]
+    lse = every_ref[:, 0, :count]
+    most = jnp.max(lse, axis=0, keepdims=True)
+    whole = most + jnp.log(jnp.sum(jnp.exp(lse - most), axis=0, keepdims=True))
+    ps = jnp.sum(every_ref[:, 0, count:], axis=0, keepdims=True)
+    g = jnp.exp(st_ref[0:1, :] * scale - whole)
     out_ref[...] = (m_ref[...] * g - c_ref[...].astype(F32)).astype(BF16)
-    loss_ref[...] = top + jnp.log(total) - ps
+    loss_ref[...] = whole - ps
+
+
+def copy_kernel(x_ref, out_hbm, sems):
+    n = out_hbm.shape[0]
+    copies = [pltpu.make_async_copy(x_ref, out_hbm.at[i], sems.at[i]) for i in range(n)]
+    for copy in copies:
+        copy.start()
+    for copy in copies:
+        copy.wait()
 
 
 def final_kernel(scale, got_ref, grad_ref):
@@ -180,7 +191,9 @@
 
     theirs = to_sides(queries, ny)
     pos_theirs = to_sides(pos, ny)
-    copies = jnp.broadcast_to(passages, (nz, rows, width))
+    (copies,) = call(
+        copy_kernel, [((nz, rows, width), BF16)], (passages,), [pltpu.SemaphoreType.DMA((nz,))], hbm_out=(0,)
+    )
     column = lax.all_to_all(copies, "z", split_axis=0, concat_axis=0, tiled=True)
     column, theirs, pos_theirs = lax.optimization_barrier((column, theirs, pos_theirs))
     column = column.reshape(n, width)
@@ -189,7 +202,7 @@
     members = ny * nx
     st1, weights, stats = call(
         functools.partial(stat_kernel, scale, rows),
-        [((8, count), F32), ((2 * n, count), BF16), ((members, 4, count), F32)],
+        [((8, count), F32), ((2 * n, count), BF16), ((members, 1, 2 * count), F32)],
         (base, column, column2, queries, pos, theirs, pos_theirs),
         [((2 * n, count), F32), ((2 * n, count), BF16), pltpu.SemaphoreType.DMA],
         4 * flops,
@@ -213,7 +226,9 @@
         6 * flops,
         hbm_in=(1,),
     )
-    out, loss = call(scale_kernel, [((width, count), BF16), ((1, count), F32)], (every, st, m, ch))
+    out, loss = call(
+        functools.partial(scale_kernel, scale), [((width, count), BF16), ((1, count), F32)], (every, st, m, ch)
+    )
     n_outer = members // 2
     out = out.reshape(n_outer, width // n_outer, count)
     got = lax.all_to_all(out, OUTER, split_axis=0, concat_axis=0, tiled=True)

time: 111 us -> 111 us (level)
  waiting for transfers between devices: 29.1 us -> 27.2 us
  blocking collectives: 30.3 us -> 32.1 us
    broadcast_in_dim x1 -> x0, local copies, waits for them, and re-layouts: 1.92 us -> none  [shards(): copies = jnp.broadcast_to(passages, (nz, rows, width))]
    all_to_all x1, waiting for transfers between devices: 1.86 us -> 0.01 us  [shards(): lax.all_to_all(stats, ('yl', *OUTER), split_axis=0, concat_axis=0, tiled=...]
    all_to_all x1, blocking collectives: 30.3 us -> 32.1 us  [shards(): got = lax.all_to_all(out, OUTER, split_axis=0, concat_axis=0, tiled=True)]
    unnamed x10 -> x12, local copies, waits for them, and re-layouts: 2.03 us -> 2.91 us
    pallas_call x5 -> x6, Pallas kernels: 14.4 us -> 14.8 us  [call(): return kernel(*operands)]
  transfers between devices with their start and end apart: 7 -> 7, of which waited for: 4 -> 3; matrix products, arithmetic and copies ran while one was open for 0% -> 0% of each run, Pallas kernels for 12% -> 11%
where the time goes in v6:
time: 111 us; the launch traced here: 110 us
  starting transfers between devices  32.2 us (29%)
  blocking collectives  32.1 us (29%)
  waiting for transfers between devices  27.2 us (25%)
  Pallas kernels  14.8 us (13%)
  local copies, waits for them, and re-layouts  3 us (3%)
    all_to_all x1, blocking collectives, shards(): got = lax.all_to_all(out, OUTER, split_axis=0, concat_axis=0, tiled=True)  32.1 us
    ppermute x3, waiting for transfers between devices, to_sides(): return lax.ppermute(x, LANE, perm)  18 us
    pallas_call x6, Pallas kernels, call(): return kernel(*operands)  14.8 us
    all_to_all x1, starting transfers between devices, shards(): lax.all_to_all(copies, 'z', split_axis=0, concat_axis=0, tiled=True)  10.3 us
    all_to_all x1, starting transfers between devices, shards(): lax.all_to_all(stats, ('yl', *OUTER), split_axis=0, concat_axis=0, tiled=...  10.1 us
    all_to_all x1, waiting for transfers between devices, shards(): lax.all_to_all(copies, 'z', split_axis=0, concat_axis=0, tiled=True)  9.2 us
    ppermute x3, starting transfers between devices, to_sides(): return lax.ppermute(x, LANE, perm)  7.06 us
    ppermute x2, starting transfers between devices, swapped(): return lax.ppermute(x, 'c', [(0, 1), (1, 0)])  4.68 us
  transfers between devices with their start and end apart: 7, of which 3 were waited for; matrix products, arithmetic and copies ran while one was open for 0% of the time, Pallas kernels for 11%

profile of v6, /device:TPU:16, one launch (start us, length us, event | category | flops | bytes accessed | tf_op | source)
XLA Modules:
  0.0 110.2 jit_solution(11147437357057893833)
XLA Ops:
  0.6 0.0 copy-start.1
  0.6 0.9 copy-done.1
  1.5 0.0 copy-start.2
  1.5 1.0 shard_map.50
  2.5 10.3 %all-to-all-start = ((bf16[8,64,768]{2,1,0:T(8,128)(2,1)}), bf16[8,64,768]{2,1,0:T(8,128)(2,1)S(1)}, u32[]{:S(2)}, u32[]{:S(2)}) async-start(bf16[8,64,768]{2,1,0:T(8,128)(2,1)} %shard_map.50), calls=%async_computation | async-start | bytes 1572864 | tf_op jit(solution)/shard_map/all_to_all | solution.py:197
  12.8 0.0 copy-done.2
  12.8 2.4 %collective-permute-start = (bf16[512,768]{1,0:T(8,128)(2,1)S(1)}, bf16[512,768]{1,0:T(8,128)(2,1)S(1)}, u32[]{:S(2)}, u32[]{:S(2)}) collective-permute-start(bf16[512,768]{1,0:T(8,128)(2,1)S(1)} %copy-done.2), channel_id=1, source_target_pairs={{0,386},{1,3},{2,0},{3,129},{128,2},{129,131},{130,128},{131,257},... | collective-permute-start | bytes 2359304 | tf_op jit(solution)/shard_map/ppermute | solution.py:32
  15.2 0.0 copy-done.5
  15.2 2.4 %collective-permute-start.1 = (s32[1,512]{1,0:T(1,128)S(1)}, s32[1,512]{1,0:T(1,128)S(1)}, u32[]{:S(2)}, u32[]{:S(2)}) collective-permute-start(s32[1,512]{1,0:T(1,128)S(1)} %bitcast.15), channel_id=1, source_target_pairs={{0,386},{1,3},{2,0},{3,129},{128,2},{129,131},{130,128},{131,257},... | collective-permute-start | bytes 6152 | tf_op jit(solution)/shard_map/ppermute | solution.py:32
  17.6 9.2 %collective-permute-done.1.posf_ref = s32[1,512]{1,0:T(1,128)S(1)} collective-permute-done((s32[1,512]{1,0:T(1,128)S(1)}, s32[1,512]{1,0:T(1,128)S(1)}, u32[]{:S(2)}, u32[]{:S(2)}) %collective-permute-start.1) | collective-permute-done | bytes 2080 | tf_op jit(solution)/shard_map/ppermute | solution.py:32
  26.7 0.0 collective-permute-done.qf_ref
  26.7 9.2 %all-to-all-done = bf16[8,64,768]{2,1,0:T(8,128)(2,1)S(1)} async-done(((bf16[8,64,768]{2,1,0:T(8,128)(2,1)}), bf16[8,64,768]{2,1,0:T(8,128)(2,1)S(1)}, u32[]{:S(2)}, u32[]{:S(2)}) %all-to-all-start) | async-done | bytes 786464 | tf_op jit(solution)/shard_map/all_to_all | solution.py:197
  35.9 0.0 copy-start
  35.9 2.3 %collective-permute-start.3 = (bf16[512,768]{1,0:T(8,128)(2,1)S(1)}, bf16[512,768]{1,0:T(8,128)(2,1)}, u32[]{:S(2)}, u32[]{:S(2)}) collective-permute-start(bf16[512,768]{1,0:T(8,128)(2,1)S(1)} %bitcast.10), channel_id=1, source_target_pairs={{0,386},{1,3},{2,0},{3,129},{128,2},{129,131},{130,128},{131,257},... | collective-permute-start | bytes 2359304 | tf_op jit(solution)/shard_map/ppermute | solution.py:32
  38.3 2.8 %collective-permute-start.2 = (bf16[512,768]{1,0:T(8,128)(2,1)S(1)}, bf16[512,768]{1,0:T(8,128)(2,1)}, u32[]{:S(2)}, u32[]{:S(2)}) collective-permute-start(bf16[512,768]{1,0:T(8,128)(2,1)S(1)} %bitcast.11), channel_id=1, source_target_pairs={{0,1},{1,0},{2,3},{3,2},{4,5},{5,4},{6,7},{7,6},{8,9},{9,8},{10,11... | collective-permute-start | bytes 2359304 | tf_op jit(solution)/shard_map/ppermute | solution.py:24
  41.1 8.8 %collective-permute-done.3.a_hbm = bf16[512,768]{1,0:T(8,128)(2,1)} collective-permute-done((bf16[512,768]{1,0:T(8,128)(2,1)S(1)}, bf16[512,768]{1,0:T(8,128)(2,1)}, u32[]{:S(2)}, u32[]{:S(2)}) %collective-permute-start.3) | collective-permute-done | bytes 786464 | tf_op jit(solution)/shard_map/ppermute | solution.py:32
  49.9 1.9 %collective-permute-start.4 = (bf16[512,768]{1,0:T(8,128)(2,1)}, bf16[512,768]{1,0:T(8,128)(2,1)S(1)}, u32[]{:S(2)}, u32[]{:S(2)}) collective-permute-start(bf16[512,768]{1,0:T(8,128)(2,1)} %collective-permute-done.3.a_hbm), channel_id=1, source_target_pairs={{0,1},{1,0},{2,3},{3,2},{4,5},{5,4},{6,7},{7,6},{8,9},{9,8},{10,11... | collective-permute-start | bytes 2359304 | tf_op jit(solution)/shard_map/ppermute | solution.py:24
  51.9 0.1 stack.23.base_ref
  52.0 0.0 collective-permute-done.2.b_ref.b_hbm
  52.0 4.4 %shard_map.51 = (f32[8,512]{1,0:T(8,128)S(1)}, bf16[1024,512]{1,0:T(8,128)(2,1)}, f32[32,1,1024]{2,1,0:T(1,128)}) custom-call(s32[5]{0:T(128)S(1)} %stack.23.base_ref, bf16[512,768]{1,0:T(8,128)(2,1)S(1)} %bitcast.12, bf16[512,768]{1,0:T(8,128)(2,1)} %collective-permute-done.2.b_ref.b_hbm, bf16[512,768]{1,0:T(8,128)(2,1)S(1)} %copy-done.2, ...), custom_call_target="tpu_custom_call" | custom-call | flops 1610612736 | bytes 4194304 | tf_op jit(solution)/shard_map/pallas_call | solution.py:169
  56.3 0.0 copy-done
  56.3 10.1 %all-to-all-start.1 = ((f32[32,1,1024]{2,1,0:T(1,128)}), f32[32,1,1024]{2,1,0:T(1,128)S(1)}, u32[]{:S(2)}, u32[]{:S(2)}) async-start(f32[32,1,1024]{2,1,0:T(1,128)} %get-tuple-element.18), calls=%async_computation.1 | async-start | bytes 262144 | tf_op jit(solution)/shard_map/all_to_all | solution.py:211
  66.5 4.0 %shard_map.52 = (f32[768,512]{1,0:T(8,128)S(1)}, bf16[768,512]{1,0:T(8,128)(2,1)S(1)}) custom-call(s32[5]{0:T(128)S(1)} %stack.23.base_ref, bf16[512,768]{1,0:T(8,128)(2,1)} %bitcast.13, bf16[512,768]{1,0:T(8,128)(2,1)} %collective-permute-done.2.b_ref.b_hbm, bf16[1024,512]{1,0:T(8,128)(2,1)} %get-tuple-element.20.w_hbm, s32[1,512]{1,0:T(1,128)S(1)} %bitcast.17), custom_call_target="tpu_custom_call" | custom-call | flops 1610612736 | bytes 4194304 | tf_op jit(solution)/shard_map/pallas_call | solution.py:169
  70.4 0.0 collective-permute-done.4.b_ref
  70.4 0.0 copy-start.3
  70.5 0.9 copy-done.3
  71.3 1.1 %copy-done.4 = bf16[512,768]{1,0:T(8,128)(2,1)S(1)} copy-done((bf16[512,768]{1,0:T(8,128)(2,1)S(1)}, bf16[512,768]{1,0:T(8,128)(2,1)}, u32[]{:S(2)}) %copy-start.4) | copy-done | bytes 786456
  72.5 4.2 %shard_map.53 = (f32[8,512]{1,0:T(8,128)S(1)}, f32[768,512]{1,0:T(8,128)S(1)}, bf16[768,512]{1,0:T(8,128)(2,1)S(1)}) custom-call(s32[5]{0:T(128)S(1)} %stack.23.base_ref, bf16[512,768]{1,0:T(8,128)(2,1)} %collective-permute-done.3.a_hbm, bf16[512,768]{1,0:T(8,128)(2,1)S(1)} %copy-done.4, bf16[512,768]{1,0:T(8,128)(2,1)S(1)} %copy-done.2, ...), custom_call_target="tpu_custom_call" | custom-call | flops 2415919104 | bytes 4194304 | tf_op jit(solution)/shard_map/pallas_call | solution.py:169
  76.7 0.0 all-to-all-done.1.every_ref
  76.7 0.6 shard_map.54
  77.3 32.1 %all_to_all.15.got_ref = bf16[16,48,512]{2,1,0:T(8,128)(2,1)S(1)} all-to-all(bf16[16,48,512]{2,1,0:T(8,128)(2,1)S(1)} %bitcast.14), channel_id=1, replica_groups=mesh['yh'=4,'x'=4,'z'=8,'yl'=2,'c'=2] {'yh','x'}, dimensions={0} | all-to-all | bytes 1572864 | tf_op jit(solution)/shard_map/all_to_all | solution.py:234
  109.4 0.7 shard_map.55
  (2 shorter events, 0.0 us)
Async XLA Ops:
  0.6 0.9 copy-start.1
  1.5 11.3 %copy-start.2 = (bf16[512,768]{1,0:T(8,128)(2,1)S(1)}, bf16[512,768]{1,0:T(8,128)(2,1)}, u32[]{:S(2)}) copy-start(bf16[512,768]{1,0:T(8,128)(2,1)} %q_ref.3) | copy-start | bytes 2359300
  1.5 13.7 %copy-start.5 = (s32[512]{0:T(512)S(1)}, s32[512]{0:T(512)}, u32[]{:S(2)}) copy-start(s32[512]{0:T(512)} %param.5) | copy-start | bytes 6148
  2.5 33.4 %all-to-all-start = ((bf16[8,64,768]{2,1,0:T(8,128)(2,1)}), bf16[8,64,768]{2,1,0:T(8,128)(2,1)S(1)}, u32[]{:S(2)}, u32[]{:S(2)}) async-start(bf16[8,64,768]{2,1,0:T(8,128)(2,1)} %shard_map.50), calls=%async_computation | async-start | bytes 1572864 | tf_op jit(solution)/shard_map/all_to_all | solution.py:197
  12.8 13.9 %collective-permute-start = (bf16[512,768]{1,0:T(8,128)(2,1)S(1)}, bf16[512,768]{1,0:T(8,128)(2,1)S(1)}, u32[]{:S(2)}, u32[]{:S(2)}) collective-permute-start(bf16[512,768]{1,0:T(8,128)(2,1)S(1)} %copy-done.2), channel_id=1, source_target_pairs={{0,386},{1,3},{2,0},{3,129},{128,2},{129,131},{130,128},{131,257},... | collective-permute-start | bytes 2359304 | tf_op jit(solution)/shard_map/ppermute | solution.py:32
  15.2 11.5 %collective-permute-start.1 = (s32[1,512]{1,0:T(1,128)S(1)}, s32[1,512]{1,0:T(1,128)S(1)}, u32[]{:S(2)}, u32[]{:S(2)}) collective-permute-start(s32[1,512]{1,0:T(1,128)S(1)} %bitcast.15), channel_id=1, source_target_pairs={{0,386},{1,3},{2,0},{3,129},{128,2},{129,131},{130,128},{131,257},... | collective-permute-start | bytes 6152 | tf_op jit(solution)/shard_map/ppermute | solution.py:32
  35.9 20.4 %copy-start = (bf16[8,64,768]{2,1,0:T(8,128)(2,1)}, bf16[8,64,768]{2,1,0:T(8,128)(2,1)S(1)}, u32[]{:S(2)}) copy-start(bf16[8,64,768]{2,1,0:T(8,128)(2,1)S(1)} %all-to-all-done) | copy-start | bytes 2359300
  35.9 14.0 %collective-permute-start.3 = (bf16[512,768]{1,0:T(8,128)(2,1)S(1)}, bf16[512,768]{1,0:T(8,128)(2,1)}, u32[]{:S(2)}, u32[]{:S(2)}) collective-permute-start(bf16[512,768]{1,0:T(8,128)(2,1)S(1)} %bitcast.10), channel_id=1, source_target_pairs={{0,386},{1,3},{2,0},{3,129},{128,2},{129,131},{130,128},{131,257},... | collective-permute-start | bytes 2359304 | tf_op jit(solution)/shard_map/ppermute | solution.py:32
  38.3 13.7 %collective-permute-start.2 = (bf16[512,768]{1,0:T(8,128)(2,1)S(1)}, bf16[512,768]{1,0:T(8,128)(2,1)}, u32[]{:S(2)}, u32[]{:S(2)}) collective-permute-start(bf16[512,768]{1,0:T(8,128)(2,1)S(1)} %bitcast.11), channel_id=1, source_target_pairs={{0,1},{1,0},{2,3},{3,2},{4,5},{5,4},{6,7},{7,6},{8,9},{9,8},{10,11... | collective-permute-start | bytes 2359304 | tf_op jit(solution)/shard_map/ppermute | solution.py:24
  49.9 20.5 %collective-permute-start.4 = (bf16[512,768]{1,0:T(8,128)(2,1)}, bf16[512,768]{1,0:T(8,128)(2,1)S(1)}, u32[]{:S(2)}, u32[]{:S(2)}) collective-permute-start(bf16[512,768]{1,0:T(8,128)(2,1)} %collective-permute-done.3.a_hbm), channel_id=1, source_target_pairs={{0,1},{1,0},{2,3},{3,2},{4,5},{5,4},{6,7},{7,6},{8,9},{9,8},{10,11... | collective-permute-start | bytes 2359304 | tf_op jit(solution)/shard_map/ppermute | solution.py:24
  56.3 20.4 %all-to-all-start.1 = ((f32[32,1,1024]{2,1,0:T(1,128)}), f32[32,1,1024]{2,1,0:T(1,128)S(1)}, u32[]{:S(2)}, u32[]{:S(2)}) async-start(f32[32,1,1024]{2,1,0:T(1,128)} %get-tuple-element.18), calls=%async_computation.1 | async-start | bytes 262144 | tf_op jit(solution)/shard_map/all_to_all | solution.py:211
  70.4 0.9 copy-start.3
  71.3 1.1 %copy-start.4 = (bf16[512,768]{1,0:T(8,128)(2,1)S(1)}, bf16[512,768]{1,0:T(8,128)(2,1)}, u32[]{:S(2)}) copy-start(bf16[512,768]{1,0:T(8,128)(2,1)} %copy-done.3) | copy-start | bytes 2359300

commit v7 on v6

--- a/solution.py
+++ b/solution.py
@@ -89,38 +89,35 @@
     copy.wait()
 
 
-def own_kernel(rows, base_ref, a_hbm, b_hbm, w_hbm, pos_ref, mix_ref, ch_ref, a_ref, b_ref, w_ref, sems):
-    pairs = ((a_hbm, a_ref), (b_hbm, b_ref), (w_hbm, w_ref))
+def load_kernel(*refs):
+    count = (len(refs) - 1) // 2
+    copies = [pltpu.make_async_copy(refs[i], refs[count + i], refs[-1].at[i]) for i in range(count)]
+    for copy in copies:
+        copy.start()
+    for copy in copies:
+        copy.wait()
+
+
+def mix_kernel(scale, rows, base_ref, a_hbm, b_hbm, wo_hbm, side_ref, side2_ref, q_ref, pos_ref, st0_ref, st_ref, m_ref, c_ref, s_ref, w_ref, a_ref, b_ref, wo_ref, sems):
+    pairs = ((a_hbm, a_ref), (b_hbm, b_ref), (wo_hbm, wo_ref))
     copies = [pltpu.make_async_copy(src, dst, sems.at[i]) for i, (src, dst) in enumerate(pairs)]
     for copy in copies:
         copy.start()
-    n = a_ref.shape[0]
-    chosen = 0.0
-    for i, p_ref in enumerate((a_ref, b_ref)):
-        hit = hits_of(pos_ref, base_ref[i], n, rows).astype(F32).astype(BF16)
-        copies[i].wait()
-        chosen += dot(p_ref[...], hit, ((0,), (0,)))
-    ch_ref[...] = chosen.astype(BF16)
-    copies[2].wait()
-    mix_ref[...] = dot(a_ref[...], w_ref[:n, :], ((0,), (0,))) + dot(b_ref[...], w_ref[n:, :], ((0,), (0,)))
-
-
-def near_kernel(scale, rows, base_ref, a_hbm, b_ref, q_ref, pos_ref, st0_ref, mix0_ref, ch0_ref, st_ref, m_ref, c_ref, s_ref, w_ref, a_ref, sem):
-    copy = pltpu.make_async_copy(a_hbm, a_ref, sem)
-    copy.start()
-    bases = (base_ref[3], base_ref[2])
     q = q_ref[...]
-    n = b_ref.shape[0]
-    s_ref[:n, :] = dot(b_ref[...], q, ((1,), (1,)))
-    copy.wait()
-    s_ref[n:, :] = dot(a_ref[...], q, ((1,), (1,)))
+    n = side2_ref.shape[0]
+    s_ref[:n, :] = dot(side2_ref[...], q, ((1,), (1,)))
+    s_ref[n:, :] = dot(side_ref[...], q, ((1,), (1,)))
     top0 = st0_ref[0:1, :]
     top = jnp.maximum(jnp.max(s_ref[...], axis=0, keepdims=True), top0)
     w_ref[...] = jnp.exp2((s_ref[...] - top) * (scale * LOG2E)).astype(BF16)
-    mix, chosen = products((b_ref, a_ref), bases, w_ref, pos_ref, rows)
     st_ref[0:1, :] = top
-    m_ref[...] = mix + mix0_ref[...] * jnp.exp2((top0 - top) * (scale * LOG2E))
-    c_ref[...] = (chosen + ch0_ref[...].astype(F32)).astype(BF16)
+    mix, chosen = products((side2_ref, side_ref), (base_ref[3], base_ref[2]), w_ref, pos_ref, rows)
+    m_ref[...] = mix
+    for copy in copies:
+        copy.wait()
+    mix, more = products((a_ref, b_ref), (base_ref[0], base_ref[1]), wo_ref, pos_ref, rows)
+    m_ref[...] += mix * jnp.exp2((top0 - top) * (scale * LOG2E))
+    c_ref[...] = (chosen + more).astype(BF16)
 
 
 def scale_kernel(scale, every_ref, st_ref, m_ref, c_ref, out_ref, loss_ref):
@@ -134,8 +131,11 @@
     loss_ref[...] = whole - ps
 
 
-def copy_kernel(x_ref, out_hbm, sems):
+def copy_kernel(x_hbm, out_hbm, x_ref, sems):
     n = out_hbm.shape[0]
+    first = pltpu.make_async_copy(x_hbm, x_ref, sems.at[n])
+    first.start()
+    first.wait()
     copies = [pltpu.make_async_copy(x_ref, out_hbm.at[i], sems.at[i]) for i in range(n)]
     for copy in copies:
         copy.start()
@@ -192,7 +192,12 @@
     theirs = to_sides(queries, ny)
     pos_theirs = to_sides(pos, ny)
     (copies,) = call(
-        copy_kernel, [((nz, rows, width), BF16)], (passages,), [pltpu.SemaphoreType.DMA((nz,))], hbm_out=(0,)
+        copy_kernel,
+        [((nz, rows, width), BF16)],
+        (passages,),
+        [((rows, width), BF16), pltpu.SemaphoreType.DMA((nz + 1,))],
+        hbm_in=(0,),
+        hbm_out=(0,),
     )
     column = lax.all_to_all(copies, "z", split_axis=0, concat_axis=0, tiled=True)
     column, theirs, pos_theirs = lax.optimization_barrier((column, theirs, pos_theirs))
@@ -209,22 +214,30 @@
         hbm_out=(1,),
     )
     every = lax.all_to_all(stats, ("yl", *OUTER), split_axis=0, concat_axis=0, tiled=True)
-    mix1, ch1 = call(
-        functools.partial(own_kernel, rows),
-        [((width, count), F32), ((width, count), BF16)],
-        (base, column, column2, weights, pos),
-        [((n, width), BF16), ((n, width), BF16), ((2 * n, count), BF16), pltpu.SemaphoreType.DMA((3,))],
-        4 * flops,
+    side2 = swapped(side)
+    queries, side = call(
+        load_kernel,
+        [(queries.shape, BF16), ((n, width), BF16)],
+        (queries, side),
+        [pltpu.SemaphoreType.DMA((2,))],
+        vmem=4,
+        hbm_in=(0, 1),
+    )
+    st, m, ch = call(
+        functools.partial(mix_kernel, scale, rows),
+        [((8, count), F32), ((width, count), F32), ((width, count), BF16)],
+        (base, column, column2, weights, side, side2, queries, pos, st1),
+        [
+            ((2 * n, count), F32),
+            ((2 * n, count), BF16),
+            ((n, width), BF16),
+            ((n, width), BF16),
+            ((2 * n, count), BF16),
+            pltpu.SemaphoreType.DMA((3,)),
+        ],
+        10 * flops,
+        vmem=24,
         hbm_in=(1, 2, 3),
-    )
-    side2 = swapped(side)
-    st, m, ch = call(
-        functools.partial(near_kernel, scale, rows),
-        [((8, count), F32), ((width, count), F32), ((width, count), BF16)],
-        (base, side, side2, queries, pos, st1, mix1, ch1),
-        [((2 * n, count), F32), ((2 * n, count), BF16), ((n, width), BF16), pltpu.SemaphoreType.DMA],
-        6 * flops,
-        hbm_in=(1,),
     )
     out, loss = call(
         functools.partial(scale_kernel, scale), [((width, count), BF16), ((1, count), F32)], (every, st, m, ch)

time: 111 us -> 108 us (0.973)
  local copies, waits for them, and re-layouts: 3 us -> 0.1 us
  waiting for transfers between devices: 27.2 us -> 28.8 us
  blocking collectives: 32.1 us -> 30.6 us
    unnamed x12 -> x8, local copies, waits for them, and re-layouts: 2.91 us -> 0.02 us
    all_to_all x1, waiting for transfers between devices: 0.01 us -> 1.57 us  [shards(): lax.all_to_all(stats, ('yl', *OUTER), split_axis=0, concat_axis=0, tiled=...]
    all_to_all x1, blocking collectives: 32.1 us -> 30.6 us  [shards(): got = lax.all_to_all(out, OUTER, split_axis=0, concat_axis=0, tiled=True)]
  transfers between devices with their start and end apart: 7 -> 7, of which waited for: 3 -> 4; matrix products, arithmetic and copies ran while one was open for 0% -> 0% of each run, Pallas kernels for 11% -> 11%
where the time goes in v7:
time: 108 us; the launch traced here: 107 us
  starting transfers between devices  32.2 us (30%)
  blocking collectives  30.6 us (28%)
  waiting for transfers between devices  28.8 us (27%)
  Pallas kernels  14.9 us (14%)
    all_to_all x1, blocking collectives, shards(): got = lax.all_to_all(out, OUTER, split_axis=0, concat_axis=0, tiled=True)  30.6 us
    ppermute x3, waiting for transfers between devices, to_sides(): return lax.ppermute(x, LANE, perm)  18 us
    pallas_call x6, Pallas kernels, call(): return kernel(*operands)  14.9 us
    all_to_all x1, starting transfers between devices, shards(): lax.all_to_all(copies, 'z', split_axis=0, concat_axis=0, tiled=True)  10.3 us
    all_to_all x1, starting transfers between devices, shards(): lax.all_to_all(stats, ('yl', *OUTER), split_axis=0, concat_axis=0, tiled=...  10.1 us
    all_to_all x1, waiting for transfers between devices, shards(): lax.all_to_all(copies, 'z', split_axis=0, concat_axis=0, tiled=True)  9.2 us
    ppermute x3, starting transfers between devices, to_sides(): return lax.ppermute(x, LANE, perm)  7.06 us
    ppermute x2, starting transfers between devices, swapped(): return lax.ppermute(x, 'c', [(0, 1), (1, 0)])  4.68 us
  transfers between devices with their start and end apart: 7, of which 4 were waited for; matrix products, arithmetic and copies ran while one was open for 0% of the time, Pallas kernels for 11%

profile of v7, /device:TPU:16, one launch (start us, length us, event | category | flops | bytes accessed | tf_op | source)
XLA Modules:
  0.0 107.4 jit_solution(17989433645316802551)
XLA Ops:
  0.6 0.0 copy-start
  0.6 0.0 copy-start.3
  0.7 1.9 %shard_map.50 = bf16[8,64,768]{2,1,0:T(8,128)(2,1)} custom-call(bf16[64,768]{1,0:T(8,128)(2,1)} %x_hbm.1), custom_call_target="tpu_custom_call" | custom-call | bytes 4194304 | tf_op jit(solution)/shard_map/pallas_call | solution.py:169
  2.6 10.3 %all-to-all-start = ((bf16[8,64,768]{2,1,0:T(8,128)(2,1)}), bf16[8,64,768]{2,1,0:T(8,128)(2,1)S(1)}, u32[]{:S(2)}, u32[]{:S(2)}) async-start(bf16[8,64,768]{2,1,0:T(8,128)(2,1)} %shard_map.50), calls=%async_computation | async-start | bytes 1572864 | tf_op jit(solution)/shard_map/all_to_all | solution.py:202
  12.9 0.0 copy-done
  12.9 2.4 %collective-permute-start = (bf16[512,768]{1,0:T(8,128)(2,1)S(1)}, bf16[512,768]{1,0:T(8,128)(2,1)S(1)}, u32[]{:S(2)}, u32[]{:S(2)}) collective-permute-start(bf16[512,768]{1,0:T(8,128)(2,1)S(1)} %copy-done), channel_id=1, source_target_pairs={{0,386},{1,3},{2,0},{3,129},{128,2},{129,131},{130,128},{131,257},... | collective-permute-start | bytes 2359304 | tf_op jit(solution)/shard_map/ppermute | solution.py:32
  15.3 0.0 copy-done.3
  15.3 2.4 %collective-permute-start.1 = (s32[1,512]{1,0:T(1,128)S(1)}, s32[1,512]{1,0:T(1,128)S(1)}, u32[]{:S(2)}, u32[]{:S(2)}) collective-permute-start(s32[1,512]{1,0:T(1,128)S(1)} %bitcast.15), channel_id=1, source_target_pairs={{0,386},{1,3},{2,0},{3,129},{128,2},{129,131},{130,128},{131,257},... | collective-permute-start | bytes 6152 | tf_op jit(solution)/shard_map/ppermute | solution.py:32
  17.7 9.2 %collective-permute-done.1.posf_ref = s32[1,512]{1,0:T(1,128)S(1)} collective-permute-done((s32[1,512]{1,0:T(1,128)S(1)}, s32[1,512]{1,0:T(1,128)S(1)}, u32[]{:S(2)}, u32[]{:S(2)}) %collective-permute-start.1) | collective-permute-done | bytes 2080 | tf_op jit(solution)/shard_map/ppermute | solution.py:32
  26.8 0.0 collective-permute-done.qf_ref
  26.8 9.2 %all-to-all-done = bf16[8,64,768]{2,1,0:T(8,128)(2,1)S(1)} async-done(((bf16[8,64,768]{2,1,0:T(8,128)(2,1)}), bf16[8,64,768]{2,1,0:T(8,128)(2,1)S(1)}, u32[]{:S(2)}, u32[]{:S(2)}) %all-to-all-start) | async-done | bytes 786464 | tf_op jit(solution)/shard_map/all_to_all | solution.py:202
  36.0 0.0 copy-start.1
  36.0 2.3 %collective-permute-start.3 = (bf16[512,768]{1,0:T(8,128)(2,1)S(1)}, bf16[512,768]{1,0:T(8,128)(2,1)}, u32[]{:S(2)}, u32[]{:S(2)}) collective-permute-start(bf16[512,768]{1,0:T(8,128)(2,1)S(1)} %bitcast.10), channel_id=1, source_target_pairs={{0,386},{1,3},{2,0},{3,129},{128,2},{129,131},{130,128},{131,257},... | collective-permute-start | bytes 2359304 | tf_op jit(solution)/shard_map/ppermute | solution.py:32
  38.4 2.8 %collective-permute-start.2 = (bf16[512,768]{1,0:T(8,128)(2,1)S(1)}, bf16[512,768]{1,0:T(8,128)(2,1)S(1)}, u32[]{:S(2)}, u32[]{:S(2)}) collective-permute-start(bf16[512,768]{1,0:T(8,128)(2,1)S(1)} %bitcast.11), channel_id=1, source_target_pairs={{0,1},{1,0},{2,3},{3,2},{4,5},{5,4},{6,7},{7,6},{8,9},{9,8},{10,11... | collective-permute-start | bytes 2359304 | tf_op jit(solution)/shard_map/ppermute | solution.py:24
  41.2 8.8 %collective-permute-done.3.refs_1_ = bf16[512,768]{1,0:T(8,128)(2,1)} collective-permute-done((bf16[512,768]{1,0:T(8,128)(2,1)S(1)}, bf16[512,768]{1,0:T(8,128)(2,1)}, u32[]{:S(2)}, u32[]{:S(2)}) %collective-permute-start.3) | collective-permute-done | bytes 786464 | tf_op jit(solution)/shard_map/ppermute | solution.py:32
  50.0 1.9 %collective-permute-start.4 = (bf16[512,768]{1,0:T(8,128)(2,1)}, bf16[512,768]{1,0:T(8,128)(2,1)}, u32[]{:S(2)}, u32[]{:S(2)}) collective-permute-start(bf16[512,768]{1,0:T(8,128)(2,1)} %collective-permute-done.3.refs_1_), channel_id=1, source_target_pairs={{0,1},{1,0},{2,3},{3,2},{4,5},{5,4},{6,7},{7,6},{8,9},{9,8},{10,11... | collective-permute-start | bytes 2359304 | tf_op jit(solution)/shard_map/ppermute | solution.py:24
  52.0 0.1 stack.23.base_ref
  52.1 0.0 collective-permute-done.2.b_ref.b_hbm
  52.1 0.0 copy-start.2
  52.1 3.8 %shard_map.51 = (f32[8,512]{1,0:T(8,128)S(1)}, bf16[1024,512]{1,0:T(8,128)(2,1)}, f32[32,1,1024]{2,1,0:T(1,128)}) custom-call(s32[5]{0:T(128)S(1)} %stack.23.base_ref, bf16[512,768]{1,0:T(8,128)(2,1)S(1)} %bitcast.12, bf16[512,768]{1,0:T(8,128)(2,1)S(1)} %collective-permute-done.2.b_ref.b_hbm, bf16[512,768]{1,0:T(8,128)(2,1)S(1)} %copy-done, ...), custom_call_target="tpu_custom_call" | custom-call | flops 1610612736 | bytes 4194304 | tf_op jit(solution)/shard_map/pallas_call | solution.py:169
  55.8 0.0 copy-done.1
  55.8 0.0 copy-done.2
  55.8 10.1 %all-to-all-start.1 = ((f32[32,1,1024]{2,1,0:T(1,128)}), f32[32,1,1024]{2,1,0:T(1,128)S(1)}, u32[]{:S(2)}, u32[]{:S(2)}) async-start(f32[32,1,1024]{2,1,0:T(1,128)} %get-tuple-element.18), calls=%async_computation.1 | async-start | bytes 262144 | tf_op jit(solution)/shard_map/all_to_all | solution.py:216
  66.0 1.4 %shard_map.52 = (bf16[512,768]{1,0:T(8,128)(2,1)S(1)}, bf16[512,768]{1,0:T(8,128)(2,1)S(1)}) custom-call(bf16[512,768]{1,0:T(8,128)(2,1)} %refs_0_.1, bf16[512,768]{1,0:T(8,128)(2,1)} %collective-permute-done.3.refs_1_), custom_call_target="tpu_custom_call" | custom-call | bytes 4194304 | tf_op jit(solution)/shard_map/pallas_call | solution.py:169
  67.4 0.0 collective-permute-done.4.side2_ref
  67.4 6.5 %shard_map.53 = (f32[8,512]{1,0:T(8,128)S(1)}, f32[768,512]{1,0:T(8,128)S(1)}, bf16[768,512]{1,0:T(8,128)(2,1)S(1)}) custom-call(s32[5]{0:T(128)S(1)} %stack.23.base_ref, bf16[512,768]{1,0:T(8,128)(2,1)} %bitcast.13, bf16[512,768]{1,0:T(8,128)(2,1)} %copy-done.2, bf16[1024,512]{1,0:T(8,128)(2,1)} %get-tuple-element.19.wo_hbm, ...), custom_call_target="tpu_custom_call" | custom-call | flops 4026531840 | bytes 4194304 | tf_op jit(solution)/shard_map/pallas_call | solution.py:169
  73.9 1.6 %all-to-all-done.1.every_ref = f32[32,1,1024]{2,1,0:T(1,128)S(1)} async-done(((f32[32,1,1024]{2,1,0:T(1,128)}), f32[32,1,1024]{2,1,0:T(1,128)S(1)}, u32[]{:S(2)}, u32[]{:S(2)}) %all-to-all-start.1) | async-done | bytes 131104 | tf_op jit(solution)/shard_map/all_to_all | solution.py:216
  75.5 0.6 shard_map.54
  76.1 30.6 %all_to_all.15.got_ref = bf16[16,48,512]{2,1,0:T(8,128)(2,1)S(1)} all-to-all(bf16[16,48,512]{2,1,0:T(8,128)(2,1)S(1)} %bitcast.14), channel_id=1, replica_groups=mesh['yh'=4,'x'=4,'z'=8,'yl'=2,'c'=2] {'yh','x'}, dimensions={0} | all-to-all | bytes 1572864 | tf_op jit(solution)/shard_map/all_to_all | solution.py:247
  106.6 0.7 shard_map.55
Async XLA Ops:
  0.6 12.3 %copy-start = (bf16[512,768]{1,0:T(8,128)(2,1)S(1)}, bf16[512,768]{1,0:T(8,128)(2,1)}, u32[]{:S(2)}) copy-start(bf16[512,768]{1,0:T(8,128)(2,1)} %refs_0_.1) | copy-start | bytes 2359300
  0.6 14.7 %copy-start.3 = (s32[512]{0:T(512)S(1)}, s32[512]{0:T(512)}, u32[]{:S(2)}) copy-start(s32[512]{0:T(512)} %param.5) | copy-start | bytes 6148
  2.6 33.4 %all-to-all-start = ((bf16[8,64,768]{2,1,0:T(8,128)(2,1)}), bf16[8,64,768]{2,1,0:T(8,128)(2,1)S(1)}, u32[]{:S(2)}, u32[]{:S(2)}) async-start(bf16[8,64,768]{2,1,0:T(8,128)(2,1)} %shard_map.50), calls=%async_computation | async-start | bytes 1572864 | tf_op jit(solution)/shard_map/all_to_all | solution.py:202
  12.9 13.9 %collective-permute-start = (bf16[512,768]{1,0:T(8,128)(2,1)S(1)}, bf16[512,768]{1,0:T(8,128)(2,1)S(1)}, u32[]{:S(2)}, u32[]{:S(2)}) collective-permute-start(bf16[512,768]{1,0:T(8,128)(2,1)S(1)} %copy-done), channel_id=1, source_target_pairs={{0,386},{1,3},{2,0},{3,129},{128,2},{129,131},{130,128},{131,257},... | collective-permute-start | bytes 2359304 | tf_op jit(solution)/shard_map/ppermute | solution.py:32
  15.3 11.5 %collective-permute-start.1 = (s32[1,512]{1,0:T(1,128)S(1)}, s32[1,512]{1,0:T(1,128)S(1)}, u32[]{:S(2)}, u32[]{:S(2)}) collective-permute-start(s32[1,512]{1,0:T(1,128)S(1)} %bitcast.15), channel_id=1, source_target_pairs={{0,386},{1,3},{2,0},{3,129},{128,2},{129,131},{130,128},{131,257},... | collective-permute-start | bytes 6152 | tf_op jit(solution)/shard_map/ppermute | solution.py:32
  36.0 19.8 %copy-start.1 = (bf16[8,64,768]{2,1,0:T(8,128)(2,1)}, bf16[8,64,768]{2,1,0:T(8,128)(2,1)S(1)}, u32[]{:S(2)}) copy-start(bf16[8,64,768]{2,1,0:T(8,128)(2,1)S(1)} %all-to-all-done) | copy-start | bytes 2359300
  36.0 14.0 %collective-permute-start.3 = (bf16[512,768]{1,0:T(8,128)(2,1)S(1)}, bf16[512,768]{1,0:T(8,128)(2,1)}, u32[]{:S(2)}, u32[]{:S(2)}) collective-permute-start(bf16[512,768]{1,0:T(8,128)(2,1)S(1)} %bitcast.10), channel_id=1, source_target_pairs={{0,386},{1,3},{2,0},{3,129},{128,2},{129,131},{130,128},{131,257},... | collective-permute-start | bytes 2359304 | tf_op jit(solution)/shard_map/ppermute | solution.py:32
  38.4 13.7 %collective-permute-start.2 = (bf16[512,768]{1,0:T(8,128)(2,1)S(1)}, bf16[512,768]{1,0:T(8,128)(2,1)S(1)}, u32[]{:S(2)}, u32[]{:S(2)}) collective-permute-start(bf16[512,768]{1,0:T(8,128)(2,1)S(1)} %bitcast.11), channel_id=1, source_target_pairs={{0,1},{1,0},{2,3},{3,2},{4,5},{5,4},{6,7},{7,6},{8,9},{9,8},{10,11... | collective-permute-start | bytes 2359304 | tf_op jit(solution)/shard_map/ppermute | solution.py:24
  50.0 17.4 %collective-permute-start.4 = (bf16[512,768]{1,0:T(8,128)(2,1)}, bf16[512,768]{1,0:T(8,128)(2,1)}, u32[]{:S(2)}, u32[]{:S(2)}) collective-permute-start(bf16[512,768]{1,0:T(8,128)(2,1)} %collective-permute-done.3.refs_1_), channel_id=1, source_target_pairs={{0,1},{1,0},{2,3},{3,2},{4,5},{5,4},{6,7},{7,6},{8,9},{9,8},{10,11... | collective-permute-start | bytes 2359304 | tf_op jit(solution)/shard_map/ppermute | solution.py:24
  52.1 3.8 %copy-start.2 = (bf16[512,768]{1,0:T(8,128)(2,1)}, bf16[512,768]{1,0:T(8,128)(2,1)S(1)}, u32[]{:S(2)}) copy-start(bf16[512,768]{1,0:T(8,128)(2,1)S(1)} %collective-permute-done.2.b_ref.b_hbm) | copy-start | bytes 2359300
  55.8 19.6 %all-to-all-start.1 = ((f32[32,1,1024]{2,1,0:T(1,128)}), f32[32,1,1024]{2,1,0:T(1,128)S(1)}, u32[]{:S(2)}, u32[]{:S(2)}) async-start(f32[32,1,1024]{2,1,0:T(1,128)} %get-tuple-element.18), calls=%async_computation.1 | async-start | bytes 262144 | tf_op jit(solution)/shard_map/all_to_all | solution.py:216

commit v8 on v7

--- a/solution.py
+++ b/solution.py
@@ -127,7 +127,13 @@
     whole = most + jnp.log(jnp.sum(jnp.exp(lse - most), axis=0, keepdims=True))
     ps = jnp.sum(every_ref[:, 0, count:], axis=0, keepdims=True)
     g = jnp.exp(st_ref[0:1, :] * scale - whole)
-    out_ref[...] = (m_ref[...] * g - c_ref[...].astype(F32)).astype(BF16)
+    out = (m_ref[...] * g - c_ref[...].astype(F32)).astype(BF16)
+    nx, width, _ = out_ref.shape
+    piece = width // 4
+    for i in range(nx):
+        for j in range(4):
+            at = (j * nx + i) * piece
+            out_ref[i, j * piece : (j + 1) * piece, :] = out[at : at + piece]
     loss_ref[...] = whole - ps
 
 
@@ -143,11 +149,11 @@
         copy.wait()
 
 
-def final_kernel(scale, got_ref, grad_ref):
+def sum_kernel(scale, got_ref, out_ref):
     total = got_ref[0].astype(F32)
     for i in range(1, got_ref.shape[0]):
         total += got_ref[i].astype(F32)
-    grad_ref[...] = (scale * total).astype(BF16)
+    out_ref[...] = (scale * total).astype(BF16)
 
 
 def call(body, out, operands, scratch=(), flops=0, vmem=12, hbm_in=(), hbm_out=()):
@@ -240,12 +246,17 @@
         hbm_in=(1, 2, 3),
     )
     out, loss = call(
-        functools.partial(scale_kernel, scale), [((width, count), BF16), ((1, count), F32)], (every, st, m, ch)
-    )
-    n_outer = members // 2
-    out = out.reshape(n_outer, width // n_outer, count)
-    got = lax.all_to_all(out, OUTER, split_axis=0, concat_axis=0, tiled=True)
-    (grad,) = call(functools.partial(final_kernel, scale), [((width // n_outer, count), BF16)], (got,))
+        functools.partial(scale_kernel, scale),
+        [((nx, width // nx, count), BF16), ((1, count), F32)],
+        (every, st, m, ch),
+    )
+    got = lax.all_to_all(out, "x", split_axis=0, concat_axis=0, tiled=True)
+    (out,) = call(functools.partial(sum_kernel, 1.0), [((width // nx, count), BF16)], (got,))
+    nyh = ny // 2
+    piece = width // nx // nyh
+    out = out.reshape(nyh, piece, count)
+    got = lax.all_to_all(out, "yh", split_axis=0, concat_axis=0, tiled=True)
+    (grad,) = call(functools.partial(sum_kernel, scale), [((piece, count), BF16)], (got,))
     return grad.T, loss.reshape(count)
 
 

time: 108 us -> 107 us (level)
  the two profiles are of different devices: /device:TPU:16 before, /device:TPU:8 now
where the time goes in v8:
time: 107 us
  starting transfers between devices  35.3 us (33%)
  blocking collectives  29.1 us (27%)
  waiting for transfers between devices  26.5 us (25%)
  Pallas kernels  15 us (14%)
    ppermute x3, waiting for transfers between devices, to_sides(): return lax.ppermute(x, LANE, perm)  15 us
    pallas_call x7, Pallas kernels, call(): return kernel(*operands)  15 us
    all_to_all x1, blocking collectives, shards(): got = lax.all_to_all(out, 'yh', split_axis=0, concat_axis=0, tiled=True)  14.9 us
    all_to_all x1, blocking collectives, shards(): got = lax.all_to_all(out, 'x', split_axis=0, concat_axis=0, tiled=True)  14.2 us
    all_to_all x1, starting transfers between devices, shards(): lax.all_to_all(copies, 'z', split_axis=0, concat_axis=0, tiled=True)  10.3 us
    all_to_all x1, starting transfers between devices, shards(): lax.all_to_all(stats, ('yl', *OUTER), split_axis=0, concat_axis=0, tiled=...  10.2 us
    ppermute x3, starting transfers between devices, to_sides(): return lax.ppermute(x, LANE, perm)  10.1 us
    all_to_all x1, waiting for transfers between devices, shards(): lax.all_to_all(copies, 'z', split_axis=0, concat_axis=0, tiled=True)  9.2 us
  transfers between devices with their start and end apart: 7, of which 4 were waited for; matrix products, arithmetic and copies ran while one was open for 0% of the time, Pallas kernels for 11%

profile of v8, /device:TPU:8, one launch (start us, length us, event | category | flops | bytes accessed | tf_op | source)
XLA Modules:
  0.0 106.8 jit_solution(2061420613225504211)
XLA Ops:
  0.6 0.0 copy-start
  0.6 0.0 copy-start.3
  0.7 1.9 %shard_map.50 = bf16[8,64,768]{2,1,0:T(8,128)(2,1)} custom-call(bf16[64,768]{1,0:T(8,128)(2,1)} %x_hbm.1), custom_call_target="tpu_custom_call" | custom-call | bytes 4194304 | tf_op jit(solution)/shard_map/pallas_call | solution.py:175
  2.6 10.3 %all-to-all-start = ((bf16[8,64,768]{2,1,0:T(8,128)(2,1)}), bf16[8,64,768]{2,1,0:T(8,128)(2,1)S(1)}, u32[]{:S(2)}, u32[]{:S(2)}) async-start(bf16[8,64,768]{2,1,0:T(8,128)(2,1)} %shard_map.50), calls=%async_computation | async-start | bytes 1572864 | tf_op jit(solution)/shard_map/all_to_all | solution.py:208
  12.9 0.0 copy-done
  12.9 2.4 %collective-permute-start = (bf16[512,768]{1,0:T(8,128)(2,1)S(1)}, bf16[512,768]{1,0:T(8,128)(2,1)S(1)}, u32[]{:S(2)}, u32[]{:S(2)}) collective-permute-start(bf16[512,768]{1,0:T(8,128)(2,1)S(1)} %copy-done), channel_id=1, source_target_pairs={{0,386},{1,3},{2,0},{3,129},{128,2},{129,131},{130,128},{131,257},... | collective-permute-start | bytes 2359304 | tf_op jit(solution)/shard_map/ppermute | solution.py:32
  15.3 0.0 copy-done.3
  15.3 5.4 %collective-permute-start.1 = (s32[1,512]{1,0:T(1,128)S(1)}, s32[1,512]{1,0:T(1,128)S(1)}, u32[]{:S(2)}, u32[]{:S(2)}) collective-permute-start(s32[1,512]{1,0:T(1,128)S(1)} %bitcast.15), channel_id=1, source_target_pairs={{0,386},{1,3},{2,0},{3,129},{128,2},{129,131},{130,128},{131,257},... | collective-permute-start | bytes 6152 | tf_op jit(solution)/shard_map/ppermute | solution.py:32
  20.7 6.1 %collective-permute-done.1.posf_ref = s32[1,512]{1,0:T(1,128)S(1)} collective-permute-done((s32[1,512]{1,0:T(1,128)S(1)}, s32[1,512]{1,0:T(1,128)S(1)}, u32[]{:S(2)}, u32[]{:S(2)}) %collective-permute-start.1) | collective-permute-done | bytes 2080 | tf_op jit(solution)/shard_map/ppermute | solution.py:32
  26.8 0.0 collective-permute-done.qf_ref
  26.8 9.2 %all-to-all-done = bf16[8,64,768]{2,1,0:T(8,128)(2,1)S(1)} async-done(((bf16[8,64,768]{2,1,0:T(8,128)(2,1)}), bf16[8,64,768]{2,1,0:T(8,128)(2,1)S(1)}, u32[]{:S(2)}, u32[]{:S(2)}) %all-to-all-start) | async-done | bytes 786464 | tf_op jit(solution)/shard_map/all_to_all | solution.py:208
  36.0 0.0 copy-start.1
  36.0 2.3 %collective-permute-start.3 = (bf16[512,768]{1,0:T(8,128)(2,1)S(1)}, bf16[512,768]{1,0:T(8,128)(2,1)}, u32[]{:S(2)}, u32[]{:S(2)}) collective-permute-start(bf16[512,768]{1,0:T(8,128)(2,1)S(1)} %bitcast.10), channel_id=1, source_target_pairs={{0,386},{1,3},{2,0},{3,129},{128,2},{129,131},{130,128},{131,257},... | collective-permute-start | bytes 2359304 | tf_op jit(solution)/shard_map/ppermute | solution.py:32
  38.4 2.8 %collective-permute-start.2 = (bf16[512,768]{1,0:T(8,128)(2,1)S(1)}, bf16[512,768]{1,0:T(8,128)(2,1)S(1)}, u32[]{:S(2)}, u32[]{:S(2)}) collective-permute-start(bf16[512,768]{1,0:T(8,128)(2,1)S(1)} %bitcast.11), channel_id=1, source_target_pairs={{0,1},{1,0},{2,3},{3,2},{4,5},{5,4},{6,7},{7,6},{8,9},{9,8},{10,11... | collective-permute-start | bytes 2359304 | tf_op jit(solution)/shard_map/ppermute | solution.py:24
  41.2 8.8 %collective-permute-done.3.refs_1_ = bf16[512,768]{1,0:T(8,128)(2,1)} collective-permute-done((bf16[512,768]{1,0:T(8,128)(2,1)S(1)}, bf16[512,768]{1,0:T(8,128)(2,1)}, u32[]{:S(2)}, u32[]{:S(2)}) %collective-permute-start.3) | collective-permute-done | bytes 786464 | tf_op jit(solution)/shard_map/ppermute | solution.py:32
  50.0 1.9 %collective-permute-start.4 = (bf16[512,768]{1,0:T(8,128)(2,1)}, bf16[512,768]{1,0:T(8,128)(2,1)}, u32[]{:S(2)}, u32[]{:S(2)}) collective-permute-start(bf16[512,768]{1,0:T(8,128)(2,1)} %collective-permute-done.3.refs_1_), channel_id=1, source_target_pairs={{0,1},{1,0},{2,3},{3,2},{4,5},{5,4},{6,7},{7,6},{8,9},{9,8},{10,11... | collective-permute-start | bytes 2359304 | tf_op jit(solution)/shard_map/ppermute | solution.py:24
  52.0 0.1 stack.23.base_ref
  52.1 0.0 collective-permute-done.2.b_ref.b_hbm
  52.1 0.0 copy-start.2
  52.1 3.8 %shard_map.51 = (f32[8,512]{1,0:T(8,128)S(1)}, bf16[1024,512]{1,0:T(8,128)(2,1)}, f32[32,1,1024]{2,1,0:T(1,128)}) custom-call(s32[5]{0:T(128)S(1)} %stack.23.base_ref, bf16[512,768]{1,0:T(8,128)(2,1)S(1)} %bitcast.12, bf16[512,768]{1,0:T(8,128)(2,1)S(1)} %collective-permute-done.2.b_ref.b_hbm, bf16[512,768]{1,0:T(8,128)(2,1)S(1)} %copy-done, ...), custom_call_target="tpu_custom_call" | custom-call | flops 1610612736 | bytes 4194304 | tf_op jit(solution)/shard_map/pallas_call | solution.py:175
  55.8 0.0 copy-done.1
  55.8 0.0 copy-done.2
  55.8 10.2 %all-to-all-start.1 = ((f32[32,1,1024]{2,1,0:T(1,128)}), f32[32,1,1024]{2,1,0:T(1,128)S(1)}, u32[]{:S(2)}, u32[]{:S(2)}) async-start(f32[32,1,1024]{2,1,0:T(1,128)} %get-tuple-element.18), calls=%async_computation.1 | async-start | bytes 262144 | tf_op jit(solution)/shard_map/all_to_all | solution.py:222
  66.1 1.4 %shard_map.52 = (bf16[512,768]{1,0:T(8,128)(2,1)S(1)}, bf16[512,768]{1,0:T(8,128)(2,1)S(1)}) custom-call(bf16[512,768]{1,0:T(8,128)(2,1)} %refs_0_.1, bf16[512,768]{1,0:T(8,128)(2,1)} %collective-permute-done.3.refs_1_), custom_call_target="tpu_custom_call" | custom-call | bytes 4194304 | tf_op jit(solution)/shard_map/pallas_call | solution.py:175
  67.5 0.0 collective-permute-done.4.side2_ref
  67.5 6.5 %shard_map.53 = (f32[8,512]{1,0:T(8,128)S(1)}, f32[768,512]{1,0:T(8,128)S(1)}, bf16[768,512]{1,0:T(8,128)(2,1)S(1)}) custom-call(s32[5]{0:T(128)S(1)} %stack.23.base_ref, bf16[512,768]{1,0:T(8,128)(2,1)} %bitcast.13, bf16[512,768]{1,0:T(8,128)(2,1)} %copy-done.2, bf16[1024,512]{1,0:T(8,128)(2,1)} %get-tuple-element.19.wo_hbm, ...), custom_call_target="tpu_custom_call" | custom-call | flops 4026531840 | bytes 4194304 | tf_op jit(solution)/shard_map/pallas_call | solution.py:175
  74.0 2.3 %all-to-all-done.1.every_ref = f32[32,1,1024]{2,1,0:T(1,128)S(1)} async-done(((f32[32,1,1024]{2,1,0:T(1,128)}), f32[32,1,1024]{2,1,0:T(1,128)S(1)}, u32[]{:S(2)}, u32[]{:S(2)}) %all-to-all-start.1) | async-done | bytes 131104 | tf_op jit(solution)/shard_map/all_to_all | solution.py:222
  76.3 0.6 shard_map.54
  77.0 14.2 %all_to_all.20.got_ref = bf16[4,192,512]{2,1,0:T(8,128)(2,1)S(1)} all-to-all(bf16[4,192,512]{2,1,0:T(8,128)(2,1)S(1)} %get-tuple-element.26), channel_id=1, replica_groups=mesh['yh'=4,'x'=4,'z'=8,'yl'=2,'c'=2] {'x'}, dimensions={0} | all-to-all | bytes 1572864 | tf_op jit(solution)/shard_map/all_to_all | solution.py:253
  91.1 0.1 shard_map.55
  91.2 14.9 %all_to_all.21.got_ref = bf16[4,48,512]{2,1,0:T(8,128)(2,1)S(1)} all-to-all(bf16[4,48,512]{2,1,0:T(8,128)(2,1)S(1)} %bitcast.14), channel_id=1, replica_groups=mesh['yh'=4,'x'=4,'z'=8,'yl'=2,'c'=2] {'yh'}, dimensions={0} | all-to-all | bytes 393216 | tf_op jit(solution)/shard_map/all_to_all | solution.py:258
  106.2 0.7 shard_map.56
Async XLA Ops:
  0.6 12.3 %copy-start = (bf16[512,768]{1,0:T(8,128)(2,1)S(1)}, bf16[512,768]{1,0:T(8,128)(2,1)}, u32[]{:S(2)}) copy-start(bf16[512,768]{1,0:T(8,128)(2,1)} %refs_0_.1) | copy-start | bytes 2359300
  0.6 14.7 %copy-start.3 = (s32[512]{0:T(512)S(1)}, s32[512]{0:T(512)}, u32[]{:S(2)}) copy-start(s32[512]{0:T(512)} %param.5) | copy-start | bytes 6148
  2.6 33.4 %all-to-all-start = ((bf16[8,64,768]{2,1,0:T(8,128)(2,1)}), bf16[8,64,768]{2,1,0:T(8,128)(2,1)S(1)}, u32[]{:S(2)}, u32[]{:S(2)}) async-start(bf16[8,64,768]{2,1,0:T(8,128)(2,1)} %shard_map.50), calls=%async_computation | async-start | bytes 1572864 | tf_op jit(solution)/shard_map/all_to_all | solution.py:208
  12.9 13.9 %collective-permute-start = (bf16[512,768]{1,0:T(8,128)(2,1)S(1)}, bf16[512,768]{1,0:T(8,128)(2,1)S(1)}, u32[]{:S(2)}, u32[]{:S(2)}) collective-permute-start(bf16[512,768]{1,0:T(8,128)(2,1)S(1)} %copy-done), channel_id=1, source_target_pairs={{0,386},{1,3},{2,0},{3,129},{128,2},{129,131},{130,128},{131,257},... | collective-permute-start | bytes 2359304 | tf_op jit(solution)/shard_map/ppermute | solution.py:32
  15.3 11.5 %collective-permute-start.1 = (s32[1,512]{1,0:T(1,128)S(1)}, s32[1,512]{1,0:T(1,128)S(1)}, u32[]{:S(2)}, u32[]{:S(2)}) collective-permute-start(s32[1,512]{1,0:T(1,128)S(1)} %bitcast.15), channel_id=1, source_target_pairs={{0,386},{1,3},{2,0},{3,129},{128,2},{129,131},{130,128},{131,257},... | collective-permute-start | bytes 6152 | tf_op jit(solution)/shard_map/ppermute | solution.py:32
  36.0 19.8 %copy-start.1 = (bf16[8,64,768]{2,1,0:T(8,128)(2,1)}, bf16[8,64,768]{2,1,0:T(8,128)(2,1)S(1)}, u32[]{:S(2)}) copy-start(bf16[8,64,768]{2,1,0:T(8,128)(2,1)S(1)} %all-to-all-done) | copy-start | bytes 2359300
  36.0 14.0 %collective-permute-start.3 = (bf16[512,768]{1,0:T(8,128)(2,1)S(1)}, bf16[512,768]{1,0:T(8,128)(2,1)}, u32[]{:S(2)}, u32[]{:S(2)}) collective-permute-start(bf16[512,768]{1,0:T(8,128)(2,1)S(1)} %bitcast.10), channel_id=1, source_target_pairs={{0,386},{1,3},{2,0},{3,129},{128,2},{129,131},{130,128},{131,257},... | collective-permute-start | bytes 2359304 | tf_op jit(solution)/shard_map/ppermute | solution.py:32
  38.4 13.7 %collective-permute-start.2 = (bf16[512,768]{1,0:T(8,128)(2,1)S(1)}, bf16[512,768]{1,0:T(8,128)(2,1)S(1)}, u32[]{:S(2)}, u32[]{:S(2)}) collective-permute-start(bf16[512,768]{1,0:T(8,128)(2,1)S(1)} %bitcast.11), channel_id=1, source_target_pairs={{0,1},{1,0},{2,3},{3,2},{4,5},{5,4},{6,7},{7,6},{8,9},{9,8},{10,11... | collective-permute-start | bytes 2359304 | tf_op jit(solution)/shard_map/ppermute | solution.py:24
  50.0 17.5 %collective-permute-start.4 = (bf16[512,768]{1,0:T(8,128)(2,1)}, bf16[512,768]{1,0:T(8,128)(2,1)}, u32[]{:S(2)}, u32[]{:S(2)}) collective-permute-start(bf16[512,768]{1,0:T(8,128)(2,1)} %collective-permute-done.3.refs_1_), channel_id=1, source_target_pairs={{0,1},{1,0},{2,3},{3,2},{4,5},{5,4},{6,7},{7,6},{8,9},{9,8},{10,11... | collective-permute-start | bytes 2359304 | tf_op jit(solution)/shard_map/ppermute | solution.py:24
  52.1 3.8 %copy-start.2 = (bf16[512,768]{1,0:T(8,128)(2,1)}, bf16[512,768]{1,0:T(8,128)(2,1)S(1)}, u32[]{:S(2)}) copy-start(bf16[512,768]{1,0:T(8,128)(2,1)S(1)} %collective-permute-done.2.b_ref.b_hbm) | copy-start | bytes 2359300
  55.8 20.5 %all-to-all-start.1 = ((f32[32,1,1024]{2,1,0:T(1,128)}), f32[32,1,1024]{2,1,0:T(1,128)S(1)}, u32[]{:S(2)}, u32[]{:S(2)}) async-start(f32[32,1,1024]{2,1,0:T(1,128)} %get-tuple-element.18), calls=%async_computation.1 | async-start | bytes 262144 | tf_op jit(solution)/shard_map/all_to_all | solution.py:222

commit v9 on v8

--- a/solution.py
+++ b/solution.py
@@ -39,21 +39,6 @@
 def hits_of(pos_ref, base, count, rows):
     j = lax.broadcasted_iota(jnp.int32, (count, 1), 0)
     return (j // rows) * (4 * rows) + j % rows == pos_ref[...] - base
-
-
-def statistics(p_refs, bases, q_ref, pos_ref, s_ref, rows):
-    q = q_ref[...]
-    top = ps = None
-    for i, p_ref in enumerate(p_refs):
-        n = p_ref.shape[0]
-        s = dot(p_ref[...], q, ((1,), (1,)))
-        s_ref[i * n : (i + 1) * n, :] = s
-        hit = hits_of(pos_ref, bases[i], n, rows)
-        t = jnp.max(s, axis=0, keepdims=True)
-        u = jnp.sum(jnp.where(hit, s, 0.0), axis=0, keepdims=True)
-        top = t if top is None else jnp.maximum(top, t)
-        ps = u if ps is None else ps + u
-    return top, ps
 
 
 def products(p_refs, bases, w_ref, pos_ref, rows):
@@ -67,19 +52,41 @@
     return mix, chosen
 
 
-def stat_kernel(scale, rows, base_ref, a_ref, b_ref, q_ref, pos_ref, qf_ref, posf_ref, st_ref, w_hbm, out_ref, s_ref, w_ref, sem):
-    bases = (base_ref[0], base_ref[1])
+def half_statistics(scale, rows, base, p_ref, q_ref, pos_ref, s_ref):
+    s_ref[...] = dot(p_ref[...], q_ref[...], ((1,), (1,)))
+    hit = hits_of(pos_ref, base, p_ref.shape[0], rows)
+    top = jnp.max(s_ref[...], axis=0, keepdims=True)
+    ps = jnp.sum(jnp.where(hit, s_ref[...], 0.0), axis=0, keepdims=True)
+    e = jnp.exp2((s_ref[...] - top) * (scale * LOG2E))
+    lse = top * scale + jnp.log(jnp.sum(e, axis=0, keepdims=True))
+    return top, e, lse, ps * scale
+
+
+def stata_kernel(scale, rows, base_ref, a_ref, q_ref, pos_ref, qf_ref, posf_ref, st_ref, w_hbm, s_ref, w_ref, sem):
+    top, e, lse, ps = half_statistics(scale, rows, base_ref[0], a_ref, q_ref, pos_ref, s_ref)
+    w_ref[...] = e.astype(BF16)
+    copy = pltpu.make_async_copy(w_ref, w_hbm, sem)
+    copy.start()
+    _, _, lse2, ps2 = half_statistics(scale, rows, base_ref[0], a_ref, qf_ref, posf_ref, s_ref)
+    for i, row in enumerate((top, lse, ps, lse2, ps2)):
+        st_ref[i : i + 1, :] = row
+    copy.wait()
+
+
+def statb_kernel(scale, rows, base_ref, b_ref, q_ref, pos_ref, qf_ref, posf_ref, st0_ref, st_ref, w_hbm, out_ref, s_ref, w_ref, sem):
     pieces = []
-    for qq, pp in ((q_ref, pos_ref), (qf_ref, posf_ref)):
-        top, ps = statistics((a_ref, b_ref), bases, qq, pp, s_ref, rows)
-        e = jnp.exp2((s_ref[...] - top) * (scale * LOG2E))
-        total = jnp.sum(e, axis=0, keepdims=True)
-        if not pieces:
+    for i, (qq, pp) in enumerate(((q_ref, pos_ref), (qf_ref, posf_ref))):
+        top, e, lse, ps = half_statistics(scale, rows, base_ref[1], b_ref, qq, pp, s_ref)
+        if i == 0:
             w_ref[...] = e.astype(BF16)
             copy = pltpu.make_async_copy(w_ref, w_hbm, sem)
             copy.start()
-            st_ref[0:1, :] = top
-        pieces.append(jnp.concatenate([top * scale + jnp.log(total), ps * scale], axis=1))
+            st_ref[0:1, :] = st0_ref[0:1, :]
+            st_ref[1:2, :] = top
+        lse0, ps0 = st0_ref[2 * i + 1 : 2 * i + 2, :], st0_ref[2 * i + 2 : 2 * i + 3, :]
+        most = jnp.maximum(lse, lse0)
+        lse = most + jnp.log(jnp.exp(lse - most) + jnp.exp(lse0 - most))
+        pieces.append(jnp.concatenate([lse, ps + ps0], axis=1))
     own, theirs = pieces
     lower = base_ref[4] == 0
     half = out_ref.shape[0] // 2
@@ -89,35 +96,39 @@
     copy.wait()
 
 
-def load_kernel(*refs):
-    count = (len(refs) - 1) // 2
-    copies = [pltpu.make_async_copy(refs[i], refs[count + i], refs[-1].at[i]) for i in range(count)]
+def side_kernel(q_hbm, side_hbm, q_ref, side_ref, s_ref, sems):
+    pairs = ((q_hbm, q_ref), (side_hbm, side_ref))
+    copies = [pltpu.make_async_copy(src, dst, sems.at[i]) for i, (src, dst) in enumerate(pairs)]
     for copy in copies:
         copy.start()
     for copy in copies:
         copy.wait()
-
-
-def mix_kernel(scale, rows, base_ref, a_hbm, b_hbm, wo_hbm, side_ref, side2_ref, q_ref, pos_ref, st0_ref, st_ref, m_ref, c_ref, s_ref, w_ref, a_ref, b_ref, wo_ref, sems):
-    pairs = ((a_hbm, a_ref), (b_hbm, b_ref), (wo_hbm, wo_ref))
+    s_ref[...] = dot(side_ref[...], q_ref[...], ((1,), (1,)))
+
+
+def mix_kernel(scale, rows, base_ref, a_hbm, b_hbm, wa_hbm, wb_hbm, side_ref, ss_ref, side2_ref, q_ref, pos_ref, st0_ref, st_ref, m_ref, c_ref, s_ref, w_ref, a_ref, b_ref, wa_ref, wb_ref, sems):
+    pairs = ((a_hbm, a_ref), (wa_hbm, wa_ref), (b_hbm, b_ref), (wb_hbm, wb_ref))
     copies = [pltpu.make_async_copy(src, dst, sems.at[i]) for i, (src, dst) in enumerate(pairs)]
     for copy in copies:
         copy.start()
-    q = q_ref[...]
     n = side2_ref.shape[0]
-    s_ref[:n, :] = dot(side2_ref[...], q, ((1,), (1,)))
-    s_ref[n:, :] = dot(side_ref[...], q, ((1,), (1,)))
-    top0 = st0_ref[0:1, :]
-    top = jnp.maximum(jnp.max(s_ref[...], axis=0, keepdims=True), top0)
-    w_ref[...] = jnp.exp2((s_ref[...] - top) * (scale * LOG2E)).astype(BF16)
+    k = scale * LOG2E
+    s_ref[...] = dot(side2_ref[...], q_ref[...], ((1,), (1,)))
+    tops = [st0_ref[0:1, :], st0_ref[1:2, :]]
+    top = jnp.maximum(jnp.max(s_ref[...], axis=0, keepdims=True), jnp.max(ss_ref[...], axis=0, keepdims=True))
+    top = jnp.maximum(top, jnp.maximum(*tops))
     st_ref[0:1, :] = top
+    w_ref[:n, :] = jnp.exp2((s_ref[...] - top) * k).astype(BF16)
+    w_ref[n:, :] = jnp.exp2((ss_ref[...] - top) * k).astype(BF16)
     mix, chosen = products((side2_ref, side_ref), (base_ref[3], base_ref[2]), w_ref, pos_ref, rows)
     m_ref[...] = mix
     for copy in copies:
         copy.wait()
-    mix, more = products((a_ref, b_ref), (base_ref[0], base_ref[1]), wo_ref, pos_ref, rows)
-    m_ref[...] += mix * jnp.exp2((top0 - top) * (scale * LOG2E))
-    c_ref[...] = (chosen + more).astype(BF16)
+    for p_ref, wo_ref, base, top0 in zip((a_ref, b_ref), (wa_ref, wb_ref), (base_ref[0], base_ref[1]), tops):
+        mix, more = products((p_ref,), (base,), wo_ref, pos_ref, rows)
+        m_ref[...] += mix * jnp.exp2((top0 - top) * k)
+        chosen += more
+    c_ref[...] = chosen.astype(BF16)
 
 
 def scale_kernel(scale, every_ref, st_ref, m_ref, c_ref, out_ref, loss_ref):
@@ -211,39 +222,50 @@
     side = to_sides(column, ny)
     column2 = swapped(column)
     members = ny * nx
-    st1, weights, stats = call(
-        functools.partial(stat_kernel, scale, rows),
-        [((8, count), F32), ((2 * n, count), BF16), ((members, 1, 2 * count), F32)],
-        (base, column, column2, queries, pos, theirs, pos_theirs),
-        [((2 * n, count), F32), ((2 * n, count), BF16), pltpu.SemaphoreType.DMA],
-        4 * flops,
+    scratch = [((n, count), F32), ((n, count), BF16), pltpu.SemaphoreType.DMA]
+    st0, wa = call(
+        functools.partial(stata_kernel, scale, rows),
+        [((8, count), F32), ((n, count), BF16)],
+        (base, column, queries, pos, theirs, pos_theirs),
+        scratch,
+        2 * flops,
+        hbm_out=(1,),
+    )
+    st1, wb, stats = call(
+        functools.partial(statb_kernel, scale, rows),
+        [((8, count), F32), ((n, count), BF16), ((members, 1, 2 * count), F32)],
+        (base, column2, queries, pos, theirs, pos_theirs, st0),
+        scratch,
+        2 * flops,
         hbm_out=(1,),
     )
     every = lax.all_to_all(stats, ("yl", *OUTER), split_axis=0, concat_axis=0, tiled=True)
     side2 = swapped(side)
-    queries, side = call(
-        load_kernel,
-        [(queries.shape, BF16), ((n, width), BF16)],
+    queries, side, scores = call(
+        side_kernel,
+        [(queries.shape, BF16), ((n, width), BF16), ((n, count), F32)],
         (queries, side),
         [pltpu.SemaphoreType.DMA((2,))],
-        vmem=4,
+        flops,
+        vmem=8,
         hbm_in=(0, 1),
     )
     st, m, ch = call(
         functools.partial(mix_kernel, scale, rows),
         [((8, count), F32), ((width, count), F32), ((width, count), BF16)],
-        (base, column, column2, weights, side, side2, queries, pos, st1),
+        (base, column, column2, wa, wb, side, scores, side2, queries, pos, st1),
         [
-            ((2 * n, count), F32),
+            ((n, count), F32),
             ((2 * n, count), BF16),
             ((n, width), BF16),
             ((n, width), BF16),
-            ((2 * n, count), BF16),
-            pltpu.SemaphoreType.DMA((3,)),
+            ((n, count), BF16),
+            ((n, count), BF16),
+            pltpu.SemaphoreType.DMA((4,)),
         ],
         10 * flops,
         vmem=24,
-        hbm_in=(1, 2, 3),
+        hbm_in=(1, 2, 3, 4),
     )
     out, loss = call(
         functools.partial(scale_kernel, scale),

time: 107 us -> 108 us (level)
    pallas_call x7 -> x8, Pallas kernels: 15 us -> 16 us  [call(): return kernel(*operands)]
  transfers between devices with their start and end apart: 7 -> 7, of which waited for: 4 -> 4; matrix products, arithmetic and copies ran while one was open for 0% -> 0% of each run, Pallas kernels for 11% -> 12%
where the time goes in v9:
time: 108 us
  starting transfers between devices  35.3 us (33%)
  blocking collectives  28.8 us (27%)
  waiting for transfers between devices  26.8 us (25%)
  Pallas kernels  16 us (15%)
    pallas_call x8, Pallas kernels, call(): return kernel(*operands)  16 us
    ppermute x3, waiting for transfers between devices, to_sides(): return lax.ppermute(x, LANE, perm)  15 us
    all_to_all x1, blocking collectives, shards(): got = lax.all_to_all(out, 'yh', split_axis=0, concat_axis=0, tiled=True)  14.7 us
    all_to_all x1, blocking collectives, shards(): got = lax.all_to_all(out, 'x', split_axis=0, concat_axis=0, tiled=True)  14.2 us
    all_to_all x1, starting transfers between devices, shards(): lax.all_to_all(copies, 'z', split_axis=0, concat_axis=0, tiled=True)  10.3 us
    all_to_all x1, starting transfers between devices, shards(): lax.all_to_all(stats, ('yl', *OUTER), split_axis=0, concat_axis=0, tiled=...  10.2 us
    ppermute x3, starting transfers between devices, to_sides(): return lax.ppermute(x, LANE, perm)  10.1 us
    all_to_all x1, waiting for transfers between devices, shards(): lax.all_to_all(copies, 'z', split_axis=0, concat_axis=0, tiled=True)  9.2 us
  transfers between devices with their start and end apart: 7, of which 4 were waited for; matrix products, arithmetic and copies ran while one was open for 0% of the time, Pallas kernels for 12%

profile of v9, /device:TPU:8, one launch (start us, length us, event | category | flops | bytes accessed | tf_op | source)
XLA Modules:
  0.0 107.9 jit_solution(3769544314480411380)
XLA Ops:
  0.6 0.0 copy-start
  0.6 0.0 copy-start.3
  0.7 1.9 %shard_map.50 = bf16[8,64,768]{2,1,0:T(8,128)(2,1)} custom-call(bf16[64,768]{1,0:T(8,128)(2,1)} %x_hbm.1), custom_call_target="tpu_custom_call" | custom-call | bytes 4194304 | tf_op jit(solution)/shard_map/pallas_call | solution.py:186
  2.6 10.3 %all-to-all-start = ((bf16[8,64,768]{2,1,0:T(8,128)(2,1)}), bf16[8,64,768]{2,1,0:T(8,128)(2,1)S(1)}, u32[]{:S(2)}, u32[]{:S(2)}) async-start(bf16[8,64,768]{2,1,0:T(8,128)(2,1)} %shard_map.50), calls=%async_computation | async-start | bytes 1572864 | tf_op jit(solution)/shard_map/all_to_all | solution.py:219
  12.9 0.0 copy-done
  12.9 2.4 %collective-permute-start = (bf16[512,768]{1,0:T(8,128)(2,1)S(1)}, bf16[512,768]{1,0:T(8,128)(2,1)S(1)}, u32[]{:S(2)}, u32[]{:S(2)}) collective-permute-start(bf16[512,768]{1,0:T(8,128)(2,1)S(1)} %copy-done), channel_id=1, source_target_pairs={{0,386},{1,3},{2,0},{3,129},{128,2},{129,131},{130,128},{131,257},... | collective-permute-start | bytes 2359304 | tf_op jit(solution)/shard_map/ppermute | solution.py:32
  15.3 0.0 copy-done.3
  15.3 5.4 %collective-permute-start.1 = (s32[1,512]{1,0:T(1,128)S(1)}, s32[1,512]{1,0:T(1,128)S(1)}, u32[]{:S(2)}, u32[]{:S(2)}) collective-permute-start(s32[1,512]{1,0:T(1,128)S(1)} %bitcast.15), channel_id=1, source_target_pairs={{0,386},{1,3},{2,0},{3,129},{128,2},{129,131},{130,128},{131,257},... | collective-permute-start | bytes 6152 | tf_op jit(solution)/shard_map/ppermute | solution.py:32
  20.7 6.1 %collective-permute-done.1.posf_ref = s32[1,512]{1,0:T(1,128)S(1)} collective-permute-done((s32[1,512]{1,0:T(1,128)S(1)}, s32[1,512]{1,0:T(1,128)S(1)}, u32[]{:S(2)}, u32[]{:S(2)}) %collective-permute-start.1) | collective-permute-done | bytes 2080 | tf_op jit(solution)/shard_map/ppermute | solution.py:32
  26.8 0.0 collective-permute-done.qf_ref
  26.8 9.2 %all-to-all-done = bf16[8,64,768]{2,1,0:T(8,128)(2,1)S(1)} async-done(((bf16[8,64,768]{2,1,0:T(8,128)(2,1)}), bf16[8,64,768]{2,1,0:T(8,128)(2,1)S(1)}, u32[]{:S(2)}, u32[]{:S(2)}) %all-to-all-start) | async-done | bytes 786464 | tf_op jit(solution)/shard_map/all_to_all | solution.py:219
  36.0 2.3 %collective-permute-start.3 = (bf16[512,768]{1,0:T(8,128)(2,1)S(1)}, bf16[512,768]{1,0:T(8,128)(2,1)}, u32[]{:S(2)}, u32[]{:S(2)}) collective-permute-start(bf16[512,768]{1,0:T(8,128)(2,1)S(1)} %bitcast.10), channel_id=1, source_target_pairs={{0,386},{1,3},{2,0},{3,129},{128,2},{129,131},{130,128},{131,257},... | collective-permute-start | bytes 2359304 | tf_op jit(solution)/shard_map/ppermute | solution.py:32
  38.4 2.8 %collective-permute-start.2 = (bf16[512,768]{1,0:T(8,128)(2,1)S(1)}, bf16[512,768]{1,0:T(8,128)(2,1)S(1)}, u32[]{:S(2)}, u32[]{:S(2)}) collective-permute-start(bf16[512,768]{1,0:T(8,128)(2,1)S(1)} %bitcast.11), channel_id=1, source_target_pairs={{0,1},{1,0},{2,3},{3,2},{4,5},{5,4},{6,7},{7,6},{8,9},{9,8},{10,11... | collective-permute-start | bytes 2359304 | tf_op jit(solution)/shard_map/ppermute | solution.py:24
  41.2 8.8 %collective-permute-done.3.side_hbm = bf16[512,768]{1,0:T(8,128)(2,1)} collective-permute-done((bf16[512,768]{1,0:T(8,128)(2,1)S(1)}, bf16[512,768]{1,0:T(8,128)(2,1)}, u32[]{:S(2)}, u32[]{:S(2)}) %collective-permute-start.3) | collective-permute-done | bytes 786464 | tf_op jit(solution)/shard_map/ppermute | solution.py:32
  50.0 1.9 %collective-permute-start.4 = (bf16[512,768]{1,0:T(8,128)(2,1)}, bf16[512,768]{1,0:T(8,128)(2,1)}, u32[]{:S(2)}, u32[]{:S(2)}) collective-permute-start(bf16[512,768]{1,0:T(8,128)(2,1)} %collective-permute-done.3.side_hbm), channel_id=1, source_target_pairs={{0,1},{1,0},{2,3},{3,2},{4,5},{5,4},{6,7},{7,6},{8,9},{9,8},{10,11... | collective-permute-start | bytes 2359304 | tf_op jit(solution)/shard_map/ppermute | solution.py:24
  52.0 0.1 stack.23.base_ref
  52.1 2.2 %shard_map.51 = (f32[8,512]{1,0:T(8,128)S(1)}, bf16[512,512]{1,0:T(8,128)(2,1)}) custom-call(s32[5]{0:T(128)S(1)} %stack.23.base_ref, bf16[512,768]{1,0:T(8,128)(2,1)S(1)} %bitcast.12, bf16[512,768]{1,0:T(8,128)(2,1)S(1)} %copy-done, s32[1,512]{1,0:T(1,128)S(1)} %bitcast.16, bf16[512,768]{1,0:T(8,128)(2,1)S(1)} %collective-permute-done.qf_ref, ...), custom_call_target="tpu_custom_call" | custom-call | flops 805306368 | bytes 4194304 | tf_op jit(solution)/shard_map/pallas_call | solution.py:186
  54.3 0.0 collective-permute-done.2.b_ref.b_hbm
  54.3 0.0 copy-start.2
  54.3 2.9 %shard_map.52 = (f32[8,512]{1,0:T(8,128)S(1)}, bf16[512,512]{1,0:T(8,128)(2,1)}, f32[32,1,1024]{2,1,0:T(1,128)}) custom-call(s32[5]{0:T(128)S(1)} %stack.23.base_ref, bf16[512,768]{1,0:T(8,128)(2,1)S(1)} %collective-permute-done.2.b_ref.b_hbm, bf16[512,768]{1,0:T(8,128)(2,1)S(1)} %copy-done, s32[1,512]{1,0:T(1,128)S(1)} %bitcast.17, ...), custom_call_target="tpu_custom_call" | custom-call | flops 805306368 | bytes 4194304 | tf_op jit(solution)/shard_map/pallas_call | solution.py:186
  57.1 0.0 copy-done.1
  57.1 0.0 copy-done.2
  57.2 10.2 %all-to-all-start.1 = ((f32[32,1,1024]{2,1,0:T(1,128)}), f32[32,1,1024]{2,1,0:T(1,128)S(1)}, u32[]{:S(2)}, u32[]{:S(2)}) async-start(f32[32,1,1024]{2,1,0:T(1,128)} %get-tuple-element.22), calls=%async_computation.1 | async-start | bytes 262144 | tf_op jit(solution)/shard_map/all_to_all | solution.py:242
  67.4 2.0 %shard_map.53 = (bf16[512,768]{1,0:T(8,128)(2,1)S(1)}, bf16[512,768]{1,0:T(8,128)(2,1)S(1)}, f32[512,512]{1,0:T(8,128)S(1)}) custom-call(bf16[512,768]{1,0:T(8,128)(2,1)} %q_hbm.1, bf16[512,768]{1,0:T(8,128)(2,1)} %collective-permute-done.3.side_hbm), custom_call_target="tpu_custom_call" | custom-call | flops 402653184 | bytes 4194304 | tf_op jit(solution)/shard_map/pallas_call | solution.py:186
  69.4 0.0 collective-permute-done.4.side2_ref
  69.4 5.6 %shard_map.54 = (f32[8,512]{1,0:T(8,128)S(1)}, f32[768,512]{1,0:T(8,128)S(1)}, bf16[768,512]{1,0:T(8,128)(2,1)S(1)}) custom-call(s32[5]{0:T(128)S(1)} %stack.23.base_ref, bf16[512,768]{1,0:T(8,128)(2,1)} %bitcast.13, bf16[512,768]{1,0:T(8,128)(2,1)} %copy-done.2, bf16[512,512]{1,0:T(8,128)(2,1)} %get-tuple-element.23.wa_hbm, ...), custom_call_target="tpu_custom_call" | custom-call | flops 4026531840 | bytes 4194304 | tf_op jit(solution)/shard_map/pallas_call | solution.py:186
  75.0 2.6 %all-to-all-done.1.every_ref = f32[32,1,1024]{2,1,0:T(1,128)S(1)} async-done(((f32[32,1,1024]{2,1,0:T(1,128)}), f32[32,1,1024]{2,1,0:T(1,128)S(1)}, u32[]{:S(2)}, u32[]{:S(2)}) %all-to-all-start.1) | async-done | bytes 131104 | tf_op jit(solution)/shard_map/all_to_all | solution.py:242
  77.6 0.6 shard_map.55
  78.3 14.2 %all_to_all.20.got_ref = bf16[4,192,512]{2,1,0:T(8,128)(2,1)S(1)} all-to-all(bf16[4,192,512]{2,1,0:T(8,128)(2,1)S(1)} %get-tuple-element.32), channel_id=1, replica_groups=mesh['yh'=4,'x'=4,'z'=8,'yl'=2,'c'=2] {'x'}, dimensions={0} | all-to-all | bytes 1572864 | tf_op jit(solution)/shard_map/all_to_all | solution.py:275
  92.4 0.1 shard_map.56
  92.5 14.7 %all_to_all.21.got_ref = bf16[4,48,512]{2,1,0:T(8,128)(2,1)S(1)} all-to-all(bf16[4,48,512]{2,1,0:T(8,128)(2,1)S(1)} %bitcast.14), channel_id=1, replica_groups=mesh['yh'=4,'x'=4,'z'=8,'yl'=2,'c'=2] {'yh'}, dimensions={0} | all-to-all | bytes 393216 | tf_op jit(solution)/shard_map/all_to_all | solution.py:280
  107.2 0.7 shard_map.57
  (1 shorter events, 0.0 us)
Async XLA Ops:
  0.6 12.3 %copy-start = (bf16[512,768]{1,0:T(8,128)(2,1)S(1)}, bf16[512,768]{1,0:T(8,128)(2,1)}, u32[]{:S(2)}) copy-start(bf16[512,768]{1,0:T(8,128)(2,1)} %q_hbm.1) | copy-start | bytes 2359300
  0.6 14.7 %copy-start.3 = (s32[512]{0:T(512)S(1)}, s32[512]{0:T(512)}, u32[]{:S(2)}) copy-start(s32[512]{0:T(512)} %param.5) | copy-start | bytes 6148
  2.6 33.4 %all-to-all-start = ((bf16[8,64,768]{2,1,0:T(8,128)(2,1)}), bf16[8,64,768]{2,1,0:T(8,128)(2,1)S(1)}, u32[]{:S(2)}, u32[]{:S(2)}) async-start(bf16[8,64,768]{2,1,0:T(8,128)(2,1)} %shard_map.50), calls=%async_computation | async-start | bytes 1572864 | tf_op jit(solution)/shard_map/all_to_all | solution.py:219
  12.9 13.9 %collective-permute-start = (bf16[512,768]{1,0:T(8,128)(2,1)S(1)}, bf16[512,768]{1,0:T(8,128)(2,1)S(1)}, u32[]{:S(2)}, u32[]{:S(2)}) collective-permute-start(bf16[512,768]{1,0:T(8,128)(2,1)S(1)} %copy-done), channel_id=1, source_target_pairs={{0,386},{1,3},{2,0},{3,129},{128,2},{129,131},{130,128},{131,257},... | collective-permute-start | bytes 2359304 | tf_op jit(solution)/shard_map/ppermute | solution.py:32
  15.3 11.5 %collective-permute-start.1 = (s32[1,512]{1,0:T(1,128)S(1)}, s32[1,512]{1,0:T(1,128)S(1)}, u32[]{:S(2)}, u32[]{:S(2)}) collective-permute-start(s32[1,512]{1,0:T(1,128)S(1)} %bitcast.15), channel_id=1, source_target_pairs={{0,386},{1,3},{2,0},{3,129},{128,2},{129,131},{130,128},{131,257},... | collective-permute-start | bytes 6152 | tf_op jit(solution)/shard_map/ppermute | solution.py:32
  36.0 21.1 %copy-start.1 = (bf16[8,64,768]{2,1,0:T(8,128)(2,1)}, bf16[8,64,768]{2,1,0:T(8,128)(2,1)S(1)}, u32[]{:S(2)}) copy-start(bf16[8,64,768]{2,1,0:T(8,128)(2,1)S(1)} %all-to-all-done) | copy-start | bytes 2359300
  36.0 14.0 %collective-permute-start.3 = (bf16[512,768]{1,0:T(8,128)(2,1)S(1)}, bf16[512,768]{1,0:T(8,128)(2,1)}, u32[]{:S(2)}, u32[]{:S(2)}) collective-permute-start(bf16[512,768]{1,0:T(8,128)(2,1)S(1)} %bitcast.10), channel_id=1, source_target_pairs={{0,386},{1,3},{2,0},{3,129},{128,2},{129,131},{130,128},{131,257},... | collective-permute-start | bytes 2359304 | tf_op jit(solution)/shard_map/ppermute | solution.py:32
  38.4 15.9 %collective-permute-start.2 = (bf16[512,768]{1,0:T(8,128)(2,1)S(1)}, bf16[512,768]{1,0:T(8,128)(2,1)S(1)}, u32[]{:S(2)}, u32[]{:S(2)}) collective-permute-start(bf16[512,768]{1,0:T(8,128)(2,1)S(1)} %bitcast.11), channel_id=1, source_target_pairs={{0,1},{1,0},{2,3},{3,2},{4,5},{5,4},{6,7},{7,6},{8,9},{9,8},{10,11... | collective-permute-start | bytes 2359304 | tf_op jit(solution)/shard_map/ppermute | solution.py:24
  50.0 19.4 %collective-permute-start.4 = (bf16[512,768]{1,0:T(8,128)(2,1)}, bf16[512,768]{1,0:T(8,128)(2,1)}, u32[]{:S(2)}, u32[]{:S(2)}) collective-permute-start(bf16[512,768]{1,0:T(8,128)(2,1)} %collective-permute-done.3.side_hbm), channel_id=1, source_target_pairs={{0,1},{1,0},{2,3},{3,2},{4,5},{5,4},{6,7},{7,6},{8,9},{9,8},{10,11... | collective-permute-start | bytes 2359304 | tf_op jit(solution)/shard_map/ppermute | solution.py:24
  54.3 2.9 %copy-start.2 = (bf16[512,768]{1,0:T(8,128)(2,1)}, bf16[512,768]{1,0:T(8,128)(2,1)S(1)}, u32[]{:S(2)}) copy-start(bf16[512,768]{1,0:T(8,128)(2,1)S(1)} %collective-permute-done.2.b_ref.b_hbm) | copy-start | bytes 2359300
  57.2 20.5 %all-to-all-start.1 = ((f32[32,1,1024]{2,1,0:T(1,128)}), f32[32,1,1024]{2,1,0:T(1,128)S(1)}, u32[]{:S(2)}, u32[]{:S(2)}) async-start(f32[32,1,1024]{2,1,0:T(1,128)} %get-tuple-element.22), calls=%async_computation.1 | async-start | bytes 262144 | tf_op jit(solution)/shard_map/all_to_all | solution.py:242

commit v10 on v8

--- a/solution.py
+++ b/solution.py
@@ -89,34 +89,36 @@
     copy.wait()
 
 
-def load_kernel(*refs):
-    count = (len(refs) - 1) // 2
-    copies = [pltpu.make_async_copy(refs[i], refs[count + i], refs[-1].at[i]) for i in range(count)]
+def side_kernel(q_hbm, side_hbm, q_ref, side_ref, s_ref, sems):
+    pairs = ((q_hbm, q_ref), (side_hbm, side_ref))
+    copies = [pltpu.make_async_copy(src, dst, sems.at[i]) for i, (src, dst) in enumerate(pairs)]
     for copy in copies:
         copy.start()
     for copy in copies:
         copy.wait()
-
-
-def mix_kernel(scale, rows, base_ref, a_hbm, b_hbm, wo_hbm, side_ref, side2_ref, q_ref, pos_ref, st0_ref, st_ref, m_ref, c_ref, s_ref, w_ref, a_ref, b_ref, wo_ref, sems):
+    s_ref[...] = dot(side_ref[...], q_ref[...], ((1,), (1,)))
+
+
+def mix_kernel(scale, rows, base_ref, a_hbm, b_hbm, wo_hbm, side_ref, ss_ref, side2_ref, q_ref, pos_ref, st0_ref, st_ref, m_ref, c_ref, s_ref, w_ref, a_ref, b_ref, wo_ref, sems):
     pairs = ((a_hbm, a_ref), (b_hbm, b_ref), (wo_hbm, wo_ref))
     copies = [pltpu.make_async_copy(src, dst, sems.at[i]) for i, (src, dst) in enumerate(pairs)]
     for copy in copies:
         copy.start()
-    q = q_ref[...]
     n = side2_ref.shape[0]
-    s_ref[:n, :] = dot(side2_ref[...], q, ((1,), (1,)))
-    s_ref[n:, :] = dot(side_ref[...], q, ((1,), (1,)))
+    k = scale * LOG2E
+    s_ref[...] = dot(side2_ref[...], q_ref[...], ((1,), (1,)))
     top0 = st0_ref[0:1, :]
-    top = jnp.maximum(jnp.max(s_ref[...], axis=0, keepdims=True), top0)
-    w_ref[...] = jnp.exp2((s_ref[...] - top) * (scale * LOG2E)).astype(BF16)
+    top = jnp.maximum(jnp.max(s_ref[...], axis=0, keepdims=True), jnp.max(ss_ref[...], axis=0, keepdims=True))
+    top = jnp.maximum(top, top0)
     st_ref[0:1, :] = top
+    w_ref[:n, :] = jnp.exp2((s_ref[...] - top) * k).astype(BF16)
+    w_ref[n:, :] = jnp.exp2((ss_ref[...] - top) * k).astype(BF16)
     mix, chosen = products((side2_ref, side_ref), (base_ref[3], base_ref[2]), w_ref, pos_ref, rows)
     m_ref[...] = mix
     for copy in copies:
         copy.wait()
     mix, more = products((a_ref, b_ref), (base_ref[0], base_ref[1]), wo_ref, pos_ref, rows)
-    m_ref[...] += mix * jnp.exp2((top0 - top) * (scale * LOG2E))
+    m_ref[...] += mix * jnp.exp2((top0 - top) * k)
     c_ref[...] = (chosen + more).astype(BF16)
 
 
@@ -221,20 +223,21 @@
     )
     every = lax.all_to_all(stats, ("yl", *OUTER), split_axis=0, concat_axis=0, tiled=True)
     side2 = swapped(side)
-    queries, side = call(
-        load_kernel,
-        [(queries.shape, BF16), ((n, width), BF16)],
+    queries, side, scores = call(
+        side_kernel,
+        [(queries.shape, BF16), ((n, width), BF16), ((n, count), F32)],
         (queries, side),
         [pltpu.SemaphoreType.DMA((2,))],
-        vmem=4,
+        flops,
+        vmem=8,
         hbm_in=(0, 1),
     )
     st, m, ch = call(
         functools.partial(mix_kernel, scale, rows),
         [((8, count), F32), ((width, count), F32), ((width, count), BF16)],
-        (base, column, column2, weights, side, side2, queries, pos, st1),
+        (base, column, column2, weights, side, scores, side2, queries, pos, st1),
         [
-            ((2 * n, count), F32),
+            ((n, count), F32),
             ((2 * n, count), BF16),
             ((n, width), BF16),
             ((n, width), BF16),

time: 107 us -> 107 us (level)
  no operation moved by 1% of the time
where the time goes in v10:
time: 107 us
  starting transfers between devices  35.3 us (33%)
  blocking collectives  29.2 us (27%)
  waiting for transfers between devices  26.4 us (25%)
  Pallas kernels  15.1 us (14%)
    pallas_call x7, Pallas kernels, call(): return kernel(*operands)  15.1 us
    all_to_all x1, blocking collectives, shards(): got = lax.all_to_all(out, 'yh', split_axis=0, concat_axis=0, tiled=True)  15 us
    ppermute x3, waiting for transfers between devices, to_sides(): return lax.ppermute(x, LANE, perm)  15 us
    all_to_all x1, blocking collectives, shards(): got = lax.all_to_all(out, 'x', split_axis=0, concat_axis=0, tiled=True)  14.2 us
    all_to_all x1, starting transfers between devices, shards(): lax.all_to_all(copies, 'z', split_axis=0, concat_axis=0, tiled=True)  10.3 us
    all_to_all x1, starting transfers between devices, shards(): lax.all_to_all(stats, ('yl', *OUTER), split_axis=0, concat_axis=0, tiled=...  10.2 us
    ppermute x3, starting transfers between devices, to_sides(): return lax.ppermute(x, LANE, perm)  10.1 us
    all_to_all x1, waiting for transfers between devices, shards(): lax.all_to_all(copies, 'z', split_axis=0, concat_axis=0, tiled=True)  9.2 us
  transfers between devices with their start and end apart: 7, of which 4 were waited for; matrix products, arithmetic and copies ran while one was open for 0% of the time, Pallas kernels for 11%

profile of v10, /device:TPU:8, one launch (start us, length us, event | category | flops | bytes accessed | tf_op | source)
XLA Modules:
  0.0 106.9 jit_solution(3408838090779147482)
XLA Ops:
  0.6 0.0 copy-start
  0.6 0.0 copy-start.3
  0.7 1.9 %shard_map.50 = bf16[8,64,768]{2,1,0:T(8,128)(2,1)} custom-call(bf16[64,768]{1,0:T(8,128)(2,1)} %x_hbm.1), custom_call_target="tpu_custom_call" | custom-call | bytes 4194304 | tf_op jit(solution)/shard_map/pallas_call | solution.py:177
  2.6 10.3 %all-to-all-start = ((bf16[8,64,768]{2,1,0:T(8,128)(2,1)}), bf16[8,64,768]{2,1,0:T(8,128)(2,1)S(1)}, u32[]{:S(2)}, u32[]{:S(2)}) async-start(bf16[8,64,768]{2,1,0:T(8,128)(2,1)} %shard_map.50), calls=%async_computation | async-start | bytes 1572864 | tf_op jit(solution)/shard_map/all_to_all | solution.py:210
  12.9 0.0 copy-done
  12.9 2.4 %collective-permute-start = (bf16[512,768]{1,0:T(8,128)(2,1)S(1)}, bf16[512,768]{1,0:T(8,128)(2,1)S(1)}, u32[]{:S(2)}, u32[]{:S(2)}) collective-permute-start(bf16[512,768]{1,0:T(8,128)(2,1)S(1)} %copy-done), channel_id=1, source_target_pairs={{0,386},{1,3},{2,0},{3,129},{128,2},{129,131},{130,128},{131,257},... | collective-permute-start | bytes 2359304 | tf_op jit(solution)/shard_map/ppermute | solution.py:32
  15.3 0.0 copy-done.3
  15.3 5.4 %collective-permute-start.1 = (s32[1,512]{1,0:T(1,128)S(1)}, s32[1,512]{1,0:T(1,128)S(1)}, u32[]{:S(2)}, u32[]{:S(2)}) collective-permute-start(s32[1,512]{1,0:T(1,128)S(1)} %bitcast.15), channel_id=1, source_target_pairs={{0,386},{1,3},{2,0},{3,129},{128,2},{129,131},{130,128},{131,257},... | collective-permute-start | bytes 6152 | tf_op jit(solution)/shard_map/ppermute | solution.py:32
  20.7 6.1 %collective-permute-done.1.posf_ref = s32[1,512]{1,0:T(1,128)S(1)} collective-permute-done((s32[1,512]{1,0:T(1,128)S(1)}, s32[1,512]{1,0:T(1,128)S(1)}, u32[]{:S(2)}, u32[]{:S(2)}) %collective-permute-start.1) | collective-permute-done | bytes 2080 | tf_op jit(solution)/shard_map/ppermute | solution.py:32
  26.8 0.0 collective-permute-done.qf_ref
  26.8 9.2 %all-to-all-done = bf16[8,64,768]{2,1,0:T(8,128)(2,1)S(1)} async-done(((bf16[8,64,768]{2,1,0:T(8,128)(2,1)}), bf16[8,64,768]{2,1,0:T(8,128)(2,1)S(1)}, u32[]{:S(2)}, u32[]{:S(2)}) %all-to-all-start) | async-done | bytes 786464 | tf_op jit(solution)/shard_map/all_to_all | solution.py:210
  36.0 0.0 copy-start.1
  36.0 2.3 %collective-permute-start.3 = (bf16[512,768]{1,0:T(8,128)(2,1)S(1)}, bf16[512,768]{1,0:T(8,128)(2,1)}, u32[]{:S(2)}, u32[]{:S(2)}) collective-permute-start(bf16[512,768]{1,0:T(8,128)(2,1)S(1)} %bitcast.10), channel_id=1, source_target_pairs={{0,386},{1,3},{2,0},{3,129},{128,2},{129,131},{130,128},{131,257},... | collective-permute-start | bytes 2359304 | tf_op jit(solution)/shard_map/ppermute | solution.py:32
  38.4 2.8 %collective-permute-start.2 = (bf16[512,768]{1,0:T(8,128)(2,1)S(1)}, bf16[512,768]{1,0:T(8,128)(2,1)S(1)}, u32[]{:S(2)}, u32[]{:S(2)}) collective-permute-start(bf16[512,768]{1,0:T(8,128)(2,1)S(1)} %bitcast.11), channel_id=1, source_target_pairs={{0,1},{1,0},{2,3},{3,2},{4,5},{5,4},{6,7},{7,6},{8,9},{9,8},{10,11... | collective-permute-start | bytes 2359304 | tf_op jit(solution)/shard_map/ppermute | solution.py:24
  41.2 8.8 %collective-permute-done.3.side_hbm = bf16[512,768]{1,0:T(8,128)(2,1)} collective-permute-done((bf16[512,768]{1,0:T(8,128)(2,1)S(1)}, bf16[512,768]{1,0:T(8,128)(2,1)}, u32[]{:S(2)}, u32[]{:S(2)}) %collective-permute-start.3) | collective-permute-done | bytes 786464 | tf_op jit(solution)/shard_map/ppermute | solution.py:32
  50.0 1.9 %collective-permute-start.4 = (bf16[512,768]{1,0:T(8,128)(2,1)}, bf16[512,768]{1,0:T(8,128)(2,1)}, u32[]{:S(2)}, u32[]{:S(2)}) collective-permute-start(bf16[512,768]{1,0:T(8,128)(2,1)} %collective-permute-done.3.side_hbm), channel_id=1, source_target_pairs={{0,1},{1,0},{2,3},{3,2},{4,5},{5,4},{6,7},{7,6},{8,9},{9,8},{10,11... | collective-permute-start | bytes 2359304 | tf_op jit(solution)/shard_map/ppermute | solution.py:24
  52.0 0.1 stack.23.base_ref
  52.1 0.0 collective-permute-done.2.b_ref.b_hbm
  52.1 0.0 copy-start.2
  52.1 3.8 %shard_map.51 = (f32[8,512]{1,0:T(8,128)S(1)}, bf16[1024,512]{1,0:T(8,128)(2,1)}, f32[32,1,1024]{2,1,0:T(1,128)}) custom-call(s32[5]{0:T(128)S(1)} %stack.23.base_ref, bf16[512,768]{1,0:T(8,128)(2,1)S(1)} %bitcast.12, bf16[512,768]{1,0:T(8,128)(2,1)S(1)} %collective-permute-done.2.b_ref.b_hbm, bf16[512,768]{1,0:T(8,128)(2,1)S(1)} %copy-done, ...), custom_call_target="tpu_custom_call" | custom-call | flops 1610612736 | bytes 4194304 | tf_op jit(solution)/shard_map/pallas_call | solution.py:177
  55.8 0.0 copy-done.1
  55.8 0.0 copy-done.2
  55.8 10.2 %all-to-all-start.1 = ((f32[32,1,1024]{2,1,0:T(1,128)}), f32[32,1,1024]{2,1,0:T(1,128)S(1)}, u32[]{:S(2)}, u32[]{:S(2)}) async-start(f32[32,1,1024]{2,1,0:T(1,128)} %get-tuple-element.19), calls=%async_computation.1 | async-start | bytes 262144 | tf_op jit(solution)/shard_map/all_to_all | solution.py:224
  66.1 2.0 %shard_map.52 = (bf16[512,768]{1,0:T(8,128)(2,1)S(1)}, bf16[512,768]{1,0:T(8,128)(2,1)S(1)}, f32[512,512]{1,0:T(8,128)S(1)}) custom-call(bf16[512,768]{1,0:T(8,128)(2,1)} %q_hbm.1, bf16[512,768]{1,0:T(8,128)(2,1)} %collective-permute-done.3.side_hbm), custom_call_target="tpu_custom_call" | custom-call | flops 402653184 | bytes 4194304 | tf_op jit(solution)/shard_map/pallas_call | solution.py:177
  68.1 0.0 collective-permute-done.4.side2_ref
  68.1 6.0 %shard_map.53 = (f32[8,512]{1,0:T(8,128)S(1)}, f32[768,512]{1,0:T(8,128)S(1)}, bf16[768,512]{1,0:T(8,128)(2,1)S(1)}) custom-call(s32[5]{0:T(128)S(1)} %stack.23.base_ref, bf16[512,768]{1,0:T(8,128)(2,1)} %bitcast.13, bf16[512,768]{1,0:T(8,128)(2,1)} %copy-done.2, bf16[1024,512]{1,0:T(8,128)(2,1)} %get-tuple-element.20.wo_hbm, ...), custom_call_target="tpu_custom_call" | custom-call | flops 4026531840 | bytes 4194304 | tf_op jit(solution)/shard_map/pallas_call | solution.py:177
  74.1 2.2 %all-to-all-done.1.every_ref = f32[32,1,1024]{2,1,0:T(1,128)S(1)} async-done(((f32[32,1,1024]{2,1,0:T(1,128)}), f32[32,1,1024]{2,1,0:T(1,128)S(1)}, u32[]{:S(2)}, u32[]{:S(2)}) %all-to-all-start.1) | async-done | bytes 131104 | tf_op jit(solution)/shard_map/all_to_all | solution.py:224
  76.3 0.6 shard_map.54
  77.0 14.2 %all_to_all.20.got_ref = bf16[4,192,512]{2,1,0:T(8,128)(2,1)S(1)} all-to-all(bf16[4,192,512]{2,1,0:T(8,128)(2,1)S(1)} %get-tuple-element.28), channel_id=1, replica_groups=mesh['yh'=4,'x'=4,'z'=8,'yl'=2,'c'=2] {'x'}, dimensions={0} | all-to-all | bytes 1572864 | tf_op jit(solution)/shard_map/all_to_all | solution.py:256
  91.1 0.1 shard_map.55
  91.2 15.0 %all_to_all.21.got_ref = bf16[4,48,512]{2,1,0:T(8,128)(2,1)S(1)} all-to-all(bf16[4,48,512]{2,1,0:T(8,128)(2,1)S(1)} %bitcast.14), channel_id=1, replica_groups=mesh['yh'=4,'x'=4,'z'=8,'yl'=2,'c'=2] {'yh'}, dimensions={0} | all-to-all | bytes 393216 | tf_op jit(solution)/shard_map/all_to_all | solution.py:261
  106.3 0.7 shard_map.56
Async XLA Ops:
  0.6 12.3 %copy-start = (bf16[512,768]{1,0:T(8,128)(2,1)S(1)}, bf16[512,768]{1,0:T(8,128)(2,1)}, u32[]{:S(2)}) copy-start(bf16[512,768]{1,0:T(8,128)(2,1)} %q_hbm.1) | copy-start | bytes 2359300
  0.6 14.7 %copy-start.3 = (s32[512]{0:T(512)S(1)}, s32[512]{0:T(512)}, u32[]{:S(2)}) copy-start(s32[512]{0:T(512)} %param.5) | copy-start | bytes 6148
  2.6 33.4 %all-to-all-start = ((bf16[8,64,768]{2,1,0:T(8,128)(2,1)}), bf16[8,64,768]{2,1,0:T(8,128)(2,1)S(1)}, u32[]{:S(2)}, u32[]{:S(2)}) async-start(bf16[8,64,768]{2,1,0:T(8,128)(2,1)} %shard_map.50), calls=%async_computation | async-start | bytes 1572864 | tf_op jit(solution)/shard_map/all_to_all | solution.py:210
  12.9 13.9 %collective-permute-start = (bf16[512,768]{1,0:T(8,128)(2,1)S(1)}, bf16[512,768]{1,0:T(8,128)(2,1)S(1)}, u32[]{:S(2)}, u32[]{:S(2)}) collective-permute-start(bf16[512,768]{1,0:T(8,128)(2,1)S(1)} %copy-done), channel_id=1, source_target_pairs={{0,386},{1,3},{2,0},{3,129},{128,2},{129,131},{130,128},{131,257},... | collective-permute-start | bytes 2359304 | tf_op jit(solution)/shard_map/ppermute | solution.py:32
  15.3 11.5 %collective-permute-start.1 = (s32[1,512]{1,0:T(1,128)S(1)}, s32[1,512]{1,0:T(1,128)S(1)}, u32[]{:S(2)}, u32[]{:S(2)}) collective-permute-start(s32[1,512]{1,0:T(1,128)S(1)} %bitcast.15), channel_id=1, source_target_pairs={{0,386},{1,3},{2,0},{3,129},{128,2},{129,131},{130,128},{131,257},... | collective-permute-start | bytes 6152 | tf_op jit(solution)/shard_map/ppermute | solution.py:32
  36.0 19.8 %copy-start.1 = (bf16[8,64,768]{2,1,0:T(8,128)(2,1)}, bf16[8,64,768]{2,1,0:T(8,128)(2,1)S(1)}, u32[]{:S(2)}) copy-start(bf16[8,64,768]{2,1,0:T(8,128)(2,1)S(1)} %all-to-all-done) | copy-start | bytes 2359300
  36.0 14.0 %collective-permute-start.3 = (bf16[512,768]{1,0:T(8,128)(2,1)S(1)}, bf16[512,768]{1,0:T(8,128)(2,1)}, u32[]{:S(2)}, u32[]{:S(2)}) collective-permute-start(bf16[512,768]{1,0:T(8,128)(2,1)S(1)} %bitcast.10), channel_id=1, source_target_pairs={{0,386},{1,3},{2,0},{3,129},{128,2},{129,131},{130,128},{131,257},... | collective-permute-start | bytes 2359304 | tf_op jit(solution)/shard_map/ppermute | solution.py:32
  38.4 13.7 %collective-permute-start.2 = (bf16[512,768]{1,0:T(8,128)(2,1)S(1)}, bf16[512,768]{1,0:T(8,128)(2,1)S(1)}, u32[]{:S(2)}, u32[]{:S(2)}) collective-permute-start(bf16[512,768]{1,0:T(8,128)(2,1)S(1)} %bitcast.11), channel_id=1, source_target_pairs={{0,1},{1,0},{2,3},{3,2},{4,5},{5,4},{6,7},{7,6},{8,9},{9,8},{10,11... | collective-permute-start | bytes 2359304 | tf_op jit(solution)/shard_map/ppermute | solution.py:24
  50.0 18.1 %collective-permute-start.4 = (bf16[512,768]{1,0:T(8,128)(2,1)}, bf16[512,768]{1,0:T(8,128)(2,1)}, u32[]{:S(2)}, u32[]{:S(2)}) collective-permute-start(bf16[512,768]{1,0:T(8,128)(2,1)} %collective-permute-done.3.side_hbm), channel_id=1, source_target_pairs={{0,1},{1,0},{2,3},{3,2},{4,5},{5,4},{6,7},{7,6},{8,9},{9,8},{10,11... | collective-permute-start | bytes 2359304 | tf_op jit(solution)/shard_map/ppermute | solution.py:24
  52.1 3.8 %copy-start.2 = (bf16[512,768]{1,0:T(8,128)(2,1)}, bf16[512,768]{1,0:T(8,128)(2,1)S(1)}, u32[]{:S(2)}) copy-start(bf16[512,768]{1,0:T(8,128)(2,1)S(1)} %collective-permute-done.2.b_ref.b_hbm) | copy-start | bytes 2359300
  55.8 20.5 %all-to-all-start.1 = ((f32[32,1,1024]{2,1,0:T(1,128)}), f32[32,1,1024]{2,1,0:T(1,128)S(1)}, u32[]{:S(2)}, u32[]{:S(2)}) async-start(f32[32,1,1024]{2,1,0:T(1,128)} %get-tuple-element.19), calls=%async_computation.1 | async-start | bytes 262144 | tf_op jit(solution)/shard_map/all_to_all | solution.py:224

commit v11 on v10

--- a/solution.py
+++ b/solution.py
@@ -151,11 +151,23 @@
         copy.wait()
 
 
-def sum_kernel(scale, got_ref, out_ref):
+def middle_kernel(base_ref, got_ref, *refs):
+    outs, sum_ref = refs[:-1], refs[-1]
     total = got_ref[0].astype(F32)
     for i in range(1, got_ref.shape[0]):
         total += got_ref[i].astype(F32)
-    out_ref[...] = (scale * total).astype(BF16)
+    sum_ref[...] = total
+    n, piece = len(outs), outs[0].shape[0]
+    for k in range(n):
+        at = pl.multiple_of(((base_ref[5] + k) & (n - 1)) * piece, 8)
+        outs[k][...] = sum_ref[pl.ds(at, piece), :].astype(BF16)
+
+
+def final_kernel(scale, *refs):
+    total = refs[0][...].astype(F32)
+    for ref in refs[1:-1]:
+        total += ref[...].astype(F32)
+    refs[-1][...] = (scale * total).astype(BF16)
 
 
 def call(body, out, operands, scratch=(), flops=0, vmem=12, hbm_in=(), hbm_out=()):
@@ -193,7 +205,7 @@
         return ((((yy >> 1) * nx + x) * nz * 2 + (yy & 1)) * 2 + cc) * rows
 
     base = jnp.stack(
-        [base_of(y, c), base_of(y, 1 - c), base_of(y + 1 - 2 * c, c), base_of(y - 1 + 2 * c, 1 - c), y & 1]
+        [base_of(y, c), base_of(y, 1 - c), base_of(y + 1 - 2 * c, c), base_of(y - 1 + 2 * c, 1 - c), y & 1, y >> 1]
     )
     pos = positive.reshape(1, count)
 
@@ -254,12 +266,13 @@
         (every, st, m, ch),
     )
     got = lax.all_to_all(out, "x", split_axis=0, concat_axis=0, tiled=True)
-    (out,) = call(functools.partial(sum_kernel, 1.0), [((width // nx, count), BF16)], (got,))
     nyh = ny // 2
     piece = width // nx // nyh
-    out = out.reshape(nyh, piece, count)
-    got = lax.all_to_all(out, "yh", split_axis=0, concat_axis=0, tiled=True)
-    (grad,) = call(functools.partial(sum_kernel, scale), [((piece, count), BF16)], (got,))
+    pieces = call(middle_kernel, [((piece, count), BF16)] * nyh, (base, got), [((width // nx, count), F32)])
+    got = [pieces[0]]
+    for k in range(1, nyh):
+        got.append(lax.ppermute(pieces[k], "yh", [(i, (i + k) % nyh) for i in range(nyh)]))
+    (grad,) = call(functools.partial(final_kernel, scale), [((piece, count), BF16)], got)
     return grad.T, loss.reshape(count)
 
 

time: 107 us -> 111 us (1.037)
  the two profiles are of different devices: /device:TPU:8 before, /device:TPU:48 now
where the time goes in v11:
time: 111 us; the launch traced here: 110 us
  starting transfers between devices  45.3 us (41%)
  waiting for transfers between devices  32.1 us (29%)
  blocking collectives  16.4 us (15%)
  Pallas kernels  15.7 us (14%)
    all_to_all x1, blocking collectives, shards(): got = lax.all_to_all(out, 'x', split_axis=0, concat_axis=0, tiled=True)  16.4 us
    ppermute x3, waiting for transfers between devices, to_sides(): return lax.ppermute(x, LANE, perm)  16.2 us
    pallas_call x7, Pallas kernels, call(): return kernel(*operands)  15.7 us
    ppermute x3, starting transfers between devices, shards(): lax.ppermute(pieces[k], 'yh', [(i, (i + k) % nyh) for i in range(nyh)])  11.7 us
    all_to_all x1, starting transfers between devices, shards(): lax.all_to_all(copies, 'z', split_axis=0, concat_axis=0, tiled=True)  10.3 us
    ppermute x3, starting transfers between devices, to_sides(): return lax.ppermute(x, LANE, perm)  9.76 us
    all_to_all x1, starting transfers between devices, shards(): lax.all_to_all(stats, ('yl', *OUTER), split_axis=0, concat_axis=0, tiled=...  9.68 us
    all_to_all x1, waiting for transfers between devices, shards(): lax.all_to_all(copies, 'z', split_axis=0, concat_axis=0, tiled=True)  9.2 us
  transfers between devices with their start and end apart: 10, of which 5 were waited for; matrix products, arithmetic and copies ran while one was open for 0% of the time, Pallas kernels for 11%

profile of v11, /device:TPU:48, one launch (start us, length us, event | category | flops | bytes accessed | tf_op | source)
XLA Modules:
  0.0 110.3 jit_solution(11312008210231446600)
XLA Ops:
  0.6 0.0 copy-start
  0.7 1.9 %shard_map.50 = bf16[8,64,768]{2,1,0:T(8,128)(2,1)} custom-call(bf16[64,768]{1,0:T(8,128)(2,1)} %x_hbm.1), custom_call_target="tpu_custom_call" | custom-call | bytes 4194304 | tf_op jit(solution)/shard_map/pallas_call | solution.py:189
  2.6 10.3 %all-to-all-start = ((bf16[8,64,768]{2,1,0:T(8,128)(2,1)}), bf16[8,64,768]{2,1,0:T(8,128)(2,1)S(1)}, u32[]{:S(2)}, u32[]{:S(2)}) async-start(bf16[8,64,768]{2,1,0:T(8,128)(2,1)} %shard_map.50), calls=%async_computation | async-start | bytes 1572864 | tf_op jit(solution)/shard_map/all_to_all | solution.py:222
  12.9 0.0 copy-done
  12.9 3.3 %collective-permute-start = (bf16[512,768]{1,0:T(8,128)(2,1)S(1)}, bf16[512,768]{1,0:T(8,128)(2,1)S(1)}, u32[]{:S(2)}, u32[]{:S(2)}) collective-permute-start(bf16[512,768]{1,0:T(8,128)(2,1)S(1)} %copy-done), channel_id=1, source_target_pairs={{0,386},{1,3},{2,0},{3,129},{128,2},{129,131},{130,128},{131,257},... | collective-permute-start | bytes 2359304 | tf_op jit(solution)/shard_map/ppermute | solution.py:32
  16.2 0.0 copy-done.3
  16.2 3.3 %collective-permute-start.1 = (s32[1,512]{1,0:T(1,128)S(1)}, s32[1,512]{1,0:T(1,128)S(1)}, u32[]{:S(2)}, u32[]{:S(2)}) collective-permute-start(s32[1,512]{1,0:T(1,128)S(1)} %bitcast.14), channel_id=1, source_target_pairs={{0,386},{1,3},{2,0},{3,129},{128,2},{129,131},{130,128},{131,257},... | collective-permute-start | bytes 6152 | tf_op jit(solution)/shard_map/ppermute | solution.py:32
  19.5 7.4 %collective-permute-done.1.posf_ref = s32[1,512]{1,0:T(1,128)S(1)} collective-permute-done((s32[1,512]{1,0:T(1,128)S(1)}, s32[1,512]{1,0:T(1,128)S(1)}, u32[]{:S(2)}, u32[]{:S(2)}) %collective-permute-start.1) | collective-permute-done | bytes 2080 | tf_op jit(solution)/shard_map/ppermute | solution.py:32
  26.8 0.0 collective-permute-done.qf_ref
  26.8 9.2 %all-to-all-done = bf16[8,64,768]{2,1,0:T(8,128)(2,1)S(1)} async-done(((bf16[8,64,768]{2,1,0:T(8,128)(2,1)}), bf16[8,64,768]{2,1,0:T(8,128)(2,1)S(1)}, u32[]{:S(2)}, u32[]{:S(2)}) %all-to-all-start) | async-done | bytes 786464 | tf_op jit(solution)/shard_map/all_to_all | solution.py:222
  36.0 3.2 %collective-permute-start.3 = (bf16[512,768]{1,0:T(8,128)(2,1)S(1)}, bf16[512,768]{1,0:T(8,128)(2,1)}, u32[]{:S(2)}, u32[]{:S(2)}) collective-permute-start(bf16[512,768]{1,0:T(8,128)(2,1)S(1)} %bitcast.10), channel_id=1, source_target_pairs={{0,386},{1,3},{2,0},{3,129},{128,2},{129,131},{130,128},{131,257},... | collective-permute-start | bytes 2359304 | tf_op jit(solution)/shard_map/ppermute | solution.py:32
  39.3 1.9 %collective-permute-start.2 = (bf16[512,768]{1,0:T(8,128)(2,1)S(1)}, bf16[512,768]{1,0:T(8,128)(2,1)S(1)}, u32[]{:S(2)}, u32[]{:S(2)}) collective-permute-start(bf16[512,768]{1,0:T(8,128)(2,1)S(1)} %bitcast.11), channel_id=1, source_target_pairs={{0,1},{1,0},{2,3},{3,2},{4,5},{5,4},{6,7},{7,6},{8,9},{9,8},{10,11... | collective-permute-start | bytes 2359304 | tf_op jit(solution)/shard_map/ppermute | solution.py:24
  41.2 8.8 %collective-permute-done.3.side_hbm = bf16[512,768]{1,0:T(8,128)(2,1)} collective-permute-done((bf16[512,768]{1,0:T(8,128)(2,1)S(1)}, bf16[512,768]{1,0:T(8,128)(2,1)}, u32[]{:S(2)}, u32[]{:S(2)}) %collective-permute-start.3) | collective-permute-done | bytes 786464 | tf_op jit(solution)/shard_map/ppermute | solution.py:32
  50.0 1.9 %collective-permute-start.4 = (bf16[512,768]{1,0:T(8,128)(2,1)}, bf16[512,768]{1,0:T(8,128)(2,1)}, u32[]{:S(2)}, u32[]{:S(2)}) collective-permute-start(bf16[512,768]{1,0:T(8,128)(2,1)} %collective-permute-done.3.side_hbm), channel_id=1, source_target_pairs={{0,1},{1,0},{2,3},{3,2},{4,5},{5,4},{6,7},{7,6},{8,9},{9,8},{10,11... | collective-permute-start | bytes 2359304 | tf_op jit(solution)/shard_map/ppermute | solution.py:24
  52.0 0.1 stack.27.base_ref
  52.0 0.0 collective-permute-done.2.b_ref.b_hbm
  52.0 3.7 %shard_map.51 = (f32[8,512]{1,0:T(8,128)S(1)}, bf16[1024,512]{1,0:T(8,128)(2,1)}, f32[32,1,1024]{2,1,0:T(1,128)}) custom-call(s32[6]{0:T(128)S(1)} %stack.27.base_ref, bf16[512,768]{1,0:T(8,128)(2,1)S(1)} %bitcast.12, bf16[512,768]{1,0:T(8,128)(2,1)S(1)} %collective-permute-done.2.b_ref.b_hbm, bf16[512,768]{1,0:T(8,128)(2,1)S(1)} %copy-done, ...), custom_call_target="tpu_custom_call" | custom-call | flops 1610612736 | bytes 4194304 | tf_op jit(solution)/shard_map/pallas_call | solution.py:189
  55.8 9.7 %all-to-all-start.1 = ((f32[32,1,1024]{2,1,0:T(1,128)}), f32[32,1,1024]{2,1,0:T(1,128)S(1)}, u32[]{:S(2)}, u32[]{:S(2)}) async-start(f32[32,1,1024]{2,1,0:T(1,128)} %get-tuple-element.23), calls=%async_computation.1 | async-start | bytes 262144 | tf_op jit(solution)/shard_map/all_to_all | solution.py:236
  65.5 2.0 %shard_map.52 = (bf16[512,768]{1,0:T(8,128)(2,1)S(1)}, bf16[512,768]{1,0:T(8,128)(2,1)S(1)}, f32[512,512]{1,0:T(8,128)S(1)}) custom-call(bf16[512,768]{1,0:T(8,128)(2,1)} %q_hbm.1, bf16[512,768]{1,0:T(8,128)(2,1)} %collective-permute-done.3.side_hbm), custom_call_target="tpu_custom_call" | custom-call | flops 402653184 | bytes 4194304 | tf_op jit(solution)/shard_map/pallas_call | solution.py:189
  67.5 0.0 collective-permute-done.4.side2_ref
  67.5 6.0 %shard_map.53 = (f32[8,512]{1,0:T(8,128)S(1)}, f32[768,512]{1,0:T(8,128)S(1)}, bf16[768,512]{1,0:T(8,128)(2,1)S(1)}) custom-call(s32[6]{0:T(128)S(1)} %stack.27.base_ref, bf16[512,768]{1,0:T(8,128)(2,1)} %bitcast.13, bf16[512,768]{1,0:T(8,128)(2,1)} %copy-done.2, bf16[1024,512]{1,0:T(8,128)(2,1)} %get-tuple-element.24.wo_hbm, ...), custom_call_target="tpu_custom_call" | custom-call | flops 4026531840 | bytes 4194304 | tf_op jit(solution)/shard_map/pallas_call | solution.py:189
  73.5 0.0 all-to-all-done.1.every_ref
  73.5 0.6 shard_map.54
  74.2 16.4 %all_to_all.15.got_ref = bf16[4,192,512]{2,1,0:T(8,128)(2,1)S(1)} all-to-all(bf16[4,192,512]{2,1,0:T(8,128)(2,1)S(1)} %get-tuple-element.32), channel_id=1, replica_groups=mesh['yh'=4,'x'=4,'z'=8,'yl'=2,'c'=2] {'x'}, dimensions={0} | all-to-all | bytes 1572864 | tf_op jit(solution)/shard_map/all_to_all | solution.py:268
  90.5 0.7 shard_map.55
  91.2 3.0 %collective-permute-start.5 = (bf16[48,512]{1,0:T(8,128)(2,1)S(1)}, bf16[48,512]{1,0:T(8,128)(2,1)S(1)}, u32[]{:S(2)}, u32[]{:S(2)}) collective-permute-start(bf16[48,512]{1,0:T(8,128)(2,1)S(1)} %get-tuple-element.34), channel_id=1, source_target_pairs={{0,128},{128,256},{256,384},{384,0},{1,129},{129,257},{257,385},{3... | collective-permute-start | bytes 147464 | tf_op jit(solution)/shard_map/ppermute | solution.py:274
  94.3 6.7 %collective-permute-start.6 = (bf16[48,512]{1,0:T(8,128)(2,1)S(1)}, bf16[48,512]{1,0:T(8,128)(2,1)S(1)}, u32[]{:S(2)}, u32[]{:S(2)}) collective-permute-start(bf16[48,512]{1,0:T(8,128)(2,1)S(1)} %get-tuple-element.35), channel_id=1, source_target_pairs={{0,256},{128,384},{256,0},{384,128},{1,257},{129,385},{257,1},{385... | collective-permute-start | bytes 147464 | tf_op jit(solution)/shard_map/ppermute | solution.py:274
  101.0 1.9 %collective-permute-start.7 = (bf16[48,512]{1,0:T(8,128)(2,1)S(1)}, bf16[48,512]{1,0:T(8,128)(2,1)S(1)}, u32[]{:S(2)}, u32[]{:S(2)}) collective-permute-start(bf16[48,512]{1,0:T(8,128)(2,1)S(1)} %get-tuple-element.36), channel_id=1, source_target_pairs={{0,384},{128,0},{256,128},{384,256},{1,385},{129,1},{257,129},{385... | collective-permute-start | bytes 147464 | tf_op jit(solution)/shard_map/ppermute | solution.py:274
  102.9 0.0 collective-permute-done.5.refs_1_
  102.9 1.2 %collective-permute-done.6.refs_2_ = bf16[48,512]{1,0:T(8,128)(2,1)S(1)} collective-permute-done((bf16[48,512]{1,0:T(8,128)(2,1)S(1)}, bf16[48,512]{1,0:T(8,128)(2,1)S(1)}, u32[]{:S(2)}, u32[]{:S(2)}) %collective-permute-start.6) | collective-permute-done | bytes 49184 | tf_op jit(solution)/shard_map/ppermute | solution.py:274
  104.2 5.5 %collective-permute-done.7.refs_3_ = bf16[48,512]{1,0:T(8,128)(2,1)S(1)} collective-permute-done((bf16[48,512]{1,0:T(8,128)(2,1)S(1)}, bf16[48,512]{1,0:T(8,128)(2,1)S(1)}, u32[]{:S(2)}, u32[]{:S(2)}) %collective-permute-start.7) | collective-permute-done | bytes 49184 | tf_op jit(solution)/shard_map/ppermute | solution.py:274
  109.6 0.7 shard_map.56
  (5 shorter events, 0.0 us)
Async XLA Ops:
  0.6 12.3 %copy-start = (bf16[512,768]{1,0:T(8,128)(2,1)S(1)}, bf16[512,768]{1,0:T(8,128)(2,1)}, u32[]{:S(2)}) copy-start(bf16[512,768]{1,0:T(8,128)(2,1)} %q_hbm.1) | copy-start | bytes 2359300
  0.6 15.5 %copy-start.3 = (s32[512]{0:T(512)S(1)}, s32[512]{0:T(512)}, u32[]{:S(2)}) copy-start(s32[512]{0:T(512)} %param.5) | copy-start | bytes 6148
  2.6 33.4 %all-to-all-start = ((bf16[8,64,768]{2,1,0:T(8,128)(2,1)}), bf16[8,64,768]{2,1,0:T(8,128)(2,1)S(1)}, u32[]{:S(2)}, u32[]{:S(2)}) async-start(bf16[8,64,768]{2,1,0:T(8,128)(2,1)} %shard_map.50), calls=%async_computation | async-start | bytes 1572864 | tf_op jit(solution)/shard_map/all_to_all | solution.py:222
  12.9 13.9 %collective-permute-start = (bf16[512,768]{1,0:T(8,128)(2,1)S(1)}, bf16[512,768]{1,0:T(8,128)(2,1)S(1)}, u32[]{:S(2)}, u32[]{:S(2)}) collective-permute-start(bf16[512,768]{1,0:T(8,128)(2,1)S(1)} %copy-done), channel_id=1, source_target_pairs={{0,386},{1,3},{2,0},{3,129},{128,2},{129,131},{130,128},{131,257},... | collective-permute-start | bytes 2359304 | tf_op jit(solution)/shard_map/ppermute | solution.py:32
  16.2 10.6 %collective-permute-start.1 = (s32[1,512]{1,0:T(1,128)S(1)}, s32[1,512]{1,0:T(1,128)S(1)}, u32[]{:S(2)}, u32[]{:S(2)}) collective-permute-start(s32[1,512]{1,0:T(1,128)S(1)} %bitcast.14), channel_id=1, source_target_pairs={{0,386},{1,3},{2,0},{3,129},{128,2},{129,131},{130,128},{131,257},... | collective-permute-start | bytes 6152 | tf_op jit(solution)/shard_map/ppermute | solution.py:32
  36.0 19.8 %copy-start.1 = (bf16[8,64,768]{2,1,0:T(8,128)(2,1)}, bf16[8,64,768]{2,1,0:T(8,128)(2,1)S(1)}, u32[]{:S(2)}) copy-start(bf16[8,64,768]{2,1,0:T(8,128)(2,1)S(1)} %all-to-all-done) | copy-start | bytes 2359300
  36.0 14.0 %collective-permute-start.3 = (bf16[512,768]{1,0:T(8,128)(2,1)S(1)}, bf16[512,768]{1,0:T(8,128)(2,1)}, u32[]{:S(2)}, u32[]{:S(2)}) collective-permute-start(bf16[512,768]{1,0:T(8,128)(2,1)S(1)} %bitcast.10), channel_id=1, source_target_pairs={{0,386},{1,3},{2,0},{3,129},{128,2},{129,131},{130,128},{131,257},... | collective-permute-start | bytes 2359304 | tf_op jit(solution)/shard_map/ppermute | solution.py:32
  39.3 12.8 %collective-permute-start.2 = (bf16[512,768]{1,0:T(8,128)(2,1)S(1)}, bf16[512,768]{1,0:T(8,128)(2,1)S(1)}, u32[]{:S(2)}, u32[]{:S(2)}) collective-permute-start(bf16[512,768]{1,0:T(8,128)(2,1)S(1)} %bitcast.11), channel_id=1, source_target_pairs={{0,1},{1,0},{2,3},{3,2},{4,5},{5,4},{6,7},{7,6},{8,9},{9,8},{10,11... | collective-permute-start | bytes 2359304 | tf_op jit(solution)/shard_map/ppermute | solution.py:24
  50.0 17.5 %collective-permute-start.4 = (bf16[512,768]{1,0:T(8,128)(2,1)}, bf16[512,768]{1,0:T(8,128)(2,1)}, u32[]{:S(2)}, u32[]{:S(2)}) collective-permute-start(bf16[512,768]{1,0:T(8,128)(2,1)} %collective-permute-done.3.side_hbm), channel_id=1, source_target_pairs={{0,1},{1,0},{2,3},{3,2},{4,5},{5,4},{6,7},{7,6},{8,9},{9,8},{10,11... | collective-permute-start | bytes 2359304 | tf_op jit(solution)/shard_map/ppermute | solution.py:24
  52.0 3.8 %copy-start.2 = (bf16[512,768]{1,0:T(8,128)(2,1)}, bf16[512,768]{1,0:T(8,128)(2,1)S(1)}, u32[]{:S(2)}) copy-start(bf16[512,768]{1,0:T(8,128)(2,1)S(1)} %collective-permute-done.2.b_ref.b_hbm) | copy-start | bytes 2359300
  55.8 17.7 %all-to-all-start.1 = ((f32[32,1,1024]{2,1,0:T(1,128)}), f32[32,1,1024]{2,1,0:T(1,128)S(1)}, u32[]{:S(2)}, u32[]{:S(2)}) async-start(f32[32,1,1024]{2,1,0:T(1,128)} %get-tuple-element.23), calls=%async_computation.1 | async-start | bytes 262144 | tf_op jit(solution)/shard_map/all_to_all | solution.py:236
  91.2 11.7 %collective-permute-start.5 = (bf16[48,512]{1,0:T(8,128)(2,1)S(1)}, bf16[48,512]{1,0:T(8,128)(2,1)S(1)}, u32[]{:S(2)}, u32[]{:S(2)}) collective-permute-start(bf16[48,512]{1,0:T(8,128)(2,1)S(1)} %get-tuple-element.34), channel_id=1, source_target_pairs={{0,128},{128,256},{256,384},{384,0},{1,129},{129,257},{257,385},{3... | collective-permute-start | bytes 147464 | tf_op jit(solution)/shard_map/ppermute | solution.py:274
  94.3 9.9 %collective-permute-start.6 = (bf16[48,512]{1,0:T(8,128)(2,1)S(1)}, bf16[48,512]{1,0:T(8,128)(2,1)S(1)}, u32[]{:S(2)}, u32[]{:S(2)}) collective-permute-start(bf16[48,512]{1,0:T(8,128)(2,1)S(1)} %get-tuple-element.35), channel_id=1, source_target_pairs={{0,256},{128,384},{256,0},{384,128},{1,257},{129,385},{257,1},{385... | collective-permute-start | bytes 147464 | tf_op jit(solution)/shard_map/ppermute | solution.py:274
  101.0 8.6 %collective-permute-start.7 = (bf16[48,512]{1,0:T(8,128)(2,1)S(1)}, bf16[48,512]{1,0:T(8,128)(2,1)S(1)}, u32[]{:S(2)}, u32[]{:S(2)}) collective-permute-start(bf16[48,512]{1,0:T(8,128)(2,1)S(1)} %get-tuple-element.36), channel_id=1, source_target_pairs={{0,384},{128,0},{256,128},{384,256},{1,385},{129,1},{257,129},{385... | collective-permute-start | bytes 147464 | tf_op jit(solution)/shard_map/ppermute | solution.py:274

commit v12 on v10

--- a/solution.py
+++ b/solution.py
@@ -27,8 +27,8 @@
 def to_sides(x, ny):
     perm = []
     for y in range(ny):
-        perm.append((2 * y, 2 * ((y - 1) % ny)))
-        perm.append((2 * y + 1, 2 * ((y + 1) % ny) + 1))
+        perm.append((2 * y, 2 * ((y + 1) % ny)))
+        perm.append((2 * y + 1, 2 * ((y - 1) % ny) + 1))
     return lax.ppermute(x, LANE, perm)
 
 
@@ -193,7 +193,7 @@
         return ((((yy >> 1) * nx + x) * nz * 2 + (yy & 1)) * 2 + cc) * rows
 
     base = jnp.stack(
-        [base_of(y, c), base_of(y, 1 - c), base_of(y + 1 - 2 * c, c), base_of(y - 1 + 2 * c, 1 - c), y & 1]
+        [base_of(y, c), base_of(y, 1 - c), base_of(y - 1 + 2 * c, c), base_of(y + 1 - 2 * c, 1 - c), y & 1]
     )
     pos = positive.reshape(1, count)
 

time: 107 us -> 109 us (1.019)
    all_to_all x1, starting transfers between devices: 10.2 us -> 11.4 us  [shards(): lax.all_to_all(stats, ('yl', *OUTER), split_axis=0, concat_axis=0, tiled=...]
where the time goes in v12:
time: 109 us; the launch traced here: 108 us
  starting transfers between devices  36 us (33%)
  blocking collectives  29.2 us (27%)
  waiting for transfers between devices  26.9 us (25%)
  Pallas kernels  15.1 us (14%)
    ppermute x3, waiting for transfers between devices, to_sides(): return lax.ppermute(x, LANE, perm)  15.5 us
    pallas_call x7, Pallas kernels, call(): return kernel(*operands)  15.1 us
    all_to_all x1, blocking collectives, shards(): got = lax.all_to_all(out, 'yh', split_axis=0, concat_axis=0, tiled=True)  15 us
    all_to_all x1, blocking collectives, shards(): got = lax.all_to_all(out, 'x', split_axis=0, concat_axis=0, tiled=True)  14.2 us
    all_to_all x1, starting transfers between devices, shards(): lax.all_to_all(stats, ('yl', *OUTER), split_axis=0, concat_axis=0, tiled=...  11.4 us
    ppermute x3, starting transfers between devices, to_sides(): return lax.ppermute(x, LANE, perm)  10.4 us
    all_to_all x1, starting transfers between devices, shards(): lax.all_to_all(copies, 'z', split_axis=0, concat_axis=0, tiled=True)  10.3 us
    all_to_all x1, waiting for transfers between devices, shards(): lax.all_to_all(copies, 'z', split_axis=0, concat_axis=0, tiled=True)  9.2 us
  transfers between devices with their start and end apart: 7, of which 4 were waited for; matrix products, arithmetic and copies ran while one was open for 0% of the time, Pallas kernels for 11%

profile of v12, /device:TPU:8, one launch (start us, length us, event | category | flops | bytes accessed | tf_op | source)
XLA Modules:
  0.0 108.1 jit_solution(6609556951477045111)
XLA Ops:
  0.6 0.0 copy-start
  0.6 0.0 copy-start.3
  0.7 1.9 %shard_map.50 = bf16[8,64,768]{2,1,0:T(8,128)(2,1)} custom-call(bf16[64,768]{1,0:T(8,128)(2,1)} %x_hbm.1), custom_call_target="tpu_custom_call" | custom-call | bytes 4194304 | tf_op jit(solution)/shard_map/pallas_call | solution.py:177
  2.6 10.3 %all-to-all-start = ((bf16[8,64,768]{2,1,0:T(8,128)(2,1)}), bf16[8,64,768]{2,1,0:T(8,128)(2,1)S(1)}, u32[]{:S(2)}, u32[]{:S(2)}) async-start(bf16[8,64,768]{2,1,0:T(8,128)(2,1)} %shard_map.50), calls=%async_computation | async-start | bytes 1572864 | tf_op jit(solution)/shard_map/all_to_all | solution.py:210
  12.9 0.0 copy-done
  12.9 3.5 %collective-permute-start = (bf16[512,768]{1,0:T(8,128)(2,1)S(1)}, bf16[512,768]{1,0:T(8,128)(2,1)S(1)}, u32[]{:S(2)}, u32[]{:S(2)}) collective-permute-start(bf16[512,768]{1,0:T(8,128)(2,1)S(1)} %copy-done), channel_id=1, source_target_pairs={{0,2},{1,387},{2,128},{3,1},{128,130},{129,3},{130,256},{131,129},... | collective-permute-start | bytes 2359304 | tf_op jit(solution)/shard_map/ppermute | solution.py:32
  16.4 0.0 copy-done.3
  16.4 3.5 %collective-permute-start.1 = (s32[1,512]{1,0:T(1,128)S(1)}, s32[1,512]{1,0:T(1,128)S(1)}, u32[]{:S(2)}, u32[]{:S(2)}) collective-permute-start(s32[1,512]{1,0:T(1,128)S(1)} %bitcast.15), channel_id=1, source_target_pairs={{0,2},{1,387},{2,128},{3,1},{128,130},{129,3},{130,256},{131,129},... | collective-permute-start | bytes 6152 | tf_op jit(solution)/shard_map/ppermute | solution.py:32
  19.9 6.9 %collective-permute-done.1.posf_ref = s32[1,512]{1,0:T(1,128)S(1)} collective-permute-done((s32[1,512]{1,0:T(1,128)S(1)}, s32[1,512]{1,0:T(1,128)S(1)}, u32[]{:S(2)}, u32[]{:S(2)}) %collective-permute-start.1) | collective-permute-done | bytes 2080 | tf_op jit(solution)/shard_map/ppermute | solution.py:32
  26.8 0.0 collective-permute-done.qf_ref
  26.8 9.2 %all-to-all-done = bf16[8,64,768]{2,1,0:T(8,128)(2,1)S(1)} async-done(((bf16[8,64,768]{2,1,0:T(8,128)(2,1)}), bf16[8,64,768]{2,1,0:T(8,128)(2,1)S(1)}, u32[]{:S(2)}, u32[]{:S(2)}) %all-to-all-start) | async-done | bytes 786464 | tf_op jit(solution)/shard_map/all_to_all | solution.py:210
  36.0 0.0 copy-start.1
  36.0 3.5 %collective-permute-start.3 = (bf16[512,768]{1,0:T(8,128)(2,1)S(1)}, bf16[512,768]{1,0:T(8,128)(2,1)}, u32[]{:S(2)}, u32[]{:S(2)}) collective-permute-start(bf16[512,768]{1,0:T(8,128)(2,1)S(1)} %bitcast.10), channel_id=1, source_target_pairs={{0,2},{1,387},{2,128},{3,1},{128,130},{129,3},{130,256},{131,129},... | collective-permute-start | bytes 2359304 | tf_op jit(solution)/shard_map/ppermute | solution.py:32
  39.5 1.9 %collective-permute-start.2 = (bf16[512,768]{1,0:T(8,128)(2,1)S(1)}, bf16[512,768]{1,0:T(8,128)(2,1)S(1)}, u32[]{:S(2)}, u32[]{:S(2)}) collective-permute-start(bf16[512,768]{1,0:T(8,128)(2,1)S(1)} %bitcast.11), channel_id=1, source_target_pairs={{0,1},{1,0},{2,3},{3,2},{4,5},{5,4},{6,7},{7,6},{8,9},{9,8},{10,11... | collective-permute-start | bytes 2359304 | tf_op jit(solution)/shard_map/ppermute | solution.py:24
  41.5 8.6 %collective-permute-done.3.side_hbm = bf16[512,768]{1,0:T(8,128)(2,1)} collective-permute-done((bf16[512,768]{1,0:T(8,128)(2,1)S(1)}, bf16[512,768]{1,0:T(8,128)(2,1)}, u32[]{:S(2)}, u32[]{:S(2)}) %collective-permute-start.3) | collective-permute-done | bytes 786464 | tf_op jit(solution)/shard_map/ppermute | solution.py:32
  50.0 1.9 %collective-permute-start.4 = (bf16[512,768]{1,0:T(8,128)(2,1)}, bf16[512,768]{1,0:T(8,128)(2,1)}, u32[]{:S(2)}, u32[]{:S(2)}) collective-permute-start(bf16[512,768]{1,0:T(8,128)(2,1)} %collective-permute-done.3.side_hbm), channel_id=1, source_target_pairs={{0,1},{1,0},{2,3},{3,2},{4,5},{5,4},{6,7},{7,6},{8,9},{9,8},{10,11... | collective-permute-start | bytes 2359304 | tf_op jit(solution)/shard_map/ppermute | solution.py:24
  52.0 0.1 stack.23.base_ref
  52.1 0.0 collective-permute-done.2.b_ref.b_hbm
  52.1 0.0 copy-start.2
  52.1 3.8 %shard_map.51 = (f32[8,512]{1,0:T(8,128)S(1)}, bf16[1024,512]{1,0:T(8,128)(2,1)}, f32[32,1,1024]{2,1,0:T(1,128)}) custom-call(s32[5]{0:T(128)S(1)} %stack.23.base_ref, bf16[512,768]{1,0:T(8,128)(2,1)S(1)} %bitcast.12, bf16[512,768]{1,0:T(8,128)(2,1)S(1)} %collective-permute-done.2.b_ref.b_hbm, bf16[512,768]{1,0:T(8,128)(2,1)S(1)} %copy-done, ...), custom_call_target="tpu_custom_call" | custom-call | flops 1610612736 | bytes 4194304 | tf_op jit(solution)/shard_map/pallas_call | solution.py:177
  55.8 0.0 copy-done.1
  55.8 0.0 copy-done.2
  55.8 11.4 %all-to-all-start.1 = ((f32[32,1,1024]{2,1,0:T(1,128)}), f32[32,1,1024]{2,1,0:T(1,128)S(1)}, u32[]{:S(2)}, u32[]{:S(2)}) async-start(f32[32,1,1024]{2,1,0:T(1,128)} %get-tuple-element.19), calls=%async_computation.1 | async-start | bytes 262144 | tf_op jit(solution)/shard_map/all_to_all | solution.py:224
  67.2 2.0 %shard_map.52 = (bf16[512,768]{1,0:T(8,128)(2,1)S(1)}, bf16[512,768]{1,0:T(8,128)(2,1)S(1)}, f32[512,512]{1,0:T(8,128)S(1)}) custom-call(bf16[512,768]{1,0:T(8,128)(2,1)} %q_hbm.1, bf16[512,768]{1,0:T(8,128)(2,1)} %collective-permute-done.3.side_hbm), custom_call_target="tpu_custom_call" | custom-call | flops 402653184 | bytes 4194304 | tf_op jit(solution)/shard_map/pallas_call | solution.py:177
  69.2 0.0 collective-permute-done.4.side2_ref
  69.3 6.0 %shard_map.53 = (f32[8,512]{1,0:T(8,128)S(1)}, f32[768,512]{1,0:T(8,128)S(1)}, bf16[768,512]{1,0:T(8,128)(2,1)S(1)}) custom-call(s32[5]{0:T(128)S(1)} %stack.23.base_ref, bf16[512,768]{1,0:T(8,128)(2,1)} %bitcast.13, bf16[512,768]{1,0:T(8,128)(2,1)} %copy-done.2, bf16[1024,512]{1,0:T(8,128)(2,1)} %get-tuple-element.20.wo_hbm, ...), custom_call_target="tpu_custom_call" | custom-call | flops 4026531840 | bytes 4194304 | tf_op jit(solution)/shard_map/pallas_call | solution.py:177
  75.3 2.3 %all-to-all-done.1.every_ref = f32[32,1,1024]{2,1,0:T(1,128)S(1)} async-done(((f32[32,1,1024]{2,1,0:T(1,128)}), f32[32,1,1024]{2,1,0:T(1,128)S(1)}, u32[]{:S(2)}, u32[]{:S(2)}) %all-to-all-start.1) | async-done | bytes 131104 | tf_op jit(solution)/shard_map/all_to_all | solution.py:224
  77.5 0.6 shard_map.54
  78.2 14.2 %all_to_all.20.got_ref = bf16[4,192,512]{2,1,0:T(8,128)(2,1)S(1)} all-to-all(bf16[4,192,512]{2,1,0:T(8,128)(2,1)S(1)} %get-tuple-element.28), channel_id=1, replica_groups=mesh['yh'=4,'x'=4,'z'=8,'yl'=2,'c'=2] {'x'}, dimensions={0} | all-to-all | bytes 1572864 | tf_op jit(solution)/shard_map/all_to_all | solution.py:256
  92.4 0.1 shard_map.55
  92.5 15.0 %all_to_all.21.got_ref = bf16[4,48,512]{2,1,0:T(8,128)(2,1)S(1)} all-to-all(bf16[4,48,512]{2,1,0:T(8,128)(2,1)S(1)} %bitcast.14), channel_id=1, replica_groups=mesh['yh'=4,'x'=4,'z'=8,'yl'=2,'c'=2] {'yh'}, dimensions={0} | all-to-all | bytes 393216 | tf_op jit(solution)/shard_map/all_to_all | solution.py:261
  107.5 0.7 shard_map.56
Async XLA Ops:
  0.6 12.3 %copy-start = (bf16[512,768]{1,0:T(8,128)(2,1)S(1)}, bf16[512,768]{1,0:T(8,128)(2,1)}, u32[]{:S(2)}) copy-start(bf16[512,768]{1,0:T(8,128)(2,1)} %q_hbm.1) | copy-start | bytes 2359300
  0.6 15.8 %copy-start.3 = (s32[512]{0:T(512)S(1)}, s32[512]{0:T(512)}, u32[]{:S(2)}) copy-start(s32[512]{0:T(512)} %param.5) | copy-start | bytes 6148
  2.6 33.4 %all-to-all-start = ((bf16[8,64,768]{2,1,0:T(8,128)(2,1)}), bf16[8,64,768]{2,1,0:T(8,128)(2,1)S(1)}, u32[]{:S(2)}, u32[]{:S(2)}) async-start(bf16[8,64,768]{2,1,0:T(8,128)(2,1)} %shard_map.50), calls=%async_computation | async-start | bytes 1572864 | tf_op jit(solution)/shard_map/all_to_all | solution.py:210
  12.9 13.9 %collective-permute-start = (bf16[512,768]{1,0:T(8,128)(2,1)S(1)}, bf16[512,768]{1,0:T(8,128)(2,1)S(1)}, u32[]{:S(2)}, u32[]{:S(2)}) collective-permute-start(bf16[512,768]{1,0:T(8,128)(2,1)S(1)} %copy-done), channel_id=1, source_target_pairs={{0,2},{1,387},{2,128},{3,1},{128,130},{129,3},{130,256},{131,129},... | collective-permute-start | bytes 2359304 | tf_op jit(solution)/shard_map/ppermute | solution.py:32
  16.4 10.4 %collective-permute-start.1 = (s32[1,512]{1,0:T(1,128)S(1)}, s32[1,512]{1,0:T(1,128)S(1)}, u32[]{:S(2)}, u32[]{:S(2)}) collective-permute-start(s32[1,512]{1,0:T(1,128)S(1)} %bitcast.15), channel_id=1, source_target_pairs={{0,2},{1,387},{2,128},{3,1},{128,130},{129,3},{130,256},{131,129},... | collective-permute-start | bytes 6152 | tf_op jit(solution)/shard_map/ppermute | solution.py:32
  36.0 19.8 %copy-start.1 = (bf16[8,64,768]{2,1,0:T(8,128)(2,1)}, bf16[8,64,768]{2,1,0:T(8,128)(2,1)S(1)}, u32[]{:S(2)}) copy-start(bf16[8,64,768]{2,1,0:T(8,128)(2,1)S(1)} %all-to-all-done) | copy-start | bytes 2359300
  36.0 14.0 %collective-permute-start.3 = (bf16[512,768]{1,0:T(8,128)(2,1)S(1)}, bf16[512,768]{1,0:T(8,128)(2,1)}, u32[]{:S(2)}, u32[]{:S(2)}) collective-permute-start(bf16[512,768]{1,0:T(8,128)(2,1)S(1)} %bitcast.10), channel_id=1, source_target_pairs={{0,2},{1,387},{2,128},{3,1},{128,130},{129,3},{130,256},{131,129},... | collective-permute-start | bytes 2359304 | tf_op jit(solution)/shard_map/ppermute | solution.py:32
  39.5 12.5 %collective-permute-start.2 = (bf16[512,768]{1,0:T(8,128)(2,1)S(1)}, bf16[512,768]{1,0:T(8,128)(2,1)S(1)}, u32[]{:S(2)}, u32[]{:S(2)}) collective-permute-start(bf16[512,768]{1,0:T(8,128)(2,1)S(1)} %bitcast.11), channel_id=1, source_target_pairs={{0,1},{1,0},{2,3},{3,2},{4,5},{5,4},{6,7},{7,6},{8,9},{9,8},{10,11... | collective-permute-start | bytes 2359304 | tf_op jit(solution)/shard_map/ppermute | solution.py:24
  50.0 19.2 %collective-permute-start.4 = (bf16[512,768]{1,0:T(8,128)(2,1)}, bf16[512,768]{1,0:T(8,128)(2,1)}, u32[]{:S(2)}, u32[]{:S(2)}) collective-permute-start(bf16[512,768]{1,0:T(8,128)(2,1)} %collective-permute-done.3.side_hbm), channel_id=1, source_target_pairs={{0,1},{1,0},{2,3},{3,2},{4,5},{5,4},{6,7},{7,6},{8,9},{9,8},{10,11... | collective-permute-start | bytes 2359304 | tf_op jit(solution)/shard_map/ppermute | solution.py:24
  52.1 3.8 %copy-start.2 = (bf16[512,768]{1,0:T(8,128)(2,1)}, bf16[512,768]{1,0:T(8,128)(2,1)S(1)}, u32[]{:S(2)}) copy-start(bf16[512,768]{1,0:T(8,128)(2,1)S(1)} %collective-permute-done.2.b_ref.b_hbm) | copy-start | bytes 2359300
  55.8 21.7 %all-to-all-start.1 = ((f32[32,1,1024]{2,1,0:T(1,128)}), f32[32,1,1024]{2,1,0:T(1,128)S(1)}, u32[]{:S(2)}, u32[]{:S(2)}) async-start(f32[32,1,1024]{2,1,0:T(1,128)} %get-tuple-element.19), calls=%async_computation.1 | async-start | bytes 262144 | tf_op jit(solution)/shard_map/all_to_all | solution.py:224

commit v13 on v12

--- a/solution.py
+++ b/solution.py
@@ -139,12 +139,9 @@
     loss_ref[...] = whole - ps
 
 
-def copy_kernel(x_hbm, out_hbm, x_ref, sems):
+def copy_kernel(x_hbm, out_hbm, sems):
     n = out_hbm.shape[0]
-    first = pltpu.make_async_copy(x_hbm, x_ref, sems.at[n])
-    first.start()
-    first.wait()
-    copies = [pltpu.make_async_copy(x_ref, out_hbm.at[i], sems.at[i]) for i in range(n)]
+    copies = [pltpu.make_async_copy(x_hbm, out_hbm.at[i], sems.at[i]) for i in range(n)]
     for copy in copies:
         copy.start()
     for copy in copies:
@@ -203,7 +200,7 @@
         copy_kernel,
         [((nz, rows, width), BF16)],
         (passages,),
-        [((rows, width), BF16), pltpu.SemaphoreType.DMA((nz + 1,))],
+        [pltpu.SemaphoreType.DMA((nz,))],
         hbm_in=(0,),
         hbm_out=(0,),
     )

time: 109 us -> 132 us (1.21)
  Pallas kernels: 15.1 us -> 38.1 us
    pallas_call x7, Pallas kernels: 15.1 us -> 38.1 us  [call(): return kernel(*operands)]
  transfers between devices with their start and end apart: 7 -> 7, of which waited for: 4 -> 4; matrix products, arithmetic and copies ran while one was open for 0% -> 0% of each run, Pallas kernels for 11% -> 9%
where the time goes in v13:
time: 132 us; the launch traced here: 131 us
  Pallas kernels  38.1 us (29%)
  starting transfers between devices  36 us (27%)
  blocking collectives  29.2 us (22%)
  waiting for transfers between devices  26.9 us (20%)
    pallas_call x7, Pallas kernels, call(): return kernel(*operands)  38.1 us
    ppermute x3, waiting for transfers between devices, to_sides(): return lax.ppermute(x, LANE, perm)  15.5 us
    all_to_all x1, blocking collectives, shards(): got = lax.all_to_all(out, 'yh', split_axis=0, concat_axis=0, tiled=True)  15 us
    all_to_all x1, blocking collectives, shards(): got = lax.all_to_all(out, 'x', split_axis=0, concat_axis=0, tiled=True)  14.2 us
    all_to_all x1, starting transfers between devices, shards(): lax.all_to_all(stats, ('yl', *OUTER), split_axis=0, concat_axis=0, tiled=...  11.4 us
    ppermute x3, starting transfers between devices, to_sides(): return lax.ppermute(x, LANE, perm)  10.4 us
    all_to_all x1, starting transfers between devices, shards(): lax.all_to_all(copies, 'z', split_axis=0, concat_axis=0, tiled=True)  10.3 us
    all_to_all x1, waiting for transfers between devices, shards(): lax.all_to_all(copies, 'z', split_axis=0, concat_axis=0, tiled=True)  9.2 us
  transfers between devices with their start and end apart: 7, of which 4 were waited for; matrix products, arithmetic and copies ran while one was open for 0% of the time, Pallas kernels for 9%

profile of v13, /device:TPU:8, one launch (start us, length us, event | category | flops | bytes accessed | tf_op | source)
XLA Modules:
  0.0 131.2 jit_solution(13271241701042946218)
XLA Ops:
  0.6 0.0 copy-start
  0.6 0.0 copy-start.3
  0.7 25.0 %shard_map.50 = bf16[8,64,768]{2,1,0:T(8,128)(2,1)} custom-call(bf16[64,768]{1,0:T(8,128)(2,1)} %x_hbm.1), custom_call_target="tpu_custom_call" | custom-call | bytes 4194304 | tf_op jit(solution)/shard_map/pallas_call | solution.py:174
  25.7 10.3 %all-to-all-start = ((bf16[8,64,768]{2,1,0:T(8,128)(2,1)}), bf16[8,64,768]{2,1,0:T(8,128)(2,1)S(1)}, u32[]{:S(2)}, u32[]{:S(2)}) async-start(bf16[8,64,768]{2,1,0:T(8,128)(2,1)} %shard_map.50), calls=%async_computation | async-start | bytes 1572864 | tf_op jit(solution)/shard_map/all_to_all | solution.py:207
  36.0 0.0 copy-done
  36.0 3.5 %collective-permute-start = (bf16[512,768]{1,0:T(8,128)(2,1)S(1)}, bf16[512,768]{1,0:T(8,128)(2,1)S(1)}, u32[]{:S(2)}, u32[]{:S(2)}) collective-permute-start(bf16[512,768]{1,0:T(8,128)(2,1)S(1)} %copy-done), channel_id=1, source_target_pairs={{0,2},{1,387},{2,128},{3,1},{128,130},{129,3},{130,256},{131,129},... | collective-permute-start | bytes 2359304 | tf_op jit(solution)/shard_map/ppermute | solution.py:32
  39.5 0.0 copy-done.3
  39.5 3.5 %collective-permute-start.1 = (s32[1,512]{1,0:T(1,128)S(1)}, s32[1,512]{1,0:T(1,128)S(1)}, u32[]{:S(2)}, u32[]{:S(2)}) collective-permute-start(s32[1,512]{1,0:T(1,128)S(1)} %bitcast.15), channel_id=1, source_target_pairs={{0,2},{1,387},{2,128},{3,1},{128,130},{129,3},{130,256},{131,129},... | collective-permute-start | bytes 6152 | tf_op jit(solution)/shard_map/ppermute | solution.py:32
  43.0 6.9 %collective-permute-done.1.posf_ref = s32[1,512]{1,0:T(1,128)S(1)} collective-permute-done((s32[1,512]{1,0:T(1,128)S(1)}, s32[1,512]{1,0:T(1,128)S(1)}, u32[]{:S(2)}, u32[]{:S(2)}) %collective-permute-start.1) | collective-permute-done | bytes 2080 | tf_op jit(solution)/shard_map/ppermute | solution.py:32
  49.9 0.0 collective-permute-done.qf_ref
  49.9 9.2 %all-to-all-done = bf16[8,64,768]{2,1,0:T(8,128)(2,1)S(1)} async-done(((bf16[8,64,768]{2,1,0:T(8,128)(2,1)}), bf16[8,64,768]{2,1,0:T(8,128)(2,1)S(1)}, u32[]{:S(2)}, u32[]{:S(2)}) %all-to-all-start) | async-done | bytes 786464 | tf_op jit(solution)/shard_map/all_to_all | solution.py:207
  59.1 0.0 copy-start.1
  59.1 3.5 %collective-permute-start.3 = (bf16[512,768]{1,0:T(8,128)(2,1)S(1)}, bf16[512,768]{1,0:T(8,128)(2,1)}, u32[]{:S(2)}, u32[]{:S(2)}) collective-permute-start(bf16[512,768]{1,0:T(8,128)(2,1)S(1)} %bitcast.10), channel_id=1, source_target_pairs={{0,2},{1,387},{2,128},{3,1},{128,130},{129,3},{130,256},{131,129},... | collective-permute-start | bytes 2359304 | tf_op jit(solution)/shard_map/ppermute | solution.py:32
  62.6 1.9 %collective-permute-start.2 = (bf16[512,768]{1,0:T(8,128)(2,1)S(1)}, bf16[512,768]{1,0:T(8,128)(2,1)S(1)}, u32[]{:S(2)}, u32[]{:S(2)}) collective-permute-start(bf16[512,768]{1,0:T(8,128)(2,1)S(1)} %bitcast.11), channel_id=1, source_target_pairs={{0,1},{1,0},{2,3},{3,2},{4,5},{5,4},{6,7},{7,6},{8,9},{9,8},{10,11... | collective-permute-start | bytes 2359304 | tf_op jit(solution)/shard_map/ppermute | solution.py:24
  64.5 8.6 %collective-permute-done.3.side_hbm = bf16[512,768]{1,0:T(8,128)(2,1)} collective-permute-done((bf16[512,768]{1,0:T(8,128)(2,1)S(1)}, bf16[512,768]{1,0:T(8,128)(2,1)}, u32[]{:S(2)}, u32[]{:S(2)}) %collective-permute-start.3) | collective-permute-done | bytes 786464 | tf_op jit(solution)/shard_map/ppermute | solution.py:32
  73.1 1.9 %collective-permute-start.4 = (bf16[512,768]{1,0:T(8,128)(2,1)}, bf16[512,768]{1,0:T(8,128)(2,1)}, u32[]{:S(2)}, u32[]{:S(2)}) collective-permute-start(bf16[512,768]{1,0:T(8,128)(2,1)} %collective-permute-done.3.side_hbm), channel_id=1, source_target_pairs={{0,1},{1,0},{2,3},{3,2},{4,5},{5,4},{6,7},{7,6},{8,9},{9,8},{10,11... | collective-permute-start | bytes 2359304 | tf_op jit(solution)/shard_map/ppermute | solution.py:24
  75.0 0.1 stack.23.base_ref
  75.1 0.0 collective-permute-done.2.b_ref.b_hbm
  75.1 0.0 copy-start.2
  75.1 3.7 %shard_map.51 = (f32[8,512]{1,0:T(8,128)S(1)}, bf16[1024,512]{1,0:T(8,128)(2,1)}, f32[32,1,1024]{2,1,0:T(1,128)}) custom-call(s32[5]{0:T(128)S(1)} %stack.23.base_ref, bf16[512,768]{1,0:T(8,128)(2,1)S(1)} %bitcast.12, bf16[512,768]{1,0:T(8,128)(2,1)S(1)} %collective-permute-done.2.b_ref.b_hbm, bf16[512,768]{1,0:T(8,128)(2,1)S(1)} %copy-done, ...), custom_call_target="tpu_custom_call" | custom-call | flops 1610612736 | bytes 4194304 | tf_op jit(solution)/shard_map/pallas_call | solution.py:174
  78.9 0.0 copy-done.1
  78.9 0.0 copy-done.2
  78.9 11.4 %all-to-all-start.1 = ((f32[32,1,1024]{2,1,0:T(1,128)}), f32[32,1,1024]{2,1,0:T(1,128)S(1)}, u32[]{:S(2)}, u32[]{:S(2)}) async-start(f32[32,1,1024]{2,1,0:T(1,128)} %get-tuple-element.19), calls=%async_computation.1 | async-start | bytes 262144 | tf_op jit(solution)/shard_map/all_to_all | solution.py:221
  90.3 2.0 %shard_map.52 = (bf16[512,768]{1,0:T(8,128)(2,1)S(1)}, bf16[512,768]{1,0:T(8,128)(2,1)S(1)}, f32[512,512]{1,0:T(8,128)S(1)}) custom-call(bf16[512,768]{1,0:T(8,128)(2,1)} %q_hbm.1, bf16[512,768]{1,0:T(8,128)(2,1)} %collective-permute-done.3.side_hbm), custom_call_target="tpu_custom_call" | custom-call | flops 402653184 | bytes 4194304 | tf_op jit(solution)/shard_map/pallas_call | solution.py:174
  92.3 0.0 collective-permute-done.4.side2_ref
  92.3 6.0 %shard_map.53 = (f32[8,512]{1,0:T(8,128)S(1)}, f32[768,512]{1,0:T(8,128)S(1)}, bf16[768,512]{1,0:T(8,128)(2,1)S(1)}) custom-call(s32[5]{0:T(128)S(1)} %stack.23.base_ref, bf16[512,768]{1,0:T(8,128)(2,1)} %bitcast.13, bf16[512,768]{1,0:T(8,128)(2,1)} %copy-done.2, bf16[1024,512]{1,0:T(8,128)(2,1)} %get-tuple-element.20.wo_hbm, ...), custom_call_target="tpu_custom_call" | custom-call | flops 4026531840 | bytes 4194304 | tf_op jit(solution)/shard_map/pallas_call | solution.py:174
  98.3 2.3 %all-to-all-done.1.every_ref = f32[32,1,1024]{2,1,0:T(1,128)S(1)} async-done(((f32[32,1,1024]{2,1,0:T(1,128)}), f32[32,1,1024]{2,1,0:T(1,128)S(1)}, u32[]{:S(2)}, u32[]{:S(2)}) %all-to-all-start.1) | async-done | bytes 131104 | tf_op jit(solution)/shard_map/all_to_all | solution.py:221
  100.6 0.6 shard_map.54
  101.2 14.2 %all_to_all.20.got_ref = bf16[4,192,512]{2,1,0:T(8,128)(2,1)S(1)} all-to-all(bf16[4,192,512]{2,1,0:T(8,128)(2,1)S(1)} %get-tuple-element.28), channel_id=1, replica_groups=mesh['yh'=4,'x'=4,'z'=8,'yl'=2,'c'=2] {'x'}, dimensions={0} | all-to-all | bytes 1572864 | tf_op jit(solution)/shard_map/all_to_all | solution.py:253
  115.4 0.1 shard_map.55
  115.5 15.0 %all_to_all.21.got_ref = bf16[4,48,512]{2,1,0:T(8,128)(2,1)S(1)} all-to-all(bf16[4,48,512]{2,1,0:T(8,128)(2,1)S(1)} %bitcast.14), channel_id=1, replica_groups=mesh['yh'=4,'x'=4,'z'=8,'yl'=2,'c'=2] {'yh'}, dimensions={0} | all-to-all | bytes 393216 | tf_op jit(solution)/shard_map/all_to_all | solution.py:258
  130.5 0.7 shard_map.56
Async XLA Ops:
  0.6 35.4 %copy-start = (bf16[512,768]{1,0:T(8,128)(2,1)S(1)}, bf16[512,768]{1,0:T(8,128)(2,1)}, u32[]{:S(2)}) copy-start(bf16[512,768]{1,0:T(8,128)(2,1)} %q_hbm.1) | copy-start | bytes 2359300
  0.6 38.8 %copy-start.3 = (s32[512]{0:T(512)S(1)}, s32[512]{0:T(512)}, u32[]{:S(2)}) copy-start(s32[512]{0:T(512)} %param.5) | copy-start | bytes 6148
  25.7 33.4 %all-to-all-start = ((bf16[8,64,768]{2,1,0:T(8,128)(2,1)}), bf16[8,64,768]{2,1,0:T(8,128)(2,1)S(1)}, u32[]{:S(2)}, u32[]{:S(2)}) async-start(bf16[8,64,768]{2,1,0:T(8,128)(2,1)} %shard_map.50), calls=%async_computation | async-start | bytes 1572864 | tf_op jit(solution)/shard_map/all_to_all | solution.py:207
  36.0 13.9 %collective-permute-start = (bf16[512,768]{1,0:T(8,128)(2,1)S(1)}, bf16[512,768]{1,0:T(8,128)(2,1)S(1)}, u32[]{:S(2)}, u32[]{:S(2)}) collective-permute-start(bf16[512,768]{1,0:T(8,128)(2,1)S(1)} %copy-done), channel_id=1, source_target_pairs={{0,2},{1,387},{2,128},{3,1},{128,130},{129,3},{130,256},{131,129},... | collective-permute-start | bytes 2359304 | tf_op jit(solution)/shard_map/ppermute | solution.py:32
  39.5 10.4 %collective-permute-start.1 = (s32[1,512]{1,0:T(1,128)S(1)}, s32[1,512]{1,0:T(1,128)S(1)}, u32[]{:S(2)}, u32[]{:S(2)}) collective-permute-start(s32[1,512]{1,0:T(1,128)S(1)} %bitcast.15), channel_id=1, source_target_pairs={{0,2},{1,387},{2,128},{3,1},{128,130},{129,3},{130,256},{131,129},... | collective-permute-start | bytes 6152 | tf_op jit(solution)/shard_map/ppermute | solution.py:32
  59.1 19.8 %copy-start.1 = (bf16[8,64,768]{2,1,0:T(8,128)(2,1)}, bf16[8,64,768]{2,1,0:T(8,128)(2,1)S(1)}, u32[]{:S(2)}) copy-start(bf16[8,64,768]{2,1,0:T(8,128)(2,1)S(1)} %all-to-all-done) | copy-start | bytes 2359300
  59.1 14.0 %collective-permute-start.3 = (bf16[512,768]{1,0:T(8,128)(2,1)S(1)}, bf16[512,768]{1,0:T(8,128)(2,1)}, u32[]{:S(2)}, u32[]{:S(2)}) collective-permute-start(bf16[512,768]{1,0:T(8,128)(2,1)S(1)} %bitcast.10), channel_id=1, source_target_pairs={{0,2},{1,387},{2,128},{3,1},{128,130},{129,3},{130,256},{131,129},... | collective-permute-start | bytes 2359304 | tf_op jit(solution)/shard_map/ppermute | solution.py:32
  62.6 12.5 %collective-permute-start.2 = (bf16[512,768]{1,0:T(8,128)(2,1)S(1)}, bf16[512,768]{1,0:T(8,128)(2,1)S(1)}, u32[]{:S(2)}, u32[]{:S(2)}) collective-permute-start(bf16[512,768]{1,0:T(8,128)(2,1)S(1)} %bitcast.11), channel_id=1, source_target_pairs={{0,1},{1,0},{2,3},{3,2},{4,5},{5,4},{6,7},{7,6},{8,9},{9,8},{10,11... | collective-permute-start | bytes 2359304 | tf_op jit(solution)/shard_map/ppermute | solution.py:24
  73.1 19.2 %collective-permute-start.4 = (bf16[512,768]{1,0:T(8,128)(2,1)}, bf16[512,768]{1,0:T(8,128)(2,1)}, u32[]{:S(2)}, u32[]{:S(2)}) collective-permute-start(bf16[512,768]{1,0:T(8,128)(2,1)} %collective-permute-done.3.side_hbm), channel_id=1, source_target_pairs={{0,1},{1,0},{2,3},{3,2},{4,5},{5,4},{6,7},{7,6},{8,9},{9,8},{10,11... | collective-permute-start | bytes 2359304 | tf_op jit(solution)/shard_map/ppermute | solution.py:24
  75.1 3.8 %copy-start.2 = (bf16[512,768]{1,0:T(8,128)(2,1)}, bf16[512,768]{1,0:T(8,128)(2,1)S(1)}, u32[]{:S(2)}) copy-start(bf16[512,768]{1,0:T(8,128)(2,1)S(1)} %collective-permute-done.2.b_ref.b_hbm) | copy-start | bytes 2359300
  78.9 21.7 %all-to-all-start.1 = ((f32[32,1,1024]{2,1,0:T(1,128)}), f32[32,1,1024]{2,1,0:T(1,128)S(1)}, u32[]{:S(2)}, u32[]{:S(2)}) async-start(f32[32,1,1024]{2,1,0:T(1,128)} %get-tuple-element.19), calls=%async_computation.1 | async-start | bytes 262144 | tf_op jit(solution)/shard_map/all_to_all | solution.py:221

commit v14 on v12

--- a/solution.py
+++ b/solution.py
@@ -67,26 +67,27 @@
     return mix, chosen
 
 
-def stat_kernel(scale, rows, base_ref, a_ref, b_ref, q_ref, pos_ref, qf_ref, posf_ref, st_ref, w_hbm, out_ref, s_ref, w_ref, sem):
+def stat_kernel(scale, rows, base_ref, a_ref, b_ref, q_ref, pos_ref, qf_ref, posf_ref, st_ref, w_hbm, out_hbm, s_ref, w_ref, row_ref, sems):
     bases = (base_ref[0], base_ref[1])
-    pieces = []
-    for qq, pp in ((q_ref, pos_ref), (qf_ref, posf_ref)):
+    half = out_hbm.shape[0] // 2
+    lower = jnp.where(base_ref[4] == 0, 0, half)
+    copies = []
+    for i, (qq, pp) in enumerate(((q_ref, pos_ref), (qf_ref, posf_ref))):
         top, ps = statistics((a_ref, b_ref), bases, qq, pp, s_ref, rows)
         e = jnp.exp2((s_ref[...] - top) * (scale * LOG2E))
         total = jnp.sum(e, axis=0, keepdims=True)
-        if not pieces:
+        row_ref[i, :, :] = jnp.concatenate([top * scale + jnp.log(total), ps * scale], axis=1)
+        first = lower if i == 0 else half - lower
+        for k in range(half):
+            copies.append(pltpu.make_async_copy(row_ref.at[i], out_hbm.at[first + k], sems.at[i * half + k]))
+            copies[-1].start()
+        if i == 0:
             w_ref[...] = e.astype(BF16)
-            copy = pltpu.make_async_copy(w_ref, w_hbm, sem)
-            copy.start()
+            copies.append(pltpu.make_async_copy(w_ref, w_hbm, sems.at[2 * half]))
+            copies[-1].start()
             st_ref[0:1, :] = top
-        pieces.append(jnp.concatenate([top * scale + jnp.log(total), ps * scale], axis=1))
-    own, theirs = pieces
-    lower = base_ref[4] == 0
-    half = out_ref.shape[0] // 2
-    shape = (half, *own.shape)
-    out_ref[:half] = jnp.broadcast_to(jnp.where(lower, own, theirs)[None], shape)
-    out_ref[half:] = jnp.broadcast_to(jnp.where(lower, theirs, own)[None], shape)
-    copy.wait()
+    for copy in copies:
+        copy.wait()
 
 
 def side_kernel(q_hbm, side_hbm, q_ref, side_ref, s_ref, sems):
@@ -217,9 +218,14 @@
         functools.partial(stat_kernel, scale, rows),
         [((8, count), F32), ((2 * n, count), BF16), ((members, 1, 2 * count), F32)],
         (base, column, column2, queries, pos, theirs, pos_theirs),
-        [((2 * n, count), F32), ((2 * n, count), BF16), pltpu.SemaphoreType.DMA],
+        [
+            ((2 * n, count), F32),
+            ((2 * n, count), BF16),
+            ((2, 1, 2 * count), F32),
+            pltpu.SemaphoreType.DMA((members + 1,)),
+        ],
         4 * flops,
-        hbm_out=(1,),
+        hbm_out=(1, 2),
     )
     every = lax.all_to_all(stats, ("yl", *OUTER), split_axis=0, concat_axis=0, tiled=True)
     side2 = swapped(side)

time: 109 us -> 109 us (level)
  no operation moved by 1% of the time
where the time goes in v14:
time: 109 us; the launch traced here: 108 us
  starting transfers between devices  36 us (33%)
  blocking collectives  29.2 us (27%)
  waiting for transfers between devices  26.9 us (25%)
  Pallas kernels  15.4 us (14%)
    ppermute x3, waiting for transfers between devices, to_sides(): return lax.ppermute(x, LANE, perm)  15.5 us
    pallas_call x7, Pallas kernels, call(): return kernel(*operands)  15.4 us
    all_to_all x1, blocking collectives, shards(): got = lax.all_to_all(out, 'yh', split_axis=0, concat_axis=0, tiled=True)  15 us
    all_to_all x1, blocking collectives, shards(): got = lax.all_to_all(out, 'x', split_axis=0, concat_axis=0, tiled=True)  14.2 us
    all_to_all x1, starting transfers between devices, shards(): lax.all_to_all(stats, ('yl', *OUTER), split_axis=0, concat_axis=0, tiled=...  11.4 us
    ppermute x3, starting transfers between devices, to_sides(): return lax.ppermute(x, LANE, perm)  10.4 us
    all_to_all x1, starting transfers between devices, shards(): lax.all_to_all(copies, 'z', split_axis=0, concat_axis=0, tiled=True)  10.3 us
    all_to_all x1, waiting for transfers between devices, shards(): lax.all_to_all(copies, 'z', split_axis=0, concat_axis=0, tiled=True)  9.2 us
  transfers between devices with their start and end apart: 7, of which 4 were waited for; matrix products, arithmetic and copies ran while one was open for 0% of the time, Pallas kernels for 11%

profile of v14, /device:TPU:8, one launch (start us, length us, event | category | flops | bytes accessed | tf_op | source)
XLA Modules:
  0.0 108.4 jit_solution(7414758693954625174)
XLA Ops:
  0.6 0.0 copy-start
  0.6 0.0 copy-start.3
  0.7 1.9 %shard_map.50 = bf16[8,64,768]{2,1,0:T(8,128)(2,1)} custom-call(bf16[64,768]{1,0:T(8,128)(2,1)} %x_hbm.1), custom_call_target="tpu_custom_call" | custom-call | bytes 4194304 | tf_op jit(solution)/shard_map/pallas_call | solution.py:178
  2.6 10.3 %all-to-all-start = ((bf16[8,64,768]{2,1,0:T(8,128)(2,1)}), bf16[8,64,768]{2,1,0:T(8,128)(2,1)S(1)}, u32[]{:S(2)}, u32[]{:S(2)}) async-start(bf16[8,64,768]{2,1,0:T(8,128)(2,1)} %shard_map.50), calls=%async_computation | async-start | bytes 1572864 | tf_op jit(solution)/shard_map/all_to_all | solution.py:211
  12.9 0.0 copy-done
  12.9 3.5 %collective-permute-start = (bf16[512,768]{1,0:T(8,128)(2,1)S(1)}, bf16[512,768]{1,0:T(8,128)(2,1)S(1)}, u32[]{:S(2)}, u32[]{:S(2)}) collective-permute-start(bf16[512,768]{1,0:T(8,128)(2,1)S(1)} %copy-done), channel_id=1, source_target_pairs={{0,2},{1,387},{2,128},{3,1},{128,130},{129,3},{130,256},{131,129},... | collective-permute-start | bytes 2359304 | tf_op jit(solution)/shard_map/ppermute | solution.py:32
  16.4 0.0 copy-done.3
  16.4 3.5 %collective-permute-start.1 = (s32[1,512]{1,0:T(1,128)S(1)}, s32[1,512]{1,0:T(1,128)S(1)}, u32[]{:S(2)}, u32[]{:S(2)}) collective-permute-start(s32[1,512]{1,0:T(1,128)S(1)} %bitcast.15), channel_id=1, source_target_pairs={{0,2},{1,387},{2,128},{3,1},{128,130},{129,3},{130,256},{131,129},... | collective-permute-start | bytes 6152 | tf_op jit(solution)/shard_map/ppermute | solution.py:32
  19.9 6.9 %collective-permute-done.1.posf_ref = s32[1,512]{1,0:T(1,128)S(1)} collective-permute-done((s32[1,512]{1,0:T(1,128)S(1)}, s32[1,512]{1,0:T(1,128)S(1)}, u32[]{:S(2)}, u32[]{:S(2)}) %collective-permute-start.1) | collective-permute-done | bytes 2080 | tf_op jit(solution)/shard_map/ppermute | solution.py:32
  26.8 0.0 collective-permute-done.qf_ref
  26.8 9.2 %all-to-all-done = bf16[8,64,768]{2,1,0:T(8,128)(2,1)S(1)} async-done(((bf16[8,64,768]{2,1,0:T(8,128)(2,1)}), bf16[8,64,768]{2,1,0:T(8,128)(2,1)S(1)}, u32[]{:S(2)}, u32[]{:S(2)}) %all-to-all-start) | async-done | bytes 786464 | tf_op jit(solution)/shard_map/all_to_all | solution.py:211
  36.0 0.0 copy-start.1
  36.0 3.5 %collective-permute-start.3 = (bf16[512,768]{1,0:T(8,128)(2,1)S(1)}, bf16[512,768]{1,0:T(8,128)(2,1)}, u32[]{:S(2)}, u32[]{:S(2)}) collective-permute-start(bf16[512,768]{1,0:T(8,128)(2,1)S(1)} %bitcast.10), channel_id=1, source_target_pairs={{0,2},{1,387},{2,128},{3,1},{128,130},{129,3},{130,256},{131,129},... | collective-permute-start | bytes 2359304 | tf_op jit(solution)/shard_map/ppermute | solution.py:32
  39.5 1.9 %collective-permute-start.2 = (bf16[512,768]{1,0:T(8,128)(2,1)S(1)}, bf16[512,768]{1,0:T(8,128)(2,1)S(1)}, u32[]{:S(2)}, u32[]{:S(2)}) collective-permute-start(bf16[512,768]{1,0:T(8,128)(2,1)S(1)} %bitcast.11), channel_id=1, source_target_pairs={{0,1},{1,0},{2,3},{3,2},{4,5},{5,4},{6,7},{7,6},{8,9},{9,8},{10,11... | collective-permute-start | bytes 2359304 | tf_op jit(solution)/shard_map/ppermute | solution.py:24
  41.5 8.6 %collective-permute-done.3.side_hbm = bf16[512,768]{1,0:T(8,128)(2,1)} collective-permute-done((bf16[512,768]{1,0:T(8,128)(2,1)S(1)}, bf16[512,768]{1,0:T(8,128)(2,1)}, u32[]{:S(2)}, u32[]{:S(2)}) %collective-permute-start.3) | collective-permute-done | bytes 786464 | tf_op jit(solution)/shard_map/ppermute | solution.py:32
  50.0 1.9 %collective-permute-start.4 = (bf16[512,768]{1,0:T(8,128)(2,1)}, bf16[512,768]{1,0:T(8,128)(2,1)}, u32[]{:S(2)}, u32[]{:S(2)}) collective-permute-start(bf16[512,768]{1,0:T(8,128)(2,1)} %collective-permute-done.3.side_hbm), channel_id=1, source_target_pairs={{0,1},{1,0},{2,3},{3,2},{4,5},{5,4},{6,7},{7,6},{8,9},{9,8},{10,11... | collective-permute-start | bytes 2359304 | tf_op jit(solution)/shard_map/ppermute | solution.py:24
  52.0 0.1 stack.23.base_ref
  52.1 0.0 collective-permute-done.2.b_ref.b_hbm
  52.1 0.0 copy-start.2
  52.1 4.0 %shard_map.51 = (f32[8,512]{1,0:T(8,128)S(1)}, bf16[1024,512]{1,0:T(8,128)(2,1)}, f32[32,1,1024]{2,1,0:T(1,128)}) custom-call(s32[5]{0:T(128)S(1)} %stack.23.base_ref, bf16[512,768]{1,0:T(8,128)(2,1)S(1)} %bitcast.12, bf16[512,768]{1,0:T(8,128)(2,1)S(1)} %collective-permute-done.2.b_ref.b_hbm, bf16[512,768]{1,0:T(8,128)(2,1)S(1)} %copy-done, ...), custom_call_target="tpu_custom_call" | custom-call | flops 1610612736 | bytes 4194304 | tf_op jit(solution)/shard_map/pallas_call | solution.py:178
  56.1 0.0 copy-done.1
  56.1 0.0 copy-done.2
  56.1 11.4 %all-to-all-start.1 = ((f32[32,1,1024]{2,1,0:T(1,128)}), f32[32,1,1024]{2,1,0:T(1,128)S(1)}, u32[]{:S(2)}, u32[]{:S(2)}) async-start(f32[32,1,1024]{2,1,0:T(1,128)} %get-tuple-element.19), calls=%async_computation.1 | async-start | bytes 262144 | tf_op jit(solution)/shard_map/all_to_all | solution.py:230
  67.5 2.0 %shard_map.52 = (bf16[512,768]{1,0:T(8,128)(2,1)S(1)}, bf16[512,768]{1,0:T(8,128)(2,1)S(1)}, f32[512,512]{1,0:T(8,128)S(1)}) custom-call(bf16[512,768]{1,0:T(8,128)(2,1)} %q_hbm.1, bf16[512,768]{1,0:T(8,128)(2,1)} %collective-permute-done.3.side_hbm), custom_call_target="tpu_custom_call" | custom-call | flops 402653184 | bytes 4194304 | tf_op jit(solution)/shard_map/pallas_call | solution.py:178
  69.5 0.0 collective-permute-done.4.side2_ref
  69.5 6.0 %shard_map.53 = (f32[8,512]{1,0:T(8,128)S(1)}, f32[768,512]{1,0:T(8,128)S(1)}, bf16[768,512]{1,0:T(8,128)(2,1)S(1)}) custom-call(s32[5]{0:T(128)S(1)} %stack.23.base_ref, bf16[512,768]{1,0:T(8,128)(2,1)} %bitcast.13, bf16[512,768]{1,0:T(8,128)(2,1)} %copy-done.2, bf16[1024,512]{1,0:T(8,128)(2,1)} %get-tuple-element.20.wo_hbm, ...), custom_call_target="tpu_custom_call" | custom-call | flops 4026531840 | bytes 4194304 | tf_op jit(solution)/shard_map/pallas_call | solution.py:178
  75.5 2.3 %all-to-all-done.1.every_ref = f32[32,1,1024]{2,1,0:T(1,128)S(1)} async-done(((f32[32,1,1024]{2,1,0:T(1,128)}), f32[32,1,1024]{2,1,0:T(1,128)S(1)}, u32[]{:S(2)}, u32[]{:S(2)}) %all-to-all-start.1) | async-done | bytes 131104 | tf_op jit(solution)/shard_map/all_to_all | solution.py:230
  77.8 0.6 shard_map.54
  78.5 14.2 %all_to_all.20.got_ref = bf16[4,192,512]{2,1,0:T(8,128)(2,1)S(1)} all-to-all(bf16[4,192,512]{2,1,0:T(8,128)(2,1)S(1)} %get-tuple-element.28), channel_id=1, replica_groups=mesh['yh'=4,'x'=4,'z'=8,'yl'=2,'c'=2] {'x'}, dimensions={0} | all-to-all | bytes 1572864 | tf_op jit(solution)/shard_map/all_to_all | solution.py:262
  92.6 0.1 shard_map.55
  92.7 15.0 %all_to_all.21.got_ref = bf16[4,48,512]{2,1,0:T(8,128)(2,1)S(1)} all-to-all(bf16[4,48,512]{2,1,0:T(8,128)(2,1)S(1)} %bitcast.14), channel_id=1, replica_groups=mesh['yh'=4,'x'=4,'z'=8,'yl'=2,'c'=2] {'yh'}, dimensions={0} | all-to-all | bytes 393216 | tf_op jit(solution)/shard_map/all_to_all | solution.py:267
  107.8 0.7 shard_map.56
Async XLA Ops:
  0.6 12.3 %copy-start = (bf16[512,768]{1,0:T(8,128)(2,1)S(1)}, bf16[512,768]{1,0:T(8,128)(2,1)}, u32[]{:S(2)}) copy-start(bf16[512,768]{1,0:T(8,128)(2,1)} %q_hbm.1) | copy-start | bytes 2359300
  0.6 15.8 %copy-start.3 = (s32[512]{0:T(512)S(1)}, s32[512]{0:T(512)}, u32[]{:S(2)}) copy-start(s32[512]{0:T(512)} %param.5) | copy-start | bytes 6148
  2.6 33.4 %all-to-all-start = ((bf16[8,64,768]{2,1,0:T(8,128)(2,1)}), bf16[8,64,768]{2,1,0:T(8,128)(2,1)S(1)}, u32[]{:S(2)}, u32[]{:S(2)}) async-start(bf16[8,64,768]{2,1,0:T(8,128)(2,1)} %shard_map.50), calls=%async_computation | async-start | bytes 1572864 | tf_op jit(solution)/shard_map/all_to_all | solution.py:211
  12.9 13.9 %collective-permute-start = (bf16[512,768]{1,0:T(8,128)(2,1)S(1)}, bf16[512,768]{1,0:T(8,128)(2,1)S(1)}, u32[]{:S(2)}, u32[]{:S(2)}) collective-permute-start(bf16[512,768]{1,0:T(8,128)(2,1)S(1)} %copy-done), channel_id=1, source_target_pairs={{0,2},{1,387},{2,128},{3,1},{128,130},{129,3},{130,256},{131,129},... | collective-permute-start | bytes 2359304 | tf_op jit(solution)/shard_map/ppermute | solution.py:32
  16.4 10.4 %collective-permute-start.1 = (s32[1,512]{1,0:T(1,128)S(1)}, s32[1,512]{1,0:T(1,128)S(1)}, u32[]{:S(2)}, u32[]{:S(2)}) collective-permute-start(s32[1,512]{1,0:T(1,128)S(1)} %bitcast.15), channel_id=1, source_target_pairs={{0,2},{1,387},{2,128},{3,1},{128,130},{129,3},{130,256},{131,129},... | collective-permute-start | bytes 6152 | tf_op jit(solution)/shard_map/ppermute | solution.py:32
  36.0 20.1 %copy-start.1 = (bf16[8,64,768]{2,1,0:T(8,128)(2,1)}, bf16[8,64,768]{2,1,0:T(8,128)(2,1)S(1)}, u32[]{:S(2)}) copy-start(bf16[8,64,768]{2,1,0:T(8,128)(2,1)S(1)} %all-to-all-done) | copy-start | bytes 2359300
  36.0 14.0 %collective-permute-start.3 = (bf16[512,768]{1,0:T(8,128)(2,1)S(1)}, bf16[512,768]{1,0:T(8,128)(2,1)}, u32[]{:S(2)}, u32[]{:S(2)}) collective-permute-start(bf16[512,768]{1,0:T(8,128)(2,1)S(1)} %bitcast.10), channel_id=1, source_target_pairs={{0,2},{1,387},{2,128},{3,1},{128,130},{129,3},{130,256},{131,129},... | collective-permute-start | bytes 2359304 | tf_op jit(solution)/shard_map/ppermute | solution.py:32
  39.5 12.5 %collective-permute-start.2 = (bf16[512,768]{1,0:T(8,128)(2,1)S(1)}, bf16[512,768]{1,0:T(8,128)(2,1)S(1)}, u32[]{:S(2)}, u32[]{:S(2)}) collective-permute-start(bf16[512,768]{1,0:T(8,128)(2,1)S(1)} %bitcast.11), channel_id=1, source_target_pairs={{0,1},{1,0},{2,3},{3,2},{4,5},{5,4},{6,7},{7,6},{8,9},{9,8},{10,11... | collective-permute-start | bytes 2359304 | tf_op jit(solution)/shard_map/ppermute | solution.py:24
  50.0 19.5 %collective-permute-start.4 = (bf16[512,768]{1,0:T(8,128)(2,1)}, bf16[512,768]{1,0:T(8,128)(2,1)}, u32[]{:S(2)}, u32[]{:S(2)}) collective-permute-start(bf16[512,768]{1,0:T(8,128)(2,1)} %collective-permute-done.3.side_hbm), channel_id=1, source_target_pairs={{0,1},{1,0},{2,3},{3,2},{4,5},{5,4},{6,7},{7,6},{8,9},{9,8},{10,11... | collective-permute-start | bytes 2359304 | tf_op jit(solution)/shard_map/ppermute | solution.py:24
  52.1 4.1 %copy-start.2 = (bf16[512,768]{1,0:T(8,128)(2,1)}, bf16[512,768]{1,0:T(8,128)(2,1)S(1)}, u32[]{:S(2)}) copy-start(bf16[512,768]{1,0:T(8,128)(2,1)S(1)} %collective-permute-done.2.b_ref.b_hbm) | copy-start | bytes 2359300
  56.1 21.7 %all-to-all-start.1 = ((f32[32,1,1024]{2,1,0:T(1,128)}), f32[32,1,1024]{2,1,0:T(1,128)S(1)}, u32[]{:S(2)}, u32[]{:S(2)}) async-start(f32[32,1,1024]{2,1,0:T(1,128)} %get-tuple-element.19), calls=%async_computation.1 | async-start | bytes 262144 | tf_op jit(solution)/shard_map/all_to_all | solution.py:230

commit v15 on v12

--- a/solution.py
+++ b/solution.py
@@ -129,13 +129,7 @@
     whole = most + jnp.log(jnp.sum(jnp.exp(lse - most), axis=0, keepdims=True))
     ps = jnp.sum(every_ref[:, 0, count:], axis=0, keepdims=True)
     g = jnp.exp(st_ref[0:1, :] * scale - whole)
-    out = (m_ref[...] * g - c_ref[...].astype(F32)).astype(BF16)
-    nx, width, _ = out_ref.shape
-    piece = width // 4
-    for i in range(nx):
-        for j in range(4):
-            at = (j * nx + i) * piece
-            out_ref[i, j * piece : (j + 1) * piece, :] = out[at : at + piece]
+    out_ref[...] = (m_ref[...] * g - c_ref[...].astype(F32)).astype(BF16)
     loss_ref[...] = whole - ps
 
 
@@ -249,17 +243,12 @@
         hbm_in=(1, 2, 3),
     )
     out, loss = call(
-        functools.partial(scale_kernel, scale),
-        [((nx, width // nx, count), BF16), ((1, count), F32)],
-        (every, st, m, ch),
-    )
-    got = lax.all_to_all(out, "x", split_axis=0, concat_axis=0, tiled=True)
-    (out,) = call(functools.partial(sum_kernel, 1.0), [((width // nx, count), BF16)], (got,))
-    nyh = ny // 2
-    piece = width // nx // nyh
-    out = out.reshape(nyh, piece, count)
-    got = lax.all_to_all(out, "yh", split_axis=0, concat_axis=0, tiled=True)
-    (grad,) = call(functools.partial(sum_kernel, scale), [((piece, count), BF16)], (got,))
+        functools.partial(scale_kernel, scale), [((width, count), BF16), ((1, count), F32)], (every, st, m, ch)
+    )
+    n_outer = members // 2
+    out = out.reshape(n_outer, width // n_outer, count)
+    got = lax.all_to_all(out, OUTER, split_axis=0, concat_axis=0, tiled=True)
+    (grad,) = call(functools.partial(sum_kernel, scale), [((width // n_outer, count), BF16)], (got,))
     return grad.T, loss.reshape(count)
 
 

time: 109 us -> 109 us (level)
  the two profiles are of different devices: /device:TPU:8 before, /device:TPU:16 now
where the time goes in v15:
time: 109 us
  starting transfers between devices  37.1 us (34%)
  blocking collectives  30.7 us (28%)
  waiting for transfers between devices  25 us (23%)
  Pallas kernels  15.1 us (14%)
    all_to_all x1, blocking collectives, shards(): got = lax.all_to_all(out, OUTER, split_axis=0, concat_axis=0, tiled=True)  30.7 us
    pallas_call x6, Pallas kernels, call(): return kernel(*operands)  15.1 us
    ppermute x3, waiting for transfers between devices, to_sides(): return lax.ppermute(x, LANE, perm)  14.3 us
    ppermute x3, starting transfers between devices, to_sides(): return lax.ppermute(x, LANE, perm)  11.7 us
    all_to_all x1, starting transfers between devices, shards(): lax.all_to_all(stats, ('yl', *OUTER), split_axis=0, concat_axis=0, tiled=...  11.3 us
    all_to_all x1, starting transfers between devices, shards(): lax.all_to_all(copies, 'z', split_axis=0, concat_axis=0, tiled=True)  10.3 us
    all_to_all x1, waiting for transfers between devices, shards(): lax.all_to_all(copies, 'z', split_axis=0, concat_axis=0, tiled=True)  9.2 us
    ppermute x2, starting transfers between devices, swapped(): return lax.ppermute(x, 'c', [(0, 1), (1, 0)])  3.83 us
  transfers between devices with their start and end apart: 7, of which 4 were waited for; matrix products, arithmetic and copies ran while one was open for 0% of the time, Pallas kernels for 11%

profile of v15, /device:TPU:16, one launch (start us, length us, event | category | flops | bytes accessed | tf_op | source)
XLA Modules:
  0.0 108.7 jit_solution(1942287782612604075)
XLA Ops:
  0.6 0.0 copy-start
  0.6 0.0 copy-start.3
  0.7 1.9 %shard_map.50 = bf16[8,64,768]{2,1,0:T(8,128)(2,1)} custom-call(bf16[64,768]{1,0:T(8,128)(2,1)} %x_hbm.1), custom_call_target="tpu_custom_call" | custom-call | bytes 4194304 | tf_op jit(solution)/shard_map/pallas_call | solution.py:171
  2.6 10.3 %all-to-all-start = ((bf16[8,64,768]{2,1,0:T(8,128)(2,1)}), bf16[8,64,768]{2,1,0:T(8,128)(2,1)S(1)}, u32[]{:S(2)}, u32[]{:S(2)}) async-start(bf16[8,64,768]{2,1,0:T(8,128)(2,1)} %shard_map.50), calls=%async_computation | async-start | bytes 1572864 | tf_op jit(solution)/shard_map/all_to_all | solution.py:204
  12.9 0.0 copy-done
  12.9 3.5 %collective-permute-start = (bf16[512,768]{1,0:T(8,128)(2,1)S(1)}, bf16[512,768]{1,0:T(8,128)(2,1)S(1)}, u32[]{:S(2)}, u32[]{:S(2)}) collective-permute-start(bf16[512,768]{1,0:T(8,128)(2,1)S(1)} %copy-done), channel_id=1, source_target_pairs={{0,2},{1,387},{2,128},{3,1},{128,130},{129,3},{130,256},{131,129},... | collective-permute-start | bytes 2359304 | tf_op jit(solution)/shard_map/ppermute | solution.py:32
  16.4 0.0 copy-done.3
  16.4 4.7 %collective-permute-start.1 = (s32[1,512]{1,0:T(1,128)S(1)}, s32[1,512]{1,0:T(1,128)S(1)}, u32[]{:S(2)}, u32[]{:S(2)}) collective-permute-start(s32[1,512]{1,0:T(1,128)S(1)} %bitcast.15), channel_id=1, source_target_pairs={{0,2},{1,387},{2,128},{3,1},{128,130},{129,3},{130,256},{131,129},... | collective-permute-start | bytes 6152 | tf_op jit(solution)/shard_map/ppermute | solution.py:32
  21.1 5.7 %collective-permute-done.1.posf_ref = s32[1,512]{1,0:T(1,128)S(1)} collective-permute-done((s32[1,512]{1,0:T(1,128)S(1)}, s32[1,512]{1,0:T(1,128)S(1)}, u32[]{:S(2)}, u32[]{:S(2)}) %collective-permute-start.1) | collective-permute-done | bytes 2080 | tf_op jit(solution)/shard_map/ppermute | solution.py:32
  26.8 0.0 collective-permute-done.qf_ref
  26.8 9.2 %all-to-all-done = bf16[8,64,768]{2,1,0:T(8,128)(2,1)S(1)} async-done(((bf16[8,64,768]{2,1,0:T(8,128)(2,1)}), bf16[8,64,768]{2,1,0:T(8,128)(2,1)S(1)}, u32[]{:S(2)}, u32[]{:S(2)}) %all-to-all-start) | async-done | bytes 786464 | tf_op jit(solution)/shard_map/all_to_all | solution.py:204
  36.0 0.0 copy-start.1
  36.0 3.5 %collective-permute-start.3 = (bf16[512,768]{1,0:T(8,128)(2,1)S(1)}, bf16[512,768]{1,0:T(8,128)(2,1)}, u32[]{:S(2)}, u32[]{:S(2)}) collective-permute-start(bf16[512,768]{1,0:T(8,128)(2,1)S(1)} %bitcast.10), channel_id=1, source_target_pairs={{0,2},{1,387},{2,128},{3,1},{128,130},{129,3},{130,256},{131,129},... | collective-permute-start | bytes 2359304 | tf_op jit(solution)/shard_map/ppermute | solution.py:32
  39.5 1.9 %collective-permute-start.2 = (bf16[512,768]{1,0:T(8,128)(2,1)S(1)}, bf16[512,768]{1,0:T(8,128)(2,1)S(1)}, u32[]{:S(2)}, u32[]{:S(2)}) collective-permute-start(bf16[512,768]{1,0:T(8,128)(2,1)S(1)} %bitcast.11), channel_id=1, source_target_pairs={{0,1},{1,0},{2,3},{3,2},{4,5},{5,4},{6,7},{7,6},{8,9},{9,8},{10,11... | collective-permute-start | bytes 2359304 | tf_op jit(solution)/shard_map/ppermute | solution.py:24
  41.5 8.6 %collective-permute-done.3.side_hbm = bf16[512,768]{1,0:T(8,128)(2,1)} collective-permute-done((bf16[512,768]{1,0:T(8,128)(2,1)S(1)}, bf16[512,768]{1,0:T(8,128)(2,1)}, u32[]{:S(2)}, u32[]{:S(2)}) %collective-permute-start.3) | collective-permute-done | bytes 786464 | tf_op jit(solution)/shard_map/ppermute | solution.py:32
  50.0 1.9 %collective-permute-start.4 = (bf16[512,768]{1,0:T(8,128)(2,1)}, bf16[512,768]{1,0:T(8,128)(2,1)}, u32[]{:S(2)}, u32[]{:S(2)}) collective-permute-start(bf16[512,768]{1,0:T(8,128)(2,1)} %collective-permute-done.3.side_hbm), channel_id=1, source_target_pairs={{0,1},{1,0},{2,3},{3,2},{4,5},{5,4},{6,7},{7,6},{8,9},{9,8},{10,11... | collective-permute-start | bytes 2359304 | tf_op jit(solution)/shard_map/ppermute | solution.py:24
  52.0 0.1 stack.23.base_ref
  52.1 0.0 collective-permute-done.2.b_ref.b_hbm
  52.1 0.0 copy-start.2
  52.1 3.8 %shard_map.51 = (f32[8,512]{1,0:T(8,128)S(1)}, bf16[1024,512]{1,0:T(8,128)(2,1)}, f32[32,1,1024]{2,1,0:T(1,128)}) custom-call(s32[5]{0:T(128)S(1)} %stack.23.base_ref, bf16[512,768]{1,0:T(8,128)(2,1)S(1)} %bitcast.12, bf16[512,768]{1,0:T(8,128)(2,1)S(1)} %collective-permute-done.2.b_ref.b_hbm, bf16[512,768]{1,0:T(8,128)(2,1)S(1)} %copy-done, ...), custom_call_target="tpu_custom_call" | custom-call | flops 1610612736 | bytes 4194304 | tf_op jit(solution)/shard_map/pallas_call | solution.py:171
  55.8 0.0 copy-done.1
  55.8 0.0 copy-done.2
  55.8 11.3 %all-to-all-start.1 = ((f32[32,1,1024]{2,1,0:T(1,128)}), f32[32,1,1024]{2,1,0:T(1,128)S(1)}, u32[]{:S(2)}, u32[]{:S(2)}) async-start(f32[32,1,1024]{2,1,0:T(1,128)} %get-tuple-element.19), calls=%async_computation.1 | async-start | bytes 262144 | tf_op jit(solution)/shard_map/all_to_all | solution.py:218
  67.1 2.0 %shard_map.52 = (bf16[512,768]{1,0:T(8,128)(2,1)S(1)}, bf16[512,768]{1,0:T(8,128)(2,1)S(1)}, f32[512,512]{1,0:T(8,128)S(1)}) custom-call(bf16[512,768]{1,0:T(8,128)(2,1)} %q_hbm.1, bf16[512,768]{1,0:T(8,128)(2,1)} %collective-permute-done.3.side_hbm), custom_call_target="tpu_custom_call" | custom-call | flops 402653184 | bytes 4194304 | tf_op jit(solution)/shard_map/pallas_call | solution.py:171
  69.1 0.0 collective-permute-done.4.side2_ref
  69.1 6.0 %shard_map.53 = (f32[8,512]{1,0:T(8,128)S(1)}, f32[768,512]{1,0:T(8,128)S(1)}, bf16[768,512]{1,0:T(8,128)(2,1)S(1)}) custom-call(s32[5]{0:T(128)S(1)} %stack.23.base_ref, bf16[512,768]{1,0:T(8,128)(2,1)} %bitcast.13, bf16[512,768]{1,0:T(8,128)(2,1)} %copy-done.2, bf16[1024,512]{1,0:T(8,128)(2,1)} %get-tuple-element.20.wo_hbm, ...), custom_call_target="tpu_custom_call" | custom-call | flops 4026531840 | bytes 4194304 | tf_op jit(solution)/shard_map/pallas_call | solution.py:171
  75.1 1.5 %all-to-all-done.1.every_ref = f32[32,1,1024]{2,1,0:T(1,128)S(1)} async-done(((f32[32,1,1024]{2,1,0:T(1,128)}), f32[32,1,1024]{2,1,0:T(1,128)S(1)}, u32[]{:S(2)}, u32[]{:S(2)}) %all-to-all-start.1) | async-done | bytes 131104 | tf_op jit(solution)/shard_map/all_to_all | solution.py:218
  76.7 0.6 shard_map.54
  77.3 30.7 %all_to_all.15.got_ref = bf16[16,48,512]{2,1,0:T(8,128)(2,1)S(1)} all-to-all(bf16[16,48,512]{2,1,0:T(8,128)(2,1)S(1)} %bitcast.14), channel_id=1, replica_groups=mesh['yh'=4,'x'=4,'z'=8,'yl'=2,'c'=2] {'yh','x'}, dimensions={0} | all-to-all | bytes 1572864 | tf_op jit(solution)/shard_map/all_to_all | solution.py:250
  108.0 0.7 shard_map.55
Async XLA Ops:
  0.6 12.3 %copy-start = (bf16[512,768]{1,0:T(8,128)(2,1)S(1)}, bf16[512,768]{1,0:T(8,128)(2,1)}, u32[]{:S(2)}) copy-start(bf16[512,768]{1,0:T(8,128)(2,1)} %q_hbm.1) | copy-start | bytes 2359300
  0.6 15.8 %copy-start.3 = (s32[512]{0:T(512)S(1)}, s32[512]{0:T(512)}, u32[]{:S(2)}) copy-start(s32[512]{0:T(512)} %param.5) | copy-start | bytes 6148
  2.6 33.4 %all-to-all-start = ((bf16[8,64,768]{2,1,0:T(8,128)(2,1)}), bf16[8,64,768]{2,1,0:T(8,128)(2,1)S(1)}, u32[]{:S(2)}, u32[]{:S(2)}) async-start(bf16[8,64,768]{2,1,0:T(8,128)(2,1)} %shard_map.50), calls=%async_computation | async-start | bytes 1572864 | tf_op jit(solution)/shard_map/all_to_all | solution.py:204
  12.9 13.9 %collective-permute-start = (bf16[512,768]{1,0:T(8,128)(2,1)S(1)}, bf16[512,768]{1,0:T(8,128)(2,1)S(1)}, u32[]{:S(2)}, u32[]{:S(2)}) collective-permute-start(bf16[512,768]{1,0:T(8,128)(2,1)S(1)} %copy-done), channel_id=1, source_target_pairs={{0,2},{1,387},{2,128},{3,1},{128,130},{129,3},{130,256},{131,129},... | collective-permute-start | bytes 2359304 | tf_op jit(solution)/shard_map/ppermute | solution.py:32
  16.4 10.4 %collective-permute-start.1 = (s32[1,512]{1,0:T(1,128)S(1)}, s32[1,512]{1,0:T(1,128)S(1)}, u32[]{:S(2)}, u32[]{:S(2)}) collective-permute-start(s32[1,512]{1,0:T(1,128)S(1)} %bitcast.15), channel_id=1, source_target_pairs={{0,2},{1,387},{2,128},{3,1},{128,130},{129,3},{130,256},{131,129},... | collective-permute-start | bytes 6152 | tf_op jit(solution)/shard_map/ppermute | solution.py:32
  36.0 19.8 %copy-start.1 = (bf16[8,64,768]{2,1,0:T(8,128)(2,1)}, bf16[8,64,768]{2,1,0:T(8,128)(2,1)S(1)}, u32[]{:S(2)}) copy-start(bf16[8,64,768]{2,1,0:T(8,128)(2,1)S(1)} %all-to-all-done) | copy-start | bytes 2359300
  36.0 14.0 %collective-permute-start.3 = (bf16[512,768]{1,0:T(8,128)(2,1)S(1)}, bf16[512,768]{1,0:T(8,128)(2,1)}, u32[]{:S(2)}, u32[]{:S(2)}) collective-permute-start(bf16[512,768]{1,0:T(8,128)(2,1)S(1)} %bitcast.10), channel_id=1, source_target_pairs={{0,2},{1,387},{2,128},{3,1},{128,130},{129,3},{130,256},{131,129},... | collective-permute-start | bytes 2359304 | tf_op jit(solution)/shard_map/ppermute | solution.py:32
  39.5 12.5 %collective-permute-start.2 = (bf16[512,768]{1,0:T(8,128)(2,1)S(1)}, bf16[512,768]{1,0:T(8,128)(2,1)S(1)}, u32[]{:S(2)}, u32[]{:S(2)}) collective-permute-start(bf16[512,768]{1,0:T(8,128)(2,1)S(1)} %bitcast.11), channel_id=1, source_target_pairs={{0,1},{1,0},{2,3},{3,2},{4,5},{5,4},{6,7},{7,6},{8,9},{9,8},{10,11... | collective-permute-start | bytes 2359304 | tf_op jit(solution)/shard_map/ppermute | solution.py:24
  50.0 19.1 %collective-permute-start.4 = (bf16[512,768]{1,0:T(8,128)(2,1)}, bf16[512,768]{1,0:T(8,128)(2,1)}, u32[]{:S(2)}, u32[]{:S(2)}) collective-permute-start(bf16[512,768]{1,0:T(8,128)(2,1)} %collective-permute-done.3.side_hbm), channel_id=1, source_target_pairs={{0,1},{1,0},{2,3},{3,2},{4,5},{5,4},{6,7},{7,6},{8,9},{9,8},{10,11... | collective-permute-start | bytes 2359304 | tf_op jit(solution)/shard_map/ppermute | solution.py:24
  52.1 3.8 %copy-start.2 = (bf16[512,768]{1,0:T(8,128)(2,1)}, bf16[512,768]{1,0:T(8,128)(2,1)S(1)}, u32[]{:S(2)}) copy-start(bf16[512,768]{1,0:T(8,128)(2,1)S(1)} %collective-permute-done.2.b_ref.b_hbm) | copy-start | bytes 2359300
  55.8 20.8 %all-to-all-start.1 = ((f32[32,1,1024]{2,1,0:T(1,128)}), f32[32,1,1024]{2,1,0:T(1,128)S(1)}, u32[]{:S(2)}, u32[]{:S(2)}) async-start(f32[32,1,1024]{2,1,0:T(1,128)} %get-tuple-element.19), calls=%async_computation.1 | async-start | bytes 262144 | tf_op jit(solution)/shard_map/all_to_all | solution.py:218

commit v16 on v13

--- a/solution.py
+++ b/solution.py
@@ -139,9 +139,9 @@
     loss_ref[...] = whole - ps
 
 
-def copy_kernel(x_hbm, out_hbm, sems):
+def copy_kernel(x_ref, out_hbm, sems):
     n = out_hbm.shape[0]
-    copies = [pltpu.make_async_copy(x_hbm, out_hbm.at[i], sems.at[i]) for i in range(n)]
+    copies = [pltpu.make_async_copy(x_ref, out_hbm.at[i], sems.at[i]) for i in range(n)]
     for copy in copies:
         copy.start()
     for copy in copies:
@@ -197,12 +197,7 @@
     theirs = to_sides(queries, ny)
     pos_theirs = to_sides(pos, ny)
     (copies,) = call(
-        copy_kernel,
-        [((nz, rows, width), BF16)],
-        (passages,),
-        [pltpu.SemaphoreType.DMA((nz,))],
-        hbm_in=(0,),
-        hbm_out=(0,),
+        copy_kernel, [((nz, rows, width), BF16)], (passages,), [pltpu.SemaphoreType.DMA((nz,))], hbm_out=(0,)
     )
     column = lax.all_to_all(copies, "z", split_axis=0, concat_axis=0, tiled=True)
     column, theirs, pos_theirs = lax.optimization_barrier((column, theirs, pos_theirs))

time: 132 us -> 109 us (0.83)
  Pallas kernels: 38.1 us -> 14.1 us
    pallas_call x7, Pallas kernels: 38.1 us -> 14.1 us  [call(): return kernel(*operands)]
  transfers between devices with their start and end apart: 7 -> 7, of which waited for: 4 -> 4; matrix products, arithmetic and copies ran while one was open for 0% -> 0% of each run, Pallas kernels for 9% -> 11%
where the time goes in v16:
time: 109 us; the launch traced here: 108 us
  starting transfers between devices  36 us (33%)
  blocking collectives  29.2 us (27%)
  waiting for transfers between devices  26.9 us (25%)
  Pallas kernels  14.1 us (13%)
    ppermute x3, waiting for transfers between devices, to_sides(): return lax.ppermute(x, LANE, perm)  15.5 us
    all_to_all x1, blocking collectives, shards(): got = lax.all_to_all(out, 'yh', split_axis=0, concat_axis=0, tiled=True)  15 us
    all_to_all x1, blocking collectives, shards(): got = lax.all_to_all(out, 'x', split_axis=0, concat_axis=0, tiled=True)  14.2 us
    pallas_call x7, Pallas kernels, call(): return kernel(*operands)  14.1 us
    all_to_all x1, starting transfers between devices, shards(): lax.all_to_all(stats, ('yl', *OUTER), split_axis=0, concat_axis=0, tiled=...  11.4 us
    ppermute x3, starting transfers between devices, to_sides(): return lax.ppermute(x, LANE, perm)  10.4 us
    all_to_all x1, starting transfers between devices, shards(): lax.all_to_all(copies, 'z', split_axis=0, concat_axis=0, tiled=True)  10.3 us
    all_to_all x1, waiting for transfers between devices, shards(): lax.all_to_all(copies, 'z', split_axis=0, concat_axis=0, tiled=True)  9.2 us
  transfers between devices with their start and end apart: 7, of which 4 were waited for; matrix products, arithmetic and copies ran while one was open for 0% of the time, Pallas kernels for 11%

profile of v16, /device:TPU:8, one launch (start us, length us, event | category | flops | bytes accessed | tf_op | source)
XLA Modules:
  0.0 108.1 jit_solution(4925405932845367099)
XLA Ops:
  0.6 0.0 copy-start
  0.6 0.0 copy-start.2
  0.7 1.0 copy-done.2
  1.6 0.0 copy-start.4
  1.6 1.0 shard_map.50
  2.6 10.3 %all-to-all-start = ((bf16[8,64,768]{2,1,0:T(8,128)(2,1)}), bf16[8,64,768]{2,1,0:T(8,128)(2,1)S(1)}, u32[]{:S(2)}, u32[]{:S(2)}) async-start(bf16[8,64,768]{2,1,0:T(8,128)(2,1)} %shard_map.50), calls=%async_computation | async-start | bytes 1572864 | tf_op jit(solution)/shard_map/all_to_all | solution.py:202
  12.9 0.0 copy-done
  12.9 3.5 %collective-permute-start = (bf16[512,768]{1,0:T(8,128)(2,1)S(1)}, bf16[512,768]{1,0:T(8,128)(2,1)S(1)}, u32[]{:S(2)}, u32[]{:S(2)}) collective-permute-start(bf16[512,768]{1,0:T(8,128)(2,1)S(1)} %copy-done), channel_id=1, source_target_pairs={{0,2},{1,387},{2,128},{3,1},{128,130},{129,3},{130,256},{131,129},... | collective-permute-start | bytes 2359304 | tf_op jit(solution)/shard_map/ppermute | solution.py:32
  16.4 0.0 copy-done.4
  16.4 3.5 %collective-permute-start.1 = (s32[1,512]{1,0:T(1,128)S(1)}, s32[1,512]{1,0:T(1,128)S(1)}, u32[]{:S(2)}, u32[]{:S(2)}) collective-permute-start(s32[1,512]{1,0:T(1,128)S(1)} %bitcast.15), channel_id=1, source_target_pairs={{0,2},{1,387},{2,128},{3,1},{128,130},{129,3},{130,256},{131,129},... | collective-permute-start | bytes 6152 | tf_op jit(solution)/shard_map/ppermute | solution.py:32
  19.9 6.9 %collective-permute-done.1.posf_ref = s32[1,512]{1,0:T(1,128)S(1)} collective-permute-done((s32[1,512]{1,0:T(1,128)S(1)}, s32[1,512]{1,0:T(1,128)S(1)}, u32[]{:S(2)}, u32[]{:S(2)}) %collective-permute-start.1) | collective-permute-done | bytes 2080 | tf_op jit(solution)/shard_map/ppermute | solution.py:32
  26.8 0.0 collective-permute-done.qf_ref
  26.8 9.2 %all-to-all-done = bf16[8,64,768]{2,1,0:T(8,128)(2,1)S(1)} async-done(((bf16[8,64,768]{2,1,0:T(8,128)(2,1)}), bf16[8,64,768]{2,1,0:T(8,128)(2,1)S(1)}, u32[]{:S(2)}, u32[]{:S(2)}) %all-to-all-start) | async-done | bytes 786464 | tf_op jit(solution)/shard_map/all_to_all | solution.py:202
  36.0 3.5 %collective-permute-start.3 = (bf16[512,768]{1,0:T(8,128)(2,1)S(1)}, bf16[512,768]{1,0:T(8,128)(2,1)}, u32[]{:S(2)}, u32[]{:S(2)}) collective-permute-start(bf16[512,768]{1,0:T(8,128)(2,1)S(1)} %bitcast.10), channel_id=1, source_target_pairs={{0,2},{1,387},{2,128},{3,1},{128,130},{129,3},{130,256},{131,129},... | collective-permute-start | bytes 2359304 | tf_op jit(solution)/shard_map/ppermute | solution.py:32
  39.5 1.9 %collective-permute-start.2 = (bf16[512,768]{1,0:T(8,128)(2,1)S(1)}, bf16[512,768]{1,0:T(8,128)(2,1)S(1)}, u32[]{:S(2)}, u32[]{:S(2)}) collective-permute-start(bf16[512,768]{1,0:T(8,128)(2,1)S(1)} %bitcast.11), channel_id=1, source_target_pairs={{0,1},{1,0},{2,3},{3,2},{4,5},{5,4},{6,7},{7,6},{8,9},{9,8},{10,11... | collective-permute-start | bytes 2359304 | tf_op jit(solution)/shard_map/ppermute | solution.py:24
  41.4 8.6 %collective-permute-done.3.side_hbm = bf16[512,768]{1,0:T(8,128)(2,1)} collective-permute-done((bf16[512,768]{1,0:T(8,128)(2,1)S(1)}, bf16[512,768]{1,0:T(8,128)(2,1)}, u32[]{:S(2)}, u32[]{:S(2)}) %collective-permute-start.3) | collective-permute-done | bytes 786464 | tf_op jit(solution)/shard_map/ppermute | solution.py:32
  50.0 1.9 %collective-permute-start.4 = (bf16[512,768]{1,0:T(8,128)(2,1)}, bf16[512,768]{1,0:T(8,128)(2,1)}, u32[]{:S(2)}, u32[]{:S(2)}) collective-permute-start(bf16[512,768]{1,0:T(8,128)(2,1)} %collective-permute-done.3.side_hbm), channel_id=1, source_target_pairs={{0,1},{1,0},{2,3},{3,2},{4,5},{5,4},{6,7},{7,6},{8,9},{9,8},{10,11... | collective-permute-start | bytes 2359304 | tf_op jit(solution)/shard_map/ppermute | solution.py:24
  52.0 0.1 stack.23.base_ref
  52.0 0.0 collective-permute-done.2.b_ref.b_hbm
  52.0 3.7 %shard_map.51 = (f32[8,512]{1,0:T(8,128)S(1)}, bf16[1024,512]{1,0:T(8,128)(2,1)}, f32[32,1,1024]{2,1,0:T(1,128)}) custom-call(s32[5]{0:T(128)S(1)} %stack.23.base_ref, bf16[512,768]{1,0:T(8,128)(2,1)S(1)} %bitcast.12, bf16[512,768]{1,0:T(8,128)(2,1)S(1)} %collective-permute-done.2.b_ref.b_hbm, bf16[512,768]{1,0:T(8,128)(2,1)S(1)} %copy-done, ...), custom_call_target="tpu_custom_call" | custom-call | flops 1610612736 | bytes 4194304 | tf_op jit(solution)/shard_map/pallas_call | solution.py:174
  55.8 0.0 copy-done.1
  55.8 0.0 copy-done.3
  55.8 11.4 %all-to-all-start.1 = ((f32[32,1,1024]{2,1,0:T(1,128)}), f32[32,1,1024]{2,1,0:T(1,128)S(1)}, u32[]{:S(2)}, u32[]{:S(2)}) async-start(f32[32,1,1024]{2,1,0:T(1,128)} %get-tuple-element.19), calls=%async_computation.1 | async-start | bytes 262144 | tf_op jit(solution)/shard_map/all_to_all | solution.py:216
  67.2 2.0 %shard_map.52 = (bf16[512,768]{1,0:T(8,128)(2,1)S(1)}, bf16[512,768]{1,0:T(8,128)(2,1)S(1)}, f32[512,512]{1,0:T(8,128)S(1)}) custom-call(bf16[512,768]{1,0:T(8,128)(2,1)} %q_hbm.1, bf16[512,768]{1,0:T(8,128)(2,1)} %collective-permute-done.3.side_hbm), custom_call_target="tpu_custom_call" | custom-call | flops 402653184 | bytes 4194304 | tf_op jit(solution)/shard_map/pallas_call | solution.py:174
  69.2 0.0 collective-permute-done.4.side2_ref
  69.2 6.0 %shard_map.53 = (f32[8,512]{1,0:T(8,128)S(1)}, f32[768,512]{1,0:T(8,128)S(1)}, bf16[768,512]{1,0:T(8,128)(2,1)S(1)}) custom-call(s32[5]{0:T(128)S(1)} %stack.23.base_ref, bf16[512,768]{1,0:T(8,128)(2,1)} %bitcast.13, bf16[512,768]{1,0:T(8,128)(2,1)} %copy-done.3, bf16[1024,512]{1,0:T(8,128)(2,1)} %get-tuple-element.20.wo_hbm, ...), custom_call_target="tpu_custom_call" | custom-call | flops 4026531840 | bytes 4194304 | tf_op jit(solution)/shard_map/pallas_call | solution.py:174
  75.2 2.3 %all-to-all-done.1.every_ref = f32[32,1,1024]{2,1,0:T(1,128)S(1)} async-done(((f32[32,1,1024]{2,1,0:T(1,128)}), f32[32,1,1024]{2,1,0:T(1,128)S(1)}, u32[]{:S(2)}, u32[]{:S(2)}) %all-to-all-start.1) | async-done | bytes 131104 | tf_op jit(solution)/shard_map/all_to_all | solution.py:216
  77.5 0.6 shard_map.54
  78.1 14.2 %all_to_all.20.got_ref = bf16[4,192,512]{2,1,0:T(8,128)(2,1)S(1)} all-to-all(bf16[4,192,512]{2,1,0:T(8,128)(2,1)S(1)} %get-tuple-element.28), channel_id=1, replica_groups=mesh['yh'=4,'x'=4,'z'=8,'yl'=2,'c'=2] {'x'}, dimensions={0} | all-to-all | bytes 1572864 | tf_op jit(solution)/shard_map/all_to_all | solution.py:248
  92.3 0.1 shard_map.55
  92.4 15.0 %all_to_all.21.got_ref = bf16[4,48,512]{2,1,0:T(8,128)(2,1)S(1)} all-to-all(bf16[4,48,512]{2,1,0:T(8,128)(2,1)S(1)} %bitcast.14), channel_id=1, replica_groups=mesh['yh'=4,'x'=4,'z'=8,'yl'=2,'c'=2] {'yh'}, dimensions={0} | all-to-all | bytes 393216 | tf_op jit(solution)/shard_map/all_to_all | solution.py:253
  107.5 0.7 shard_map.56
  (2 shorter events, 0.0 us)
Async XLA Ops:
  0.6 12.3 %copy-start = (bf16[512,768]{1,0:T(8,128)(2,1)S(1)}, bf16[512,768]{1,0:T(8,128)(2,1)}, u32[]{:S(2)}) copy-start(bf16[512,768]{1,0:T(8,128)(2,1)} %q_hbm.1) | copy-start | bytes 2359300
  0.6 1.0 copy-start.2
  1.6 14.8 %copy-start.4 = (s32[512]{0:T(512)S(1)}, s32[512]{0:T(512)}, u32[]{:S(2)}) copy-start(s32[512]{0:T(512)} %param.5) | copy-start | bytes 6148
  2.6 33.4 %all-to-all-start = ((bf16[8,64,768]{2,1,0:T(8,128)(2,1)}), bf16[8,64,768]{2,1,0:T(8,128)(2,1)S(1)}, u32[]{:S(2)}, u32[]{:S(2)}) async-start(bf16[8,64,768]{2,1,0:T(8,128)(2,1)} %shard_map.50), calls=%async_computation | async-start | bytes 1572864 | tf_op jit(solution)/shard_map/all_to_all | solution.py:202
  12.9 13.9 %collective-permute-start = (bf16[512,768]{1,0:T(8,128)(2,1)S(1)}, bf16[512,768]{1,0:T(8,128)(2,1)S(1)}, u32[]{:S(2)}, u32[]{:S(2)}) collective-permute-start(bf16[512,768]{1,0:T(8,128)(2,1)S(1)} %copy-done), channel_id=1, source_target_pairs={{0,2},{1,387},{2,128},{3,1},{128,130},{129,3},{130,256},{131,129},... | collective-permute-start | bytes 2359304 | tf_op jit(solution)/shard_map/ppermute | solution.py:32
  16.4 10.4 %collective-permute-start.1 = (s32[1,512]{1,0:T(1,128)S(1)}, s32[1,512]{1,0:T(1,128)S(1)}, u32[]{:S(2)}, u32[]{:S(2)}) collective-permute-start(s32[1,512]{1,0:T(1,128)S(1)} %bitcast.15), channel_id=1, source_target_pairs={{0,2},{1,387},{2,128},{3,1},{128,130},{129,3},{130,256},{131,129},... | collective-permute-start | bytes 6152 | tf_op jit(solution)/shard_map/ppermute | solution.py:32
  36.0 19.8 %copy-start.1 = (bf16[8,64,768]{2,1,0:T(8,128)(2,1)}, bf16[8,64,768]{2,1,0:T(8,128)(2,1)S(1)}, u32[]{:S(2)}) copy-start(bf16[8,64,768]{2,1,0:T(8,128)(2,1)S(1)} %all-to-all-done) | copy-start | bytes 2359300
  36.0 14.0 %collective-permute-start.3 = (bf16[512,768]{1,0:T(8,128)(2,1)S(1)}, bf16[512,768]{1,0:T(8,128)(2,1)}, u32[]{:S(2)}, u32[]{:S(2)}) collective-permute-start(bf16[512,768]{1,0:T(8,128)(2,1)S(1)} %bitcast.10), channel_id=1, source_target_pairs={{0,2},{1,387},{2,128},{3,1},{128,130},{129,3},{130,256},{131,129},... | collective-permute-start | bytes 2359304 | tf_op jit(solution)/shard_map/ppermute | solution.py:32
  39.5 12.5 %collective-permute-start.2 = (bf16[512,768]{1,0:T(8,128)(2,1)S(1)}, bf16[512,768]{1,0:T(8,128)(2,1)S(1)}, u32[]{:S(2)}, u32[]{:S(2)}) collective-permute-start(bf16[512,768]{1,0:T(8,128)(2,1)S(1)} %bitcast.11), channel_id=1, source_target_pairs={{0,1},{1,0},{2,3},{3,2},{4,5},{5,4},{6,7},{7,6},{8,9},{9,8},{10,11... | collective-permute-start | bytes 2359304 | tf_op jit(solution)/shard_map/ppermute | solution.py:24
  50.0 19.2 %collective-permute-start.4 = (bf16[512,768]{1,0:T(8,128)(2,1)}, bf16[512,768]{1,0:T(8,128)(2,1)}, u32[]{:S(2)}, u32[]{:S(2)}) collective-permute-start(bf16[512,768]{1,0:T(8,128)(2,1)} %collective-permute-done.3.side_hbm), channel_id=1, source_target_pairs={{0,1},{1,0},{2,3},{3,2},{4,5},{5,4},{6,7},{7,6},{8,9},{9,8},{10,11... | collective-permute-start | bytes 2359304 | tf_op jit(solution)/shard_map/ppermute | solution.py:24
  52.0 3.8 %copy-start.3 = (bf16[512,768]{1,0:T(8,128)(2,1)}, bf16[512,768]{1,0:T(8,128)(2,1)S(1)}, u32[]{:S(2)}) copy-start(bf16[512,768]{1,0:T(8,128)(2,1)S(1)} %collective-permute-done.2.b_ref.b_hbm) | copy-start | bytes 2359300
  55.8 21.7 %all-to-all-start.1 = ((f32[32,1,1024]{2,1,0:T(1,128)}), f32[32,1,1024]{2,1,0:T(1,128)S(1)}, u32[]{:S(2)}, u32[]{:S(2)}) async-start(f32[32,1,1024]{2,1,0:T(1,128)} %get-tuple-element.19), calls=%async_computation.1 | async-start | bytes 262144 | tf_op jit(solution)/shard_map/all_to_all | solution.py:216
